TPU v7x, 32 devices: a whole 2x2x4 slice. The times are simulated.
32 devices in a mesh: shard: 4 (over z), tensor: 2 (over core), section: 4 (over y, x).
Axes of the slice: x: 2, y: 2, z: 4, core: 2. Of those that a mesh axis runs over, the one named last changes fastest.
Arguments:
- gradient: bfloat16 [2560, 2560], P('shard', ('tensor', 'section')), may hold values from -100 to 100
- gain_grad: float32 [2, 2560], P(None, 'shard'), may hold values from -12 to 12
- left_statistic: float32 [2560, 2560], P('shard', ('tensor', 'section')), may hold values from -1 to 3, as said below
- left_basis: float32 [2560, 2560], P('shard', ('tensor', 'section')), may hold values from -1 to 1.5
- first_moment: float32 [2560, 2560], P('shard', ('tensor', 'section')), may hold values from -3 to 3
- second_moment: float32 [2560, 2560], P('shard', ('tensor', 'section')), may hold values from 0.2 to 2
- norm_gains: float32 [2, 2560], P(None, 'shard'), may hold values from 0.5 to 1.5
- gain_first: float32 [2, 2560], P(None, 'shard'), may hold values from -2 to 2
- gain_second: float32 [2, 2560], P(None, 'shard'), may hold values from 0.5 to 5
Outputs:
- update: float32 [2560, 2560], P('shard', ('tensor', 'section'))
- new_first: float32 [2560, 2560], P('shard', ('tensor', 'section'))
- new_second: float32 [2560, 2560], P('shard', ('tensor', 'section'))
- new_statistic: float32 [2560, 2560], P('shard', ('tensor', 'section'))
- new_basis: float32 [2560, 2560], P('shard', ('tensor', 'section'))
- new_gains: float32 [2, 2560], P(None, 'shard')
- new_gain_first: float32 [2, 2560], P(None, 'shard')
- new_gain_second: float32 [2, 2560], P(None, 'shard')
Inputs may be any that keep to these rules, and one draw needn't show every extreme that they name: `left_statistic`: symmetric.
All inputs are finite; a program needn't handle non-finite values.
Results may differ from a plain program's by a relative error of at most 0.0003.
Values may be sent and summed in bfloat16 or wider, within the bound.
A program may use at most 128 MiB of HBM per device.

v0:
```python
import jax
import jax.numpy as jnp
from jax import lax
from jax.sharding import PartitionSpec as P

D = 2560
NS_STEPS = 3


def matmul(left_side, right_side):
    return jnp.dot(
        left_side, right_side, precision=lax.Precision.HIGHEST, preferred_element_type=jnp.float32
    )


def times_rows(full_rows, segment):
    return matmul(full_rows, segment)


def transposed_terms(full_rows, local_block):
    return matmul(full_rows.T, local_block)


def row_panel(local_block):
    return lax.all_gather(local_block, ("tensor", "section"), axis=1, tiled=True)


def on_device(
    gradient,
    gain_grad,
    left_statistic,
    left_basis,
    first_moment,
    second_moment,
    norm_gains,
    gain_first,
    gain_second,
):
    group_size = lax.axis_size(("tensor", "section"))
    grad_float = gradient.astype(jnp.float32)
    local_sum = jnp.sum(grad_float * grad_float) + jnp.sum(gain_grad * gain_grad) / group_size
    squares_total = lax.psum(local_sum, ("shard", "tensor", "section"))
    clip_factor = jnp.minimum(1.0, D / jnp.sqrt(squares_total + 1e-06))
    clipped = clip_factor * grad_float
    rotate_scale = 1.0
    outer_scale = 1.0
    basis_rows = row_panel(left_basis)
    rotated = rotate_scale * lax.psum_scatter(
        transposed_terms(basis_rows, clipped), "shard", scatter_dimension=0, tiled=True
    )
    partner = clip_factor * lax.all_gather(gradient, "shard", axis=0, tiled=True).astype(
        jnp.float32
    )
    outer_rows = matmul(clipped, partner.T)
    outer_part = lax.psum_scatter(
        outer_rows, ("tensor", "section"), scatter_dimension=1, tiled=True
    )
    new_statistic = 0.95 * left_statistic + 0.05 / D * (outer_scale * outer_part)
    new_first = 0.9 * first_moment + 0.1 * rotated
    new_second = 0.95 * second_moment + 0.05 * rotated * rotated
    direction = new_first / (jnp.sqrt(new_second) + 1e-08)
    update = times_rows(basis_rows, lax.all_gather(direction, "shard", axis=0, tiled=True))
    statistic_rows = row_panel(new_statistic)
    power_product = times_rows(
        statistic_rows, lax.all_gather(left_basis, "shard", axis=0, tiled=True)
    )
    power_sum = lax.psum(jnp.sum(power_product * power_product), ("shard", "tensor", "section"))
    iterate = 0.9 * jnp.sqrt(D / (power_sum + 1e-06)) * power_product
    for sweep_index in range(NS_STEPS):
        iterate_rows = row_panel(iterate)
        gram_block = lax.psum_scatter(
            transposed_terms(iterate_rows, iterate), "shard", scatter_dimension=0, tiled=True
        )
        applied = times_rows(iterate_rows, lax.all_gather(gram_block, "shard", axis=0, tiled=True))
        iterate = 1.5 * iterate - 0.5 * applied
    gain_clipped = clip_factor * gain_grad
    new_gain_first = 0.9 * gain_first + 0.1 * gain_clipped
    new_gain_second = 0.95 * gain_second + 0.05 * gain_clipped * gain_clipped
    new_gains = norm_gains - 0.01 * new_gain_first / (jnp.sqrt(new_gain_second) + 1e-08)
    return (
        update,
        new_first,
        new_second,
        new_statistic,
        iterate,
        new_gains,
        new_gain_first,
        new_gain_second,
    )


def solution(mesh):
    return jax.shard_map(
        on_device,
        mesh=mesh,
        in_specs=(
            P("shard", ("tensor", "section")),
            P(None, "shard"),
            P("shard", ("tensor", "section")),
            P("shard", ("tensor", "section")),
            P("shard", ("tensor", "section")),
            P("shard", ("tensor", "section")),
            P(None, "shard"),
            P(None, "shard"),
            P(None, "shard"),
        ),
        out_specs=(
            P("shard", ("tensor", "section")),
            P("shard", ("tensor", "section")),
            P("shard", ("tensor", "section")),
            P("shard", ("tensor", "section")),
            P("shard", ("tensor", "section")),
            P(None, "shard"),
            P(None, "shard"),
            P(None, "shard"),
        ),
        check_vma=False,
    )
```

profile of v0, /device:TPU:8, one launch (start us, length us, event | category | flops | bytes accessed | tf_op | source)
XLA Modules:
  0.0 1137.3 jit_solution(16108901470709755)
XLA Ops:
  7.2 0.0 all-gather.16.cloned.1.call-start
  7.2 0.7 all-gather.16.cloned.1.call-update
  7.9 0.0 reduce-scatter.8.cloned.1.call-start
  7.9 1.3 multiply_reduce_fusion.1
  9.9 1.8 fusion.7
  12.4 43.4 %psum.14 = f32[]{:T(128)} all-reduce(f32[]{:T(128)S(6)} %add.50), channel_id=1, replica_groups=mesh['shard'=4,'tensor'=2,'section'=4] {'shard','tensor','section'}, use_global_device_ids=true, to_apply=%region_2.0 | all-reduce | flops 1 | bytes 8 | tf_op jit(solution)/shard_map/psum | solution.py:42
  56.5 0.0 all-gather.16.cloned.1.call-done
  56.5 14.8 %fusion = f32[640,2560]{0,1:T(8,128)} fusion(bf16[2560,320]{0,1:T(8,128)(2,1)} %all-gather.16.cloned.1.call-done, f32[]{:T(128)S(6)} %min.3, bf16[640,320]{0,1:T(8,128)(2,1)} %param.9), kind=kOutput, calls=%fused_computation.1 | convolution fusion | flops 6293504000 | bytes 8601604 | tf_op jit(solution)/shard_map/dot_general | solution.py:11
  71.3 0.0 reduce-scatter.8.cloned.1.call-update
  71.4 0.0 all-gather.20.cloned.1.call-start
  71.4 0.7 all-gather.20.cloned.1.call-update
  72.1 0.0 all-gather.18.cloned.1.call-start
  72.1 61.7 %reduce-scatter.8.cloned.1.call-done = f32[640,320]{0,1:T(8,128)} async-done(((f32[640,2560]{0,1:T(8,128)}), f32[640,320]{0,1:T(8,128)}) %reduce-scatter.8.cloned.1.call-update) | async-done | bytes 819216 | tf_op jit(solution)/shard_map/reduce_scatter | solution.py:55
  133.9 2.2 multiply_add_fusion
  136.1 0.0 all-gather.18.cloned.1.call-update
  136.1 0.6 all-gather.22.cloned.1.call-start
  136.6 62.1 %all-gather.20.cloned.1.call-done = f32[2560,320]{0,1:T(8,128)} async-done(((f32[640,320]{0,1:T(8,128)}), f32[2560,320]{0,1:T(8,128)}) %all-gather.20.cloned.1.call-update) | async-done | bytes 3276816 | tf_op jit(solution)/shard_map/all_gather | solution.py:65
  198.8 50.2 %all-gather.18.cloned.1.call-done = f32[640,2560]{0,1:T(8,128)} async-done(((f32[640,320]{0,1:T(8,128)}), f32[640,2560]{0,1:T(8,128)}) %all-gather.18.cloned.1.call-update) | async-done | bytes 6553616 | tf_op jit(solution)/shard_map/all_gather | solution.py:25
  249.0 11.6 %multiply_reduce_fusion = (f32[]{:T(128)}, f32[640,320]{0,1:T(8,128)S(1)}) fusion(f32[640,2560]{0,1:T(8,128)} %all-gather.18.cloned.1.call-done, f32[2560,320]{0,1:T(8,128)} %all-gather.20.cloned.1.call-done), kind=kOutput, calls=%fused_computation.17 | convolution fusion | flops 6291865600 | bytes 10649604 | tf_op jit(solution)/shard_map/dot_general | solution.py:11
  260.6 39.5 %psum.15 = f32[]{:T(128)} all-reduce(f32[]{:T(128)} %get-tuple-element.14), channel_id=1, replica_groups=mesh['shard'=4,'tensor'=2,'section'=4] {'shard','tensor','section'}, use_global_device_ids=true, to_apply=%region_6.0 | all-reduce | flops 1 | bytes 8 | tf_op jit(solution)/shard_map/psum | solution.py:67
  300.9 0.9 broadcast_multiply_fusion
  301.8 0.0 all-gather.22.cloned.1.call-update
  301.8 0.0 reduce-scatter.10.cloned.1.call-start
  301.9 47.7 %all-gather.22.cloned.1.call-done = f32[640,2560]{0,1:T(8,128)} async-done(((f32[640,320]{0,1:T(8,128)}), f32[640,2560]{0,1:T(8,128)}) %all-gather.22.cloned.1.call-update) | async-done | bytes 6553616 | tf_op jit(solution)/shard_map/all_gather | solution.py:25
  349.6 15.1 %fusion.14 = f32[2560,320]{1,0:T(8,128)} fusion(f32[640,2560]{0,1:T(8,128)} %all-gather.22.cloned.1.call-done, f32[640,320]{0,1:T(8,128)} %broadcast_multiply_fusion), kind=kOutput, calls=%fused_computation.29 | convolution fusion | flops 6291456000 | bytes 10649600 | tf_op jit(solution)/shard_map/dot_general | solution.py:11
  364.7 0.0 reduce-scatter.10.cloned.1.call-update
  364.7 0.0 all-gather.24.cloned.1.call-start
  364.8 72.6 %reduce-scatter.10.cloned.1.call-done = f32[640,320]{1,0:T(8,128)} async-done(((f32[2560,320]{1,0:T(8,128)}), f32[640,320]{1,0:T(8,128)}) %reduce-scatter.10.cloned.1.call-update) | async-done | bytes 819216 | tf_op jit(solution)/shard_map/reduce_scatter | solution.py:71
  437.4 0.0 all-gather.24.cloned.1.call-update
  437.4 0.2 all-gather.26.cloned.1.call-start
  437.6 75.8 %all-gather.24.cloned.1.call-done = f32[2560,320]{1,0:T(8,128)} async-done(((f32[640,320]{1,0:T(8,128)}), f32[2560,320]{1,0:T(8,128)}) %all-gather.24.cloned.1.call-update) | async-done | bytes 3276816 | tf_op jit(solution)/shard_map/all_gather | solution.py:74
  513.4 12.1 %fusion.4 = f32[640,320]{0,1:T(8,128)} fusion(f32[640,2560]{0,1:T(8,128)} %all-gather.22.cloned.1.call-done, f32[2560,320]{1,0:T(8,128)} %all-gather.24.cloned.1.call-done, f32[640,320]{0,1:T(8,128)S(1)} %copy-done.2), kind=kOutput, calls=%fused_computation.9 | convolution fusion | flops 6292070400 | bytes 11468800 | tf_op jit(solution)/shard_map/dot_general | solution.py:11
  525.5 0.0 all-gather.26.cloned.1.call-update
  525.5 0.0 reduce-scatter.12.cloned.1.call-start
  525.6 47.9 %all-gather.26.cloned.1.call-done = f32[640,2560]{0,1:T(8,128)} async-done(((f32[640,320]{0,1:T(8,128)}), f32[640,2560]{0,1:T(8,128)}) %all-gather.26.cloned.1.call-update) | async-done | bytes 6553616 | tf_op jit(solution)/shard_map/all_gather | solution.py:25
  573.5 15.1 %fusion.15 = f32[2560,320]{1,0:T(8,128)} fusion(f32[640,2560]{0,1:T(8,128)} %all-gather.26.cloned.1.call-done, f32[640,320]{0,1:T(8,128)} %fusion.4), kind=kOutput, calls=%fused_computation.30 | convolution fusion | flops 6291456000 | bytes 10649600 | tf_op jit(solution)/shard_map/dot_general | solution.py:11
  588.6 0.0 reduce-scatter.12.cloned.1.call-update
  588.6 0.0 all-gather.28.cloned.1.call-start
  588.6 72.6 %reduce-scatter.12.cloned.1.call-done = f32[640,320]{1,0:T(8,128)} async-done(((f32[2560,320]{1,0:T(8,128)}), f32[640,320]{1,0:T(8,128)}) %reduce-scatter.12.cloned.1.call-update) | async-done | bytes 819216 | tf_op jit(solution)/shard_map/reduce_scatter | solution.py:71
  661.3 0.0 all-gather.28.cloned.1.call-update
  661.3 0.0 all-gather.12.cloned.1.call-start
  661.3 0.7 all-gather.12.cloned.1.call-update
  662.0 0.3 all-gather.30.cloned.1.call-start
  662.3 74.8 %all-gather.28.cloned.1.call-done = f32[2560,320]{1,0:T(8,128)} async-done(((f32[640,320]{1,0:T(8,128)}), f32[2560,320]{1,0:T(8,128)}) %all-gather.28.cloned.1.call-update) | async-done | bytes 3276816 | tf_op jit(solution)/shard_map/all_gather | solution.py:74
  737.1 12.1 %fusion.5 = f32[640,320]{0,1:T(8,128)} fusion(f32[640,2560]{0,1:T(8,128)} %all-gather.26.cloned.1.call-done, f32[2560,320]{1,0:T(8,128)} %all-gather.28.cloned.1.call-done, f32[640,320]{0,1:T(8,128)S(1)} %copy-done.1), kind=kOutput, calls=%fused_computation.10 | convolution fusion | flops 6292070400 | bytes 11468800 | tf_op jit(solution)/shard_map/dot_general | solution.py:11
  749.3 0.0 reduce-scatter.6.cloned.1.call-start
  749.3 37.7 %all-gather.12.cloned.1.call-done = f32[640,2560]{0,1:T(8,128)} async-done(((f32[640,320]{0,1:T(8,128)}), f32[640,2560]{0,1:T(8,128)}) %all-gather.12.cloned.1.call-update) | async-done | bytes 6553616 | tf_op jit(solution)/shard_map/all_gather | solution.py:25
  787.0 11.4 %convolution_bitcast_fusion = f32[2560,320]{0,1:T(8,128)} fusion(f32[640,2560]{0,1:T(8,128)} %all-gather.12.cloned.1.call-done, bf16[640,320]{0,1:T(8,128)(2,1)S(1)} %copy-done.3, f32[]{:T(128)S(6)} %min.3), kind=kOutput, calls=%fused_computation | convolution fusion | flops 6291865600 | bytes 10240004 | tf_op jit(solution)/shard_map/dot_general | solution.py:11
  798.4 0.0 reduce-scatter.6.cloned.1.call-update
  798.5 0.3 reduce-scatter.14.cloned.1.call-start
  798.8 37.4 %all-gather.30.cloned.1.call-done = f32[640,2560]{0,1:T(8,128)} async-done(((f32[640,320]{0,1:T(8,128)}), f32[640,2560]{0,1:T(8,128)}) %all-gather.30.cloned.1.call-update) | async-done | bytes 6553616 | tf_op jit(solution)/shard_map/all_gather | solution.py:25
  836.2 14.8 %fusion.16 = f32[2560,320]{1,0:T(8,128)} fusion(f32[640,2560]{0,1:T(8,128)} %all-gather.30.cloned.1.call-done, f32[640,320]{0,1:T(8,128)S(1)} %copy-done), kind=kOutput, calls=%fused_computation.31 | convolution fusion | flops 6291456000 | bytes 10649600 | tf_op jit(solution)/shard_map/dot_general | solution.py:11
  851.0 0.0 reduce-scatter.14.cloned.1.call-update
  851.1 0.0 all-gather.14.cloned.1.call-start
  851.2 49.4 %reduce-scatter.6.cloned.1.call-done = f32[640,320]{0,1:T(8,128)} async-done(((f32[2560,320]{0,1:T(8,128)}), f32[640,320]{0,1:T(8,128)}) %reduce-scatter.6.cloned.1.call-update) | async-done | bytes 819216 | tf_op jit(solution)/shard_map/reduce_scatter | solution.py:48
  900.5 2.8 add_divide_fusion
  903.3 0.3 all-gather.32.cloned.1.call-start
  903.7 72.2 %reduce-scatter.14.cloned.1.call-done = f32[640,320]{1,0:T(8,128)} async-done(((f32[2560,320]{1,0:T(8,128)}), f32[640,320]{1,0:T(8,128)}) %reduce-scatter.14.cloned.1.call-update) | async-done | bytes 819216 | tf_op jit(solution)/shard_map/reduce_scatter | solution.py:71
  975.9 0.0 all-gather.32.cloned.1.call-update
  975.9 0.6 divide_subtract_fusion
  976.5 65.2 %all-gather.14.cloned.1.call-done = f32[2560,320]{0,1:T(8,128)} async-done(((f32[640,320]{0,1:T(8,128)}), f32[2560,320]{0,1:T(8,128)}) %all-gather.14.cloned.1.call-update) | async-done | bytes 3276816 | tf_op jit(solution)/shard_map/all_gather | solution.py:62
  1041.7 11.7 %convolution_bitcast_fusion.1 = f32[640,320]{0,1:T(8,128)} fusion(f32[2560,320]{0,1:T(8,128)} %all-gather.14.cloned.1.call-done, f32[640,2560]{0,1:T(8,128)} %all-gather.12.cloned.1.call-done), kind=kOutput, calls=%fused_computation.5 | convolution fusion | flops 6291456000 | bytes 10649600 | tf_op jit(solution)/shard_map/dot_general | solution.py:11
  1053.4 64.7 %all-gather.32.cloned.1.call-done = f32[2560,320]{1,0:T(8,128)} async-done(((f32[640,320]{1,0:T(8,128)}), f32[2560,320]{1,0:T(8,128)}) %all-gather.32.cloned.1.call-update) | async-done | bytes 3276816 | tf_op jit(solution)/shard_map/all_gather | solution.py:74
  1118.1 12.1 %fusion.6 = f32[640,320]{0,1:T(8,128)} fusion(f32[640,2560]{0,1:T(8,128)} %all-gather.30.cloned.1.call-done, f32[2560,320]{1,0:T(8,128)} %all-gather.32.cloned.1.call-done, f32[640,320]{0,1:T(8,128)S(1)} %copy-done), kind=kOutput, calls=%fused_computation.11 | convolution fusion | flops 6292070400 | bytes 11468800 | tf_op jit(solution)/shard_map/dot_general | solution.py:11
  (24 shorter events, 0.1 us)
Async XLA Ops:
  7.2 49.4 %all-gather.16.cloned.1.call-start = ((), (), s32[]{:S(2)}) async-start(), calls=%async_computation.8 | async-start | bytes 2048000 | tf_op jit(solution)/shard_map/all_gather | solution.py:51
  7.9 126.0 %reduce-scatter.8.cloned.1.call-start = ((), (), s32[]{:S(2)}) async-start(), calls=%async_computation.9 | async-start | bytes 7372800 | tf_op jit(solution)/shard_map/reduce_scatter | solution.py:55
  71.3 62.6 %copy-start.6 = (f32[640,320]{0,1:T(8,128)S(1)}, f32[640,320]{0,1:T(8,128)}, u32[]{:S(2)}) copy-start(f32[640,320]{0,1:T(8,128)} %param.11) | copy-start | bytes 2457604
  71.4 127.4 %all-gather.20.cloned.1.call-start = ((), (), s32[]{:S(2)}) async-start(), calls=%async_computation.11 | async-start | bytes 4096000 | tf_op jit(solution)/shard_map/all_gather | solution.py:65
  72.1 176.9 %all-gather.18.cloned.1.call-start = ((), (), s32[]{:S(2)}) async-start(), calls=%async_computation.10 | async-start | bytes 7372800 | tf_op jit(solution)/shard_map/all_gather | solution.py:25
  136.1 213.5 %all-gather.22.cloned.1.call-start = ((), (), s32[]{:S(2)}) async-start(), calls=%async_computation.12 | async-start | bytes 7372800 | tf_op jit(solution)/shard_map/all_gather | solution.py:25
  301.8 135.6 %reduce-scatter.10.cloned.1.call-start = ((), (), s32[]{:S(2)}) async-start(), calls=%async_computation.13 | async-start | bytes 4915200 | tf_op jit(solution)/shard_map/reduce_scatter | solution.py:71
  364.7 148.7 %copy-start.2 = (f32[640,320]{0,1:T(8,128)S(1)}, f32[640,320]{0,1:T(8,128)}, u32[]{:S(2)}) copy-start(f32[640,320]{0,1:T(8,128)} %broadcast_multiply_fusion) | copy-start | bytes 2457604
  364.7 148.7 %all-gather.24.cloned.1.call-start = ((), (), s32[]{:S(2)}) async-start(), calls=%async_computation.14 | async-start | bytes 4915200 | tf_op jit(solution)/shard_map/all_gather | solution.py:74
  437.4 136.1 %all-gather.26.cloned.1.call-start = ((), (), s32[]{:S(2)}) async-start(), calls=%async_computation.15 | async-start | bytes 7372800 | tf_op jit(solution)/shard_map/all_gather | solution.py:25
  525.5 135.8 %reduce-scatter.12.cloned.1.call-start = ((), (), s32[]{:S(2)}) async-start(), calls=%async_computation.16 | async-start | bytes 4915200 | tf_op jit(solution)/shard_map/reduce_scatter | solution.py:71
  588.6 148.6 %copy-start.1 = (f32[640,320]{0,1:T(8,128)S(1)}, f32[640,320]{0,1:T(8,128)}, u32[]{:S(2)}) copy-start(f32[640,320]{0,1:T(8,128)} %fusion.4) | copy-start | bytes 2457604
  588.6 148.6 %all-gather.28.cloned.1.call-start = ((), (), s32[]{:S(2)}) async-start(), calls=%async_computation.17 | async-start | bytes 4915200 | tf_op jit(solution)/shard_map/all_gather | solution.py:74
  661.3 125.8 %all-gather.12.cloned.1.call-start = ((), (), s32[]{:S(2)}) async-start(), calls=%async_computation.5 | async-start | bytes 7372800 | tf_op jit(solution)/shard_map/all_gather | solution.py:25
  662.0 125.0 %copy-start.3 = (bf16[640,320]{0,1:T(8,128)(2,1)S(1)}, bf16[640,320]{0,1:T(8,128)(2,1)}, u32[]{:S(2)}) copy-start(bf16[640,320]{0,1:T(8,128)(2,1)} %param.9) | copy-start | bytes 1228804
  662.0 174.1 %all-gather.30.cloned.1.call-start = ((), (), s32[]{:S(2)}) async-start(), calls=%async_computation.18 | async-start | bytes 7372800 | tf_op jit(solution)/shard_map/all_gather | solution.py:25
  749.3 86.9 %copy-start = (f32[640,320]{0,1:T(8,128)S(1)}, f32[640,320]{0,1:T(8,128)}, u32[]{:S(2)}) copy-start(f32[640,320]{0,1:T(8,128)} %fusion.5) | copy-start | bytes 2457604
  749.3 151.3 %reduce-scatter.6.cloned.1.call-start = ((), (), s32[]{:S(2)}) async-start(), calls=%async_computation.6 | async-start | bytes 4096000 | tf_op jit(solution)/shard_map/reduce_scatter | solution.py:48
  798.5 177.4 %reduce-scatter.14.cloned.1.call-start = ((), (), s32[]{:S(2)}) async-start(), calls=%async_computation.19 | async-start | bytes 4915200 | tf_op jit(solution)/shard_map/reduce_scatter | solution.py:71
  851.0 49.5 %copy-start.4 = (f32[640,320]{0,1:T(8,128)S(1)}, f32[640,320]{0,1:T(8,128)}, u32[]{:S(2)}) copy-start(f32[640,320]{0,1:T(8,128)} %param.14) | copy-start | bytes 2457604
  851.0 49.5 %copy-start.5 = (f32[640,320]{0,1:T(8,128)S(1)}, f32[640,320]{0,1:T(8,128)}, u32[]{:S(2)}) copy-start(f32[640,320]{0,1:T(8,128)} %param.13) | copy-start | bytes 2457604
  851.1 124.8 %copy-start.7 = (f32[2,640]{1,0:T(2,128)S(1)}, f32[2,640]{1,0:T(2,128)}, u32[]{:S(2)}) copy-start(f32[2,640]{1,0:T(2,128)} %param.10) | copy-start | bytes 15364
  851.1 124.8 %copy-start.8 = (f32[2,640]{1,0:T(2,128)S(1)}, f32[2,640]{1,0:T(2,128)}, u32[]{:S(2)}) copy-start(f32[2,640]{1,0:T(2,128)} %param.15) | copy-start | bytes 15364
  851.1 124.8 %copy-start.9 = (f32[2,640]{1,0:T(2,128)S(1)}, f32[2,640]{1,0:T(2,128)}, u32[]{:S(2)}) copy-start(f32[2,640]{1,0:T(2,128)} %param.16) | copy-start | bytes 15364
  851.1 124.8 %copy-start.10 = (f32[2,640]{1,0:T(2,128)S(1)}, f32[2,640]{1,0:T(2,128)}, u32[]{:S(2)}) copy-start(f32[2,640]{1,0:T(2,128)} %param.17) | copy-start | bytes 15364
  851.1 190.6 %all-gather.14.cloned.1.call-start = ((), (), s32[]{:S(2)}) async-start(), calls=%async_computation.7 | async-start | bytes 4096000 | tf_op jit(solution)/shard_map/all_gather | solution.py:62
  903.3 214.8 %all-gather.32.cloned.1.call-start = ((), (), s32[]{:S(2)}) async-start(), calls=%async_computation.20 | async-start | bytes 4915200 | tf_op jit(solution)/shard_map/all_gather | solution.py:74
Sparse Core Ops, SparseCore 0:
  9.6 39.6 all-gather.15
  71.5 62.3 reduce-scatter.7
  135.5 63.1 all-gather.19
  201.3 47.6 all-gather.17
  301.9 47.5 all-gather.21
  364.8 72.5 reduce-scatter.9
  439.0 74.3 all-gather.23
  525.6 47.8 all-gather.25
  588.7 72.5 reduce-scatter.11
  662.8 74.3 all-gather.27
  739.2 47.8 all-gather.11
  789.5 46.6 all-gather.29
  838.6 61.8 reduce-scatter.5
  902.8 73.0 reduce-scatter.13
  977.9 63.7 all-gather.13
  1043.2 74.8 all-gather.31
where the time goes:
time: 1150 us; the launch traced here: 1140 us
  waiting for transfers between devices  894 us (78%)
  matrix products  131 us (11%)
  blocking collectives  82.9 us (7%)
  between operations  17.3 us (2%)
    all_gather x5, waiting for transfers between devices, row_panel(): lax.all_gather(local_block, ('tensor', 'section'), axis=1, tiled=True)  221 us
    reduce_scatter x3, waiting for transfers between devices, on_device(): lax.psum_scatter(transposed_terms(iterate_rows, iterate), 'shard', scatte...  217 us
    all_gather x3, waiting for transfers between devices, on_device(): lax.all_gather(gram_block, 'shard', axis=0, tiled=True)  215 us
    dot_general x10, matrix products, matmul(): jnp.dot(left_side, right_side, precision=lax.Precision.HIGHEST, preferred...  131 us
    all_gather x1, waiting for transfers between devices, on_device(): lax.all_gather(direction, 'shard', axis=0, tiled=True)  65.2 us
    all_gather x1, waiting for transfers between devices, on_device(): lax.all_gather(left_basis, 'shard', axis=0, tiled=True)  62.1 us
    reduce_scatter x1, waiting for transfers between devices, on_device(): lax.psum_scatter(outer_rows, ('tensor', 'section'), scatter_dimension=1,...  61.7 us
    reduce_scatter x1, waiting for transfers between devices, on_device(): lax.psum_scatter(transposed_terms(basis_rows, clipped), 'shard', scatter_...  49.4 us
  transfers between devices with their start and end apart: 16, of which 15 were waited for; matrix products, arithmetic and copies ran while one was open for 5% of the time, Pallas kernels for 0%

commit v1 on v0

v1 whole, which is shorter than its diff:
```python
import jax
import jax.numpy as jnp
from jax import lax
from jax.sharding import PartitionSpec as P

D = 2560
NS_STEPS = 3
GROUP = ("tensor", "section")
EVERY = ("shard", "tensor", "section")
PAD = 16


def matmul(left_side, right_side):
    return jnp.dot(
        left_side, right_side, precision=lax.Precision.HIGH, preferred_element_type=jnp.float32
    )


def row_panel(local_block):
    return lax.all_gather(local_block, GROUP, axis=1, tiled=True)


def pack(block):
    top = jnp.max(jnp.abs(block), axis=0, keepdims=True)
    power = jnp.clip(jnp.ceil(jnp.log2(jnp.maximum(top, 1e-30))) - 14.0, -110.0, 120.0)
    scaled = block * jnp.exp2(-power)
    tail = jnp.broadcast_to(power, (PAD, block.shape[1]))
    return jnp.concatenate([scaled, tail], axis=0).astype(jnp.float16)


def unpack(payload):
    values = payload.astype(jnp.float32)
    return values[..., :-PAD, :] * jnp.exp2(values[..., -PAD : -PAD + 1, :])


def shift_pairs(shards, offset):
    return [(source, (source + offset) % shards) for source in range(shards)]


def scatter_sum(partial, shards, place):
    rows = partial.shape[0] // shards
    if shards > 8:
        return lax.psum_scatter(partial, "shard", scatter_dimension=0, tiled=True)
    total = lax.dynamic_slice_in_dim(partial, place * rows, rows, 0)
    for offset in range(1, shards):
        target = (place + offset) % shards
        chunk = lax.dynamic_slice_in_dim(partial, target * rows, rows, 0)
        total = total + unpack(
            lax.ppermute(pack(chunk), "shard", shift_pairs(shards, offset))
        )
    return total


def outer_block(gradient, shards, group, place, member):
    rows, cols = gradient.shape
    if rows % cols == 0 and shards <= 8:
        grad_rows = row_panel(gradient)
        own = lax.dynamic_slice_in_dim(grad_rows, (member * cols) % rows, cols, 0)
        other = jnp.zeros_like(own)
        for offset in range(1, shards):
            pairs = []
            for column in range(group):
                home = column * cols // rows
                pairs.append(
                    (home * group + column, (home + offset) % shards * group + column)
                )
            other = other + lax.ppermute(own, EVERY, pairs)
        partner = jnp.where(place == member * cols // rows, own, other)
        return jnp.dot(grad_rows, partner.T, preferred_element_type=jnp.float32)
    partner = lax.all_gather(gradient, "shard", axis=0, tiled=True)
    product = jnp.dot(gradient, partner.T, preferred_element_type=jnp.float32)
    return lax.psum_scatter(product, GROUP, scatter_dimension=1, tiled=True)


def on_device(
    gradient,
    gain_grad,
    left_statistic,
    left_basis,
    first_moment,
    second_moment,
    norm_gains,
    gain_first,
    gain_second,
):
    group = lax.axis_size(GROUP)
    shards = lax.axis_size("shard")
    place = lax.axis_index("shard")
    member = lax.axis_index(GROUP)
    rows, cols = gradient.shape
    grad_float = gradient.astype(jnp.float32)
    local_sum = jnp.sum(grad_float * grad_float) + jnp.sum(gain_grad * gain_grad) / group
    squares_total = lax.psum(local_sum, EVERY)
    clip_factor = jnp.minimum(1.0, D / jnp.sqrt(squares_total + 1e-06))
    outer_part = outer_block(gradient, shards, group, place, member)
    new_statistic = 0.95 * left_statistic + (0.05 / D * clip_factor * clip_factor) * outer_part
    statistic_rows = row_panel(new_statistic)
    basis_columns = lax.all_gather(left_basis, "shard", axis=0, tiled=True)
    power_product = matmul(statistic_rows, basis_columns)
    power_sum = lax.psum(jnp.sum(power_product * power_product), EVERY)
    power_rows = row_panel(power_product)
    scale = 0.9 * jnp.sqrt(D / (power_sum + 1e-06))
    iterate = scale * power_product
    iterate_rows = scale * power_rows
    basis_rows = row_panel(left_basis)
    row_index = place * rows + lax.broadcasted_iota(jnp.int32, (rows, cols), 0)
    col_index = member * cols + lax.broadcasted_iota(jnp.int32, (rows, cols), 1)
    eye = (row_index == col_index).astype(jnp.float32)
    for sweep_index in range(NS_STEPS):
        if sweep_index:
            iterate_rows = unpack(row_panel(pack(iterate)))
        gram_block = scatter_sum(matmul(iterate_rows.T, iterate), shards, place)
        gathered = lax.all_gather(pack(gram_block - eye), "shard", axis=0)
        excess = unpack(gathered).reshape(D, cols)
        iterate = iterate - 0.5 * matmul(iterate_rows, excess)
    rotated = clip_factor * lax.psum_scatter(
        matmul(basis_rows.T, grad_float), "shard", scatter_dimension=0, tiled=True
    )
    new_first = 0.9 * first_moment + 0.1 * rotated
    new_second = 0.95 * second_moment + 0.05 * rotated * rotated
    direction = new_first / (jnp.sqrt(new_second) + 1e-08)
    direction_columns = lax.all_gather(
        direction.astype(jnp.float16), "shard", axis=0, tiled=True
    ).astype(jnp.float32)
    update = matmul(basis_rows, direction_columns)
    gain_clipped = clip_factor * gain_grad
    new_gain_first = 0.9 * gain_first + 0.1 * gain_clipped
    new_gain_second = 0.95 * gain_second + 0.05 * gain_clipped * gain_clipped
    new_gains = norm_gains - 0.01 * new_gain_first / (jnp.sqrt(new_gain_second) + 1e-08)
    return (
        update,
        new_first,
        new_second,
        new_statistic,
        iterate,
        new_gains,
        new_gain_first,
        new_gain_second,
    )


def solution(mesh):
    matrix = P("shard", GROUP)
    vector = P(None, "shard")
    return jax.shard_map(
        on_device,
        mesh=mesh,
        in_specs=(
            matrix,
            vector,
            matrix,
            matrix,
            matrix,
            matrix,
            vector,
            vector,
            vector,
        ),
        out_specs=(matrix, matrix, matrix, matrix, matrix, vector, vector, vector),
        check_vma=False,
    )
```

time: 1150 us -> 895 us (0.78)
  waiting for transfers between devices: 894 us -> 250 us
  blocking collectives: 82.9 us -> 493 us
  matrix products: 131 us -> 58.4 us
  local copies, waits for them, and re-layouts: 0.06 us -> 23.3 us
  starting transfers between devices: 2.1 us -> 19.4 us
  other arithmetic: 9.63 us -> 23.5 us
    all_gather x11 -> x5, waiting for transfers between devices: 564 us -> 121 us  [the longest x4 121 us: row_panel(): return lax.all_gather(local_block, GROUP, axis=1, tiled=True)]
    all_gather x0 -> x6, blocking collectives: none -> 330 us  [the longest x2 155 us: row_panel(): return lax.all_gather(local_block, GROUP, axis=1, tiled=True)]
    reduce_scatter x5 -> x1, waiting for transfers between devices: 329 us -> 91.7 us  [on_device(): lax.psum_scatter(matmul(basis_rows.T, grad_float), 'shard', scatter_dimen...]
    psum x2, blocking collectives: 82.9 us -> 163 us  [the longest x1 123 us: on_device(): squares_total = lax.psum(local_sum, EVERY)]
    dot_general x10, matrix products: 131 us -> 58.4 us  [the longest x9 52.1 us: matmul(): jnp.dot(left_side, right_side, precision=lax.Precision.HIGH, preferred_el...]
    ppermute x0 -> x12, waiting for transfers between devices: none -> 35.7 us  [the longest x9 35.7 us: scatter_sum(): lax.ppermute(pack(chunk), 'shard', shift_pairs(shards, offset))]
    ppermute x0 -> x12, starting transfers between devices: none -> 18.6 us  [the longest x9 13.7 us: scatter_sum(): lax.ppermute(pack(chunk), 'shard', shift_pairs(shards, offset))]
    ppermute x0 -> x3, local copies, waits for them, and re-layouts: none -> 11.6 us  [outer_block(): other = other + lax.ppermute(own, EVERY, pairs)]
  transfers between devices with their start and end apart: 16 -> 18, of which waited for: 15 -> 8; matrix products, arithmetic and copies ran while one was open for 5% -> 7% of each run, Pallas kernels for 0% -> 0%
where the time goes in v1:
time: 895 us; the launch traced here: 886 us
  blocking collectives  493 us (55%)
  waiting for transfers between devices  250 us (28%)
  matrix products  58.4 us (7%)
  other arithmetic  23.5 us (3%)
  local copies, waits for them, and re-layouts  23.3 us (3%)
  starting transfers between devices  19.4 us (2%)
  between operations  17.8 us (2%)
    all_gather x2, blocking collectives, row_panel(): return lax.all_gather(local_block, GROUP, axis=1, tiled=True)  155 us
    psum x1, blocking collectives, on_device(): squares_total = lax.psum(local_sum, EVERY)  123 us
    all_gather x4, waiting for transfers between devices, row_panel(): return lax.all_gather(local_block, GROUP, axis=1, tiled=True)  121 us
    all_gather x3, blocking collectives, on_device(): gathered = lax.all_gather(pack(gram_block - eye), 'shard', axis=0)  106 us
    reduce_scatter x1, waiting for transfers between devices, on_device(): lax.psum_scatter(matmul(basis_rows.T, grad_float), 'shard', scatter_dimen...  91.7 us
    all_gather x1, blocking collectives, on_device(): lax.all_gather(direction.astype(jnp.float16), 'shard', axis=0, tiled=True)  69.6 us
    dot_general x9, matrix products, matmul(): jnp.dot(left_side, right_side, precision=lax.Precision.HIGH, preferred_el...  52.1 us
    psum x1, blocking collectives, on_device(): power_sum = lax.psum(jnp.sum(power_product * power_product), EVERY)  39.9 us
  transfers between devices with their start and end apart: 18, of which 8 were waited for; matrix products, arithmetic and copies ran while one was open for 7% of the time, Pallas kernels for 0%

profile of v1, /device:TPU:8, one launch (start us, length us, event | category | flops | bytes accessed | tf_op | source)
XLA Modules:
  0.0 886.1 jit_solution(3843210332075015325)
XLA Ops:
  7.2 0.7 all-gather.14.cloned.1.call-update
  7.9 0.7 all-gather.18.cloned.1.call-update
  8.7 35.2 %all-gather.14.cloned.1.call-done = bf16[640,2560]{0,1:T(8,128)(2,1)} async-done(((bf16[640,320]{0,1:T(8,128)(2,1)}), bf16[640,2560]{0,1:T(8,128)(2,1)}) %all-gather.14.cloned.1.call-update) | async-done | bytes 3276816 | tf_op jit(solution)/shard_map/all_gather | solution.py:20
  43.9 2.8 constant_dynamic-slice_fusion
  46.7 3.4 copy.24
  50.1 1.3 collective-permute-start
  51.4 1.8 collective-permute-start.1
  53.2 1.8 collective-permute-start.2
  55.0 0.6 multiply_reduce_fusion.2
  56.3 0.8 multiply_reduce_fusion.1
  57.8 123.0 %psum.14 = f32[]{:T(128)} all-reduce(f32[]{:T(128)S(6)} %add.276), channel_id=1, replica_groups=mesh['shard'=4,'tensor'=2,'section'=4] {'shard','tensor','section'}, use_global_device_ids=true, to_apply=%region_2.0 | all-reduce | flops 1 | bytes 8 | tf_op jit(solution)/shard_map/psum | solution.py:93
  181.5 3.8 copy.26
  185.4 3.9 copy.27
  189.3 3.9 copy.29
  193.2 6.3 fusion.37
  199.5 0.5 all-gather.12.cloned.1.call-update
  200.1 46.5 %all-gather.16.cloned.1.call-done = f32[640,2560]{0,1:T(8,128)} async-done(((f32[640,320]{0,1:T(8,128)}), f32[640,2560]{0,1:T(8,128)}) %all-gather.16.cloned.1.call-update) | async-done | bytes 6553616 | tf_op jit(solution)/shard_map/all_gather | solution.py:20
  246.7 9.4 %multiply_reduce_fusion = (f32[]{:T(128)}, f32[640,320]{0,1:T(8,128)}) fusion(f32[640,2560]{0,1:T(8,128)} %all-gather.16.cloned.1.call-done, f32[2560,320]{0,1:T(8,128)} %all-gather.18.cloned.1.call-done), kind=kOutput, calls=%fused_computation.94 | convolution fusion | flops 3146137600 | bytes 10649604 | tf_op jit(solution)/shard_map/dot_general | solution.py:14
  256.1 0.6 reduce-scatter.2.cloned.1.call-start
  256.7 38.4 %all-gather.12.cloned.1.call-done = f32[640,2560]{0,1:T(8,128)} async-done(((f32[640,320]{0,1:T(8,128)}), f32[640,2560]{0,1:T(8,128)}) %all-gather.12.cloned.1.call-update) | async-done | bytes 6553616 | tf_op jit(solution)/shard_map/all_gather | solution.py:20
  295.1 7.3 fusion.101
  302.4 0.6 copy-done.3
  303.1 0.6 divide_subtract_fusion
  303.7 39.9 %psum.15 = f32[]{:T(128)} all-reduce(f32[]{:T(128)} %get-tuple-element.66), channel_id=1, replica_groups=mesh['shard'=4,'tensor'=2,'section'=4] {'shard','tensor','section'}, use_global_device_ids=true, to_apply=%region_5.6 | all-reduce | flops 1 | bytes 8 | tf_op jit(solution)/shard_map/psum | solution.py:100
  344.3 1.0 all-gather.20.cloned.1.call-done
  345.3 6.5 fusion.2
  352.5 0.9 pad_maximum_fusion
  353.4 1.5 collective-permute-start.3
  355.0 0.9 pad_maximum_fusion.1
  356.0 1.4 collective-permute-start.4
  357.5 0.9 pad_maximum_fusion.2
  358.4 1.5 collective-permute-start.5
  359.9 91.7 %reduce-scatter.2.cloned.1.call-done = f32[640,320]{0,1:T(8,128)} async-done(((f32[2560,320]{0,1:T(8,128)}), f32[640,320]{0,1:T(8,128)}) %reduce-scatter.2.cloned.1.call-update) | async-done | bytes 819216 | tf_op jit(solution)/shard_map/reduce_scatter | solution.py:116
  451.6 3.3 divide_convert_fusion
  454.9 1.1 convert_element_type.89
  456.0 1.1 convert_element_type.90
  457.4 1.1 convert_element_type.91
  458.7 0.5 abs_reduce_fusion.10
  459.6 34.8 %all-gather.21 = f16[4,656,320]{1,2,0:T(8,128)(2,1)S(1)} all-gather(f16[1,656,320]{1,2,0:T(8,128)(2,1)S(1)} %pad_maximum_fusion.3), channel_id=1, replica_groups=mesh['shard'=4,'tensor'=2,'section'=4] {'shard'}, dimensions={0}, use_global_device_ids=true | all-gather | bytes 2099200 | tf_op jit(solution)/shard_map/all_gather | solution.py:113
  495.8 1.2 slice-done
  496.9 0.8 slice-done.1
  498.0 4.6 abs_reduce_fusion.9
  503.0 77.1 %all-gather.22 = f16[656,2560]{0,1:T(8,128)(2,1)S(1)} all-gather(f16[656,320]{0,1:T(8,128)(2,1)S(1)} %pad_maximum_fusion.4), channel_id=1, replica_groups=mesh['shard'=4,'tensor'=2,'section'=4] {'tensor','section'}, dimensions={1}, use_global_device_ids=true | all-gather | bytes 3778560 | tf_op jit(solution)/shard_map/all_gather | solution.py:20
  580.1 0.6 convert_element_type.94
  581.1 4.3 fusion.5
  586.3 0.9 collective-permute-start.6
  587.5 2.8 collective-permute-start.7
  590.5 0.8 collective-permute-start.8
  591.2 69.6 %all-gather.26 = f16[2560,320]{0,1:T(8,128)(2,1)S(1)} all-gather(f16[640,320]{0,1:T(8,128)(2,1)S(1)} %get-tuple-element.26), channel_id=1, replica_groups=mesh['shard'=4,'tensor'=2,'section'=4] {'shard'}, dimensions={0}, use_global_device_ids=true | all-gather | bytes 2048000 | tf_op jit(solution)/shard_map/all_gather | solution.py:122
  661.5 0.5 abs_reduce_fusion.5
  662.4 34.4 %all-gather.23 = f16[4,656,320]{1,2,0:T(8,128)(2,1)S(1)} all-gather(f16[1,656,320]{1,2,0:T(8,128)(2,1)S(1)} %pad_maximum_fusion.8), channel_id=1, replica_groups=mesh['shard'=4,'tensor'=2,'section'=4] {'shard'}, dimensions={0}, use_global_device_ids=true | all-gather | bytes 2099200 | tf_op jit(solution)/shard_map/all_gather | solution.py:113
  698.2 4.7 abs_reduce_fusion.4
  703.3 77.6 %all-gather.24 = f16[656,2560]{0,1:T(8,128)(2,1)S(1)} all-gather(f16[656,320]{0,1:T(8,128)(2,1)S(1)} %pad_maximum_fusion.9), channel_id=1, replica_groups=mesh['shard'=4,'tensor'=2,'section'=4] {'tensor','section'}, dimensions={1}, use_global_device_ids=true | all-gather | bytes 3778560 | tf_op jit(solution)/shard_map/all_gather | solution.py:20
  780.9 0.6 convert_element_type.99
  782.0 4.3 fusion.7
  787.2 3.2 collective-permute-start.9
  790.7 1.1 collective-permute-start.10
  792.0 0.5 collective-permute-start.11
  792.5 5.6 convolution_bitcast_fusion
  798.2 25.0 %collective-permute-done.9 = f16[656,320]{0,1:T(8,128)(2,1)S(1)} collective-permute-done((f16[656,320]{0,1:T(8,128)(2,1)S(1)}, f16[656,320]{0,1:T(8,128)(2,1)S(1)}, u32[]{:S(2)}, u32[]{:S(2)}) %collective-permute-start.9) | collective-permute-done | bytes 419872 | tf_op jit(solution)/shard_map/ppermute | solution.py:49
  823.2 10.3 %collective-permute-done.10 = f16[656,320]{0,1:T(8,128)(2,1)S(1)} collective-permute-done((f16[656,320]{0,1:T(8,128)(2,1)S(1)}, f16[656,320]{0,1:T(8,128)(2,1)S(1)}, u32[]{:S(2)}, u32[]{:S(2)}) %collective-permute-start.10) | collective-permute-done | bytes 419872 | tf_op jit(solution)/shard_map/ppermute | solution.py:49
  834.5 0.5 abs_reduce_fusion
  835.4 36.8 %all-gather.25 = f16[4,656,320]{1,2,0:T(8,128)(2,1)S(1)} all-gather(f16[1,656,320]{1,2,0:T(8,128)(2,1)S(1)} %pad_maximum_fusion.13), channel_id=1, replica_groups=mesh['shard'=4,'tensor'=2,'section'=4] {'shard'}, dimensions={0}, use_global_device_ids=true | all-gather | bytes 2099200 | tf_op jit(solution)/shard_map/all_gather | solution.py:113
  873.6 5.5 fusion.41
  (120 shorter events, 13.0 us)
Async XLA Ops:
  7.2 36.8 %all-gather.14.cloned.1.call-start = ((), (), s32[]{:S(2)}) async-start(), calls=%async_computation.3 | async-start | bytes 3686400 | tf_op jit(solution)/shard_map/all_gather | solution.py:20
  7.9 192.2 %all-gather.18.cloned.1.call-start = ((), (), s32[]{:S(2)}) async-start(), calls=%async_computation.5 | async-start | bytes 4096000 | tf_op jit(solution)/shard_map/all_gather | solution.py:98
  8.7 238.0 %all-gather.16.cloned.1.call-start = ((), (), s32[]{:S(2)}) async-start(), calls=%async_computation.4 | async-start | bytes 7372800 | tf_op jit(solution)/shard_map/all_gather | solution.py:20
  8.7 46.3 %copy-start.2 = (f32[2,640]{1,0:T(2,128)S(1)}, f32[2,640]{1,0:T(2,128)}, u32[]{:S(2)}) copy-start(f32[2,640]{1,0:T(2,128)} %param.10) | copy-start | bytes 15364
  8.7 47.6 %copy-start.1 = (bf16[640,320]{0,1:T(8,128)(2,1)S(1)}, bf16[640,320]{0,1:T(8,128)(2,1)}, u32[]{:S(2)}) copy-start(bf16[640,320]{0,1:T(8,128)(2,1)} %param.9) | copy-start | bytes 1228804
  50.1 131.4 %collective-permute-start = (bf16[320,2560]{1,0:T(8,128)(2,1)}, bf16[320,2560]{1,0:T(8,128)(2,1)}, u32[]{:S(2)}, u32[]{:S(2)}) collective-permute-start(bf16[320,2560]{1,0:T(8,128)(2,1)} %copy.24), channel_id=1, source_target_pairs={{0,8},{1,9},{10,18},{11,19},{20,28},{21,29},{30,6},{31,7}} | collective-permute-start | bytes 4915208 | tf_op jit(solution)/shard_map/ppermute | solution.py:67
  51.4 134.0 %collective-permute-start.1 = (bf16[320,2560]{1,0:T(8,128)(2,1)}, bf16[320,2560]{1,0:T(8,128)(2,1)}, u32[]{:S(2)}, u32[]{:S(2)}) collective-permute-start(bf16[320,2560]{1,0:T(8,128)(2,1)} %copy.24), channel_id=1, source_target_pairs={{0,16},{1,17},{10,26},{11,27},{20,4},{21,5},{30,14},{31,15}} | collective-permute-start | bytes 4915208 | tf_op jit(solution)/shard_map/ppermute | solution.py:67
  53.2 136.1 %collective-permute-start.2 = (bf16[320,2560]{1,0:T(8,128)(2,1)}, bf16[320,2560]{1,0:T(8,128)(2,1)}, u32[]{:S(2)}, u32[]{:S(2)}) collective-permute-start(bf16[320,2560]{1,0:T(8,128)(2,1)} %copy.24), channel_id=1, source_target_pairs={{0,24},{1,25},{10,2},{11,3},{20,12},{21,13},{30,22},{31,23}} | collective-permute-start | bytes 4915208 | tf_op jit(solution)/shard_map/ppermute | solution.py:67
  185.4 7.8 copy-start.6
  199.5 95.6 %all-gather.12.cloned.1.call-start = ((), (), s32[]{:S(2)}) async-start(), calls=%async_computation.1 | async-start | bytes 7372800 | tf_op jit(solution)/shard_map/all_gather | solution.py:20
  200.1 145.3 %all-gather.20.cloned.1.call-start = ((), (), s32[]{:S(2)}) async-start(), calls=%async_computation.6 | async-start | bytes 7372800 | tf_op jit(solution)/shard_map/all_gather | solution.py:20
  256.1 195.5 %reduce-scatter.2.cloned.1.call-start = ((), (), s32[]{:S(2)}) async-start(), calls=%async_computation.2 | async-start | bytes 4096000 | tf_op jit(solution)/shard_map/reduce_scatter | solution.py:116
  302.3 0.7 copy-start.3
  302.3 0.7 copy-start.4
  302.3 0.7 copy-start.5
  353.4 101.4 %collective-permute-start.3 = (f16[656,320]{0,1:T(8,128)(2,1)}, f16[656,320]{0,1:T(8,128)(2,1)}, u32[]{:S(2)}, u32[]{:S(2)}) collective-permute-start(f16[656,320]{0,1:T(8,128)(2,1)} %pad_maximum_fusion), channel_id=1, source_target_pairs={{0,8},{8,16},{16,24},{24,0},{1,9},{9,17},{17,25},{25,1},{2,10},{10... | collective-permute-start | bytes 1259528 | tf_op jit(solution)/shard_map/ppermute | solution.py:49
  356.0 100.0 %collective-permute-start.4 = (f16[656,320]{0,1:T(8,128)(2,1)}, f16[656,320]{0,1:T(8,128)(2,1)}, u32[]{:S(2)}, u32[]{:S(2)}) collective-permute-start(f16[656,320]{0,1:T(8,128)(2,1)} %pad_maximum_fusion.1), channel_id=1, source_target_pairs={{0,16},{8,24},{16,0},{24,8},{1,17},{9,25},{17,1},{25,9},{2,18},{10... | collective-permute-start | bytes 1259528 | tf_op jit(solution)/shard_map/ppermute | solution.py:49
  358.4 99.0 %collective-permute-start.5 = (f16[656,320]{0,1:T(8,128)(2,1)}, f16[656,320]{0,1:T(8,128)(2,1)}, u32[]{:S(2)}, u32[]{:S(2)}) collective-permute-start(f16[656,320]{0,1:T(8,128)(2,1)} %pad_maximum_fusion.2), channel_id=1, source_target_pairs={{0,24},{8,0},{16,8},{24,16},{1,25},{9,1},{17,9},{25,17},{2,26},{10... | collective-permute-start | bytes 1259528 | tf_op jit(solution)/shard_map/ppermute | solution.py:49
  494.8 2.2 slice-start
  495.1 2.7 slice-start.1
  495.4 2.6 copy-start
  586.3 74.5 %collective-permute-start.6 = (f16[656,320]{0,1:T(8,128)(2,1)S(1)}, f16[656,320]{0,1:T(8,128)(2,1)S(1)}, u32[]{:S(2)}, u32[]{:S(2)}) collective-permute-start(f16[656,320]{0,1:T(8,128)(2,1)S(1)} %pad_maximum_fusion.5), channel_id=1, source_target_pairs={{0,8},{8,16},{16,24},{24,0},{1,9},{9,17},{17,25},{25,1},{2,10},{10... | collective-permute-start | bytes 1259528 | tf_op jit(solution)/shard_map/ppermute | solution.py:49
  587.5 73.4 %collective-permute-start.7 = (f16[656,320]{0,1:T(8,128)(2,1)S(1)}, f16[656,320]{0,1:T(8,128)(2,1)S(1)}, u32[]{:S(2)}, u32[]{:S(2)}) collective-permute-start(f16[656,320]{0,1:T(8,128)(2,1)S(1)} %pad_maximum_fusion.6), channel_id=1, source_target_pairs={{0,16},{8,24},{16,0},{24,8},{1,17},{9,25},{17,1},{25,9},{2,18},{10... | collective-permute-start | bytes 1259528 | tf_op jit(solution)/shard_map/ppermute | solution.py:49
  590.5 70.8 %collective-permute-start.8 = (f16[656,320]{0,1:T(8,128)(2,1)S(1)}, f16[656,320]{0,1:T(8,128)(2,1)S(1)}, u32[]{:S(2)}, u32[]{:S(2)}) collective-permute-start(f16[656,320]{0,1:T(8,128)(2,1)S(1)} %pad_maximum_fusion.7), channel_id=1, source_target_pairs={{0,24},{8,0},{16,8},{24,16},{1,25},{9,1},{17,9},{25,17},{2,26},{10... | collective-permute-start | bytes 1259528 | tf_op jit(solution)/shard_map/ppermute | solution.py:49
  780.9 11.6 %slice-start.2 = ((s8[6553600]{0:T(1024)(128)(4,1)}), s8[4194304]{0:T(1024)(128)(4,1)S(1)}, s32[]{:S(2)}) async-start(s8[6553600]{0:T(1024)(128)(4,1)} %bitcast.35), calls=%async_computation.9 | async-start | bytes 8388608
  782.0 10.6 %slice-start.3 = ((s8[6553600]{0:T(1024)(128)(4,1)}), s8[2359296]{0:T(1024)(128)(4,1)S(1)}, s32[]{:S(2)}) async-start(s8[6553600]{0:T(1024)(128)(4,1)} %bitcast.35), calls=%async_computation.10 | async-start | bytes 4718592
  787.2 35.9 %collective-permute-start.9 = (f16[656,320]{0,1:T(8,128)(2,1)S(1)}, f16[656,320]{0,1:T(8,128)(2,1)S(1)}, u32[]{:S(2)}, u32[]{:S(2)}) collective-permute-start(f16[656,320]{0,1:T(8,128)(2,1)S(1)} %pad_maximum_fusion.10), channel_id=1, source_target_pairs={{0,8},{8,16},{16,24},{24,0},{1,9},{9,17},{17,25},{25,1},{2,10},{10... | collective-permute-start | bytes 1259528 | tf_op jit(solution)/shard_map/ppermute | solution.py:49
  790.7 42.9 %collective-permute-start.10 = (f16[656,320]{0,1:T(8,128)(2,1)S(1)}, f16[656,320]{0,1:T(8,128)(2,1)S(1)}, u32[]{:S(2)}, u32[]{:S(2)}) collective-permute-start(f16[656,320]{0,1:T(8,128)(2,1)S(1)} %pad_maximum_fusion.11), channel_id=1, source_target_pairs={{0,16},{8,24},{16,0},{24,8},{1,17},{9,25},{17,1},{25,9},{2,18},{10... | collective-permute-start | bytes 1259528 | tf_op jit(solution)/shard_map/ppermute | solution.py:49
  792.0 42.2 %collective-permute-start.11 = (f16[656,320]{0,1:T(8,128)(2,1)S(1)}, f16[656,320]{0,1:T(8,128)(2,1)S(1)}, u32[]{:S(2)}, u32[]{:S(2)}) collective-permute-start(f16[656,320]{0,1:T(8,128)(2,1)S(1)} %pad_maximum_fusion.12), channel_id=1, source_target_pairs={{0,24},{8,0},{16,8},{24,16},{1,25},{9,1},{17,9},{25,17},{2,26},{10... | collective-permute-start | bytes 1259528 | tf_op jit(solution)/shard_map/ppermute | solution.py:49
Sparse Core Ops, SparseCore 0:
  9.9 34.0 all-gather.13
  45.5 88.9 all-gather.17
  199.6 47.0 all-gather.15
  248.4 46.6 all-gather.11
  297.4 47.9 all-gather.19
  347.5 104.0 reduce-scatter.1

commit v2 on v1

--- a/solution.py
+++ b/solution.py
@@ -33,28 +33,89 @@
     return values[..., :-PAD, :] * jnp.exp2(values[..., -PAD : -PAD + 1, :])
 
 
-def shift_pairs(shards, offset):
-    return [(source, (source + offset) % shards) for source in range(shards)]
-
-
-def scatter_sum(partial, shards, place):
-    rows = partial.shape[0] // shards
+def partners(size):
+    if size & (size - 1) == 0:
+        return [[(one, one ^ offset) for one in range(size)] for offset in range(1, size)]
+    return [
+        [(one, (one + offset) % size) for one in range(size)] for offset in range(1, size)
+    ]
+
+
+def place_of_source(place, offset, size):
+    return place ^ offset if size & (size - 1) == 0 else (place - offset) % size
+
+
+def place_of_target(place, offset, size):
+    return place ^ offset if size & (size - 1) == 0 else (place + offset) % size
+
+
+def shard_total(value, shards):
     if shards > 8:
-        return lax.psum_scatter(partial, "shard", scatter_dimension=0, tiled=True)
-    total = lax.dynamic_slice_in_dim(partial, place * rows, rows, 0)
-    for offset in range(1, shards):
-        target = (place + offset) % shards
-        chunk = lax.dynamic_slice_in_dim(partial, target * rows, rows, 0)
-        total = total + unpack(
-            lax.ppermute(pack(chunk), "shard", shift_pairs(shards, offset))
+        return lax.psum(value, "shard")
+    tile = jnp.full((8, 128), value, jnp.float32)
+    total = value
+    for pairs in partners(shards):
+        total = total + lax.ppermute(tile, "shard", pairs)[0, 0]
+    return total
+
+
+def rows_times_shards(full_rows, block, shards, place, encode, decode):
+    if shards > 8:
+        gathered = decode(lax.all_gather(encode(block), "shard", axis=0))
+        return matmul(full_rows, gathered.reshape(-1, block.shape[1]))
+    rows = block.shape[0]
+    sent = encode(block)
+    pieces = [block] + [
+        decode(lax.ppermute(sent, "shard", pairs)) for pairs in partners(shards)
+    ]
+    total = None
+    for offset, piece in enumerate(pieces):
+        source = place_of_source(place, offset, shards)
+        left = lax.dynamic_slice_in_dim(full_rows, source * rows, rows, 1)
+        term = matmul(left, piece)
+        total = term if total is None else total + term
+    return total
+
+
+def scatter_product(full_rows, block, shards, place):
+    if shards > 8:
+        return lax.psum_scatter(
+            matmul(full_rows.T, block), "shard", scatter_dimension=0, tiled=True
         )
+    rows = full_rows.shape[1] // shards
+    arrived = []
+    for offset, pairs in enumerate(partners(shards), 1):
+        target = place_of_target(place, offset, shards)
+        chunk = matmul(lax.dynamic_slice_in_dim(full_rows, target * rows, rows, 1).T, block)
+        arrived.append(lax.ppermute(pack(chunk), "shard", pairs))
+    total = matmul(lax.dynamic_slice_in_dim(full_rows, place * rows, rows, 1).T, block)
+    for payload in arrived:
+        total = total + unpack(payload)
     return total
 
 
-def outer_block(gradient, shards, group, place, member):
+def packed_row_panel(block):
+    sections = lax.axis_size("section")
+    cores = lax.axis_size("tensor")
+    section = lax.axis_index("section")
+    core = lax.axis_index("tensor")
+    own = pack(block)
+    stack = jnp.zeros((cores * sections,) + own.shape, own.dtype)
+    pieces = [own] + [lax.ppermute(own, "section", pairs) for pairs in partners(sections)]
+    for offset, piece in enumerate(pieces):
+        column = place_of_source(section, offset, sections)
+        stack = lax.dynamic_update_index_in_dim(stack, piece, core * sections + column, 0)
+        for shift, pairs in enumerate(partners(cores), 1):
+            other = place_of_source(core, shift, cores)
+            stack = lax.dynamic_update_index_in_dim(
+                stack, lax.ppermute(piece, "tensor", pairs), other * sections + column, 0
+            )
+    return unpack(stack).transpose(1, 0, 2).reshape(block.shape[0], -1)
+
+
+def outer_block(gradient, grad_rows, shards, group, place, member):
     rows, cols = gradient.shape
     if rows % cols == 0 and shards <= 8:
-        grad_rows = row_panel(gradient)
         own = lax.dynamic_slice_in_dim(grad_rows, (member * cols) % rows, cols, 0)
         other = jnp.zeros_like(own)
         for offset in range(1, shards):
@@ -89,40 +150,53 @@
     member = lax.axis_index(GROUP)
     rows, cols = gradient.shape
     grad_float = gradient.astype(jnp.float32)
-    local_sum = jnp.sum(grad_float * grad_float) + jnp.sum(gain_grad * gain_grad) / group
-    squares_total = lax.psum(local_sum, EVERY)
+    grad_rows = row_panel(gradient)
+    grad_rows_float = grad_rows.astype(jnp.float32)
+    squares_total = shard_total(
+        jnp.sum(grad_rows_float * grad_rows_float) + jnp.sum(gain_grad * gain_grad), shards
+    )
     clip_factor = jnp.minimum(1.0, D / jnp.sqrt(squares_total + 1e-06))
-    outer_part = outer_block(gradient, shards, group, place, member)
+    outer_part = outer_block(gradient, grad_rows, shards, group, place, member)
     new_statistic = 0.95 * left_statistic + (0.05 / D * clip_factor * clip_factor) * outer_part
     statistic_rows = row_panel(new_statistic)
-    basis_columns = lax.all_gather(left_basis, "shard", axis=0, tiled=True)
-    power_product = matmul(statistic_rows, basis_columns)
-    power_sum = lax.psum(jnp.sum(power_product * power_product), EVERY)
+    power_product = rows_times_shards(
+        statistic_rows, left_basis, shards, place, lambda x: x, lambda x: x
+    )
     power_rows = row_panel(power_product)
+    power_sum = shard_total(jnp.sum(power_rows * power_rows), shards)
     scale = 0.9 * jnp.sqrt(D / (power_sum + 1e-06))
     iterate = scale * power_product
     iterate_rows = scale * power_rows
-    basis_rows = row_panel(left_basis)
+    late_basis, power_rows = lax.optimization_barrier((left_basis, power_rows))
+    basis_rows = row_panel(late_basis)
     row_index = place * rows + lax.broadcasted_iota(jnp.int32, (rows, cols), 0)
     col_index = member * cols + lax.broadcasted_iota(jnp.int32, (rows, cols), 1)
     eye = (row_index == col_index).astype(jnp.float32)
     for sweep_index in range(NS_STEPS):
         if sweep_index:
-            iterate_rows = unpack(row_panel(pack(iterate)))
-        gram_block = scatter_sum(matmul(iterate_rows.T, iterate), shards, place)
-        gathered = lax.all_gather(pack(gram_block - eye), "shard", axis=0)
-        excess = unpack(gathered).reshape(D, cols)
-        iterate = iterate - 0.5 * matmul(iterate_rows, excess)
+            iterate_rows = packed_row_panel(iterate)
+            gram_block = scatter_product(iterate_rows, iterate, shards, place)
+        else:
+            gram_block = (scale * scale) * scatter_product(
+                power_rows, power_product, shards, place
+            )
+        iterate = iterate - 0.5 * rows_times_shards(
+            iterate_rows, gram_block - eye, shards, place, pack, unpack
+        )
     rotated = clip_factor * lax.psum_scatter(
         matmul(basis_rows.T, grad_float), "shard", scatter_dimension=0, tiled=True
     )
     new_first = 0.9 * first_moment + 0.1 * rotated
     new_second = 0.95 * second_moment + 0.05 * rotated * rotated
     direction = new_first / (jnp.sqrt(new_second) + 1e-08)
-    direction_columns = lax.all_gather(
-        direction.astype(jnp.float16), "shard", axis=0, tiled=True
-    ).astype(jnp.float32)
-    update = matmul(basis_rows, direction_columns)
+    update = rows_times_shards(
+        basis_rows,
+        direction,
+        shards,
+        place,
+        lambda x: x.astype(jnp.float16),
+        lambda x: x.astype(jnp.float32),
+    )
     gain_clipped = clip_factor * gain_grad
     new_gain_first = 0.9 * gain_first + 0.1 * gain_clipped
     new_gain_second = 0.95 * gain_second + 0.05 * gain_clipped * gain_clipped

time: 895 us -> 1090 us (1.22)
  blocking collectives: 493 us -> 0 us
  local copies, waits for them, and re-layouts: 23.3 us -> 423 us
  waiting for transfers between devices: 250 us -> 462 us
  starting transfers between devices: 19.4 us -> 56.9 us
  matrix products: 58.4 us -> 80.7 us
    all_gather x6 -> x0, blocking collectives: 330 us -> none  [the longest x2 155 us: row_panel(): return lax.all_gather(local_block, GROUP, axis=1, tiled=True)]
    dynamic_update_slice x0 -> x16, local copies, waits for them, and re-layouts: none -> 329 us  [the longest x8 165 us: packed_row_panel(): lax.dynamic_update_index_in_dim(stack, lax.ppermute(piece, 'tensor', pair...]
    ppermute x9 -> x44, waiting for transfers between devices: 35.7 us -> 337 us  [the longest x15 140 us: rows_times_shards(): lax.ppermute(sent, 'shard', pairs)]
    psum x2 -> x0, blocking collectives: 163 us -> none  [the longest x1 123 us: on_device(): squares_total = lax.psum(local_sum, EVERY)]
    reduce_scatter x1, waiting for transfers between devices: 91.7 us -> 0.01 us  [on_device(): lax.psum_scatter(matmul(basis_rows.T, grad_float), 'shard', scatter_dimen...]
    broadcast_in_dim x0 -> x16, local copies, waits for them, and re-layouts: none -> 43.4 us  [the longest x8 26.7 us: packed_row_panel(): lax.dynamic_update_index_in_dim(stack, lax.ppermute(piece, 'tensor', pair...]
    ppermute x9 -> x44, starting transfers between devices: 13.7 us -> 51.4 us  [the longest x15 22.1 us: rows_times_shards(): lax.ppermute(sent, 'shard', pairs)]
    dot_general x9 -> x33, matrix products: 52.1 us -> 75.2 us  [matmul(): jnp.dot(left_side, right_side, precision=lax.Precision.HIGH, preferred_el...]
  transfers between devices with their start and end apart: 18 -> 52, of which waited for: 8 -> 26; matrix products, arithmetic and copies ran while one was open for 7% -> 47% of each run, Pallas kernels for 0% -> 0%
where the time goes in v2:
time: 1090 us; the launch traced here: 1080 us
  waiting for transfers between devices  462 us (42%)
  local copies, waits for them, and re-layouts  423 us (39%)
  matrix products  80.7 us (7%)
  starting transfers between devices  56.9 us (5%)
  other arithmetic  32.4 us (3%)
  between operations  21 us (2%)
    dynamic_update_slice x8, local copies, waits for them, and re-layouts, packed_row_panel(): lax.dynamic_update_index_in_dim(stack, lax.ppermute(piece, 'tensor', pair...  165 us
    dynamic_update_slice x8, local copies, waits for them, and re-layouts, packed_row_panel(): lax.dynamic_update_index_in_dim(stack, piece, core * sections + column, 0)  164 us
    ppermute x15, waiting for transfers between devices, rows_times_shards(): lax.ppermute(sent, 'shard', pairs)  140 us
    all_gather x4, waiting for transfers between devices, row_panel(): return lax.all_gather(local_block, GROUP, axis=1, tiled=True)  124 us
    ppermute x9, waiting for transfers between devices, scatter_product(): arrived.append(lax.ppermute(pack(chunk), 'shard', pairs))  80.8 us
    ppermute x6, waiting for transfers between devices, shard_total(): total = total + lax.ppermute(tile, 'shard', pairs)[0, 0]  75.8 us
    dot_general x33, matrix products, matmul(): jnp.dot(left_side, right_side, precision=lax.Precision.HIGH, preferred_el...  75.2 us
    ppermute x6, waiting for transfers between devices, packed_row_panel(): lax.ppermute(own, 'section', pairs)  40.8 us
  transfers between devices with their start and end apart: 52, of which 26 were waited for; matrix products, arithmetic and copies ran while one was open for 47% of the time, Pallas kernels for 0%

profile of v2, /device:TPU:8, one launch (start us, length us, event | category | flops | bytes accessed | tf_op | source)
XLA Modules:
  0.0 1075.7 jit_solution(15083884259176803140)
XLA Ops:
  8.0 36.0 %all-gather.5.cloned.1.call-done = bf16[640,2560]{0,1:T(8,128)(2,1)} async-done(((bf16[640,320]{0,1:T(8,128)(2,1)}), bf16[640,2560]{0,1:T(8,128)(2,1)}) %all-gather.5.cloned.1.call-update) | async-done | bytes 3276816 | tf_op jit(solution)/shard_map/all_gather | solution.py:20
  44.0 4.2 constant_dynamic-slice_fusion
  48.2 4.0 copy.70
  61.3 5.8 collective-permute-start
  67.1 43.6 %collective-permute-done = f32[8,128]{1,0:T(8,128)S(1)} collective-permute-done((f32[8,128]{1,0:T(8,128)S(1)}, f32[8,128]{1,0:T(8,128)S(1)}, u32[]{:S(2)}, u32[]{:S(2)}) %collective-permute-start) | collective-permute-done | bytes 4128 | tf_op jit(solution)/shard_map/ppermute | solution.py:58
  115.5 3.9 copy.72
  119.3 3.8 copy.73
  123.2 3.9 copy.75
  127.1 5.5 fusion.137
  137.1 40.7 %all-gather.7.cloned.1.call-done = f32[640,2560]{0,1:T(8,128)} async-done(((f32[640,320]{0,1:T(8,128)}), f32[640,2560]{0,1:T(8,128)}) %all-gather.7.cloned.1.call-update) | async-done | bytes 6553616 | tf_op jit(solution)/shard_map/all_gather | solution.py:20
  183.7 4.6 collective-permute-done.8
  192.0 47.4 %all-gather.9.cloned.1.call-done = f32[640,2560]{0,1:T(8,128)} async-done(((f32[640,320]{0,1:T(8,128)}), f32[640,2560]{0,1:T(8,128)}) %all-gather.9.cloned.1.call-update) | async-done | bytes 6553616 | tf_op jit(solution)/shard_map/all_gather | solution.py:20
  259.0 23.1 %collective-permute-done.12 = f32[8,128]{1,0:T(8,128)S(1)} collective-permute-done((f32[8,128]{1,0:T(8,128)S(1)}, f32[8,128]{1,0:T(8,128)S(1)}, u32[]{:S(2)}, u32[]{:S(2)}) %collective-permute-start.12) | collective-permute-done | bytes 4128 | tf_op jit(solution)/shard_map/ppermute | solution.py:58
  285.7 7.9 collective-permute-done.13
  297.9 3.4 abs_reduce_fusion.10
  301.7 3.4 collective-permute-start.19
  308.4 26.7 %collective-permute-done.19 = f16[656,320]{0,1:T(8,128)(2,1)S(1)} collective-permute-done((f16[656,320]{0,1:T(8,128)(2,1)S(1)}, f16[656,320]{0,1:T(8,128)(2,1)S(1)}, u32[]{:S(2)}, u32[]{:S(2)}) %collective-permute-start.19) | collective-permute-done | bytes 419872 | tf_op jit(solution)/shard_map/ppermute | solution.py:69
  335.2 11.8 %collective-permute-done.20 = f16[656,320]{0,1:T(8,128)(2,1)S(1)} collective-permute-done((f16[656,320]{0,1:T(8,128)(2,1)S(1)}, f16[656,320]{0,1:T(8,128)(2,1)S(1)}, u32[]{:S(2)}, u32[]{:S(2)}) %collective-permute-start.20) | collective-permute-done | bytes 419872 | tf_op jit(solution)/shard_map/ppermute | solution.py:69
  355.9 10.7 collective-permute-done.22
  366.6 10.8 %collective-permute-done.24 = f16[656,320]{0,1:T(8,128)(2,1)} collective-permute-done((f16[656,320]{0,1:T(8,128)(2,1)S(1)}, f16[656,320]{0,1:T(8,128)(2,1)}, u32[]{:S(2)}, u32[]{:S(2)}) %collective-permute-start.24) | collective-permute-done | bytes 419872 | tf_op jit(solution)/shard_map/ppermute | solution.py:104
  382.6 20.5 %dynamic_update_slice.49 = f16[8,656,320]{2,0,1:T(8,128)(2,1)} dynamic-update-slice(f16[8,656,320]{2,0,1:T(8,128)(2,1)} %broadcast.747.clone, f16[1,656,320]{2,0,1:T(2,128)(2,1)S(1)} %copy.76, s32[]{:T(128)S(6)} %select_n.104, s32[]{:T(128)} %constant.119.clone.1, s32[]{:T(128)} %constant.119.clone.1) | dynamic-update-slice | bytes 839684 | tf_op jit(solution)/shard_map/jit(dynamic_update_index_in_dim)/dynamic_update_slice | solution.py:107
  403.1 3.4 copy.77
  406.5 3.3 copy.78
  414.2 20.6 %dynamic_update_slice.50 = f16[8,656,320]{2,0,1:T(8,128)(2,1)} dynamic-update-slice(f16[8,656,320]{2,0,1:T(8,128)(2,1)} %dynamic_update_slice.49, f16[1,656,320]{2,0,1:T(2,128)(2,1)} %copy.77, s32[]{:T(128)S(6)} %select_n.105, s32[]{:T(128)} %constant.119.clone.1, s32[]{:T(128)} %constant.119.clone.1) | dynamic-update-slice | bytes 839684 | tf_op jit(solution)/shard_map/jit(dynamic_update_index_in_dim)/dynamic_update_slice | solution.py:110
  434.8 20.6 %dynamic_update_slice.51 = f16[8,656,320]{2,0,1:T(8,128)(2,1)} dynamic-update-slice(f16[8,656,320]{2,0,1:T(8,128)(2,1)} %dynamic_update_slice.50, f16[1,656,320]{2,0,1:T(2,128)(2,1)} %copy.78, s32[]{:T(128)S(6)} %select_n.106, s32[]{:T(128)} %constant.119.clone.1, s32[]{:T(128)} %constant.119.clone.1) | dynamic-update-slice | bytes 839684 | tf_op jit(solution)/shard_map/jit(dynamic_update_index_in_dim)/dynamic_update_slice | solution.py:107
  458.7 3.3 copy.81
  462.1 3.4 copy.83
  465.5 20.6 %dynamic_update_slice.52 = f16[8,656,320]{2,0,1:T(8,128)(2,1)} dynamic-update-slice(f16[8,656,320]{2,0,1:T(8,128)(2,1)} %dynamic_update_slice.51, f16[1,656,320]{2,0,1:T(2,128)(2,1)} %copy.79, s32[]{:T(128)S(6)} %select_n.107, s32[]{:T(128)} %constant.119.clone.1, s32[]{:T(128)} %constant.119.clone.1) | dynamic-update-slice | bytes 839684 | tf_op jit(solution)/shard_map/jit(dynamic_update_index_in_dim)/dynamic_update_slice | solution.py:110
  486.0 20.5 %dynamic_update_slice.53 = f16[8,656,320]{2,0,1:T(8,128)(2,1)} dynamic-update-slice(f16[8,656,320]{2,0,1:T(8,128)(2,1)} %dynamic_update_slice.52, f16[1,656,320]{2,0,1:T(2,128)(2,1)S(1)} %copy.80, s32[]{:T(128)S(6)} %select_n.108, s32[]{:T(128)} %constant.119.clone.1, s32[]{:T(128)} %constant.119.clone.1) | dynamic-update-slice | bytes 839684 | tf_op jit(solution)/shard_map/jit(dynamic_update_index_in_dim)/dynamic_update_slice | solution.py:107
  506.5 20.7 %dynamic_update_slice.54 = f16[8,656,320]{2,0,1:T(8,128)(2,1)} dynamic-update-slice(f16[8,656,320]{2,0,1:T(8,128)(2,1)} %dynamic_update_slice.53, f16[1,656,320]{2,0,1:T(2,128)(2,1)} %copy.81, s32[]{:T(128)S(6)} %select_n.109, s32[]{:T(128)} %constant.119.clone.1, s32[]{:T(128)} %constant.119.clone.1) | dynamic-update-slice | bytes 839684 | tf_op jit(solution)/shard_map/jit(dynamic_update_index_in_dim)/dynamic_update_slice | solution.py:110
  527.2 20.5 %dynamic_update_slice.55 = f16[8,656,320]{2,0,1:T(8,128)(2,1)} dynamic-update-slice(f16[8,656,320]{2,0,1:T(8,128)(2,1)} %dynamic_update_slice.54, f16[1,656,320]{2,0,1:T(2,128)(2,1)S(1)} %copy.82, s32[]{:T(128)S(6)} %select_n.110, s32[]{:T(128)} %constant.119.clone.1, s32[]{:T(128)} %constant.119.clone.1) | dynamic-update-slice | bytes 839684 | tf_op jit(solution)/shard_map/jit(dynamic_update_index_in_dim)/dynamic_update_slice | solution.py:107
  547.7 20.5 %dynamic_update_slice.56 = f16[8,656,320]{2,0,1:T(8,128)(2,1)} dynamic-update-slice(f16[8,656,320]{2,0,1:T(8,128)(2,1)} %dynamic_update_slice.55, f16[1,656,320]{2,0,1:T(2,128)(2,1)S(1)} %copy-done.6, s32[]{:T(128)S(6)} %select_n.111, s32[]{:T(128)} %constant.119.clone.1, s32[]{:T(128)} %constant.119.clone.1) | dynamic-update-slice | bytes 839684 | tf_op jit(solution)/shard_map/jit(dynamic_update_index_in_dim)/dynamic_update_slice | solution.py:110
  570.9 3.6 fusion.1
  574.5 8.9 copy.84
  595.5 8.7 collective-permute-done.28
  604.3 21.0 %collective-permute-done.29 = f16[656,320]{0,1:T(8,128)(2,1)S(1)} collective-permute-done((f16[656,320]{0,1:T(8,128)(2,1)S(1)}, f16[656,320]{0,1:T(8,128)(2,1)S(1)}, u32[]{:S(2)}, u32[]{:S(2)}) %collective-permute-start.29) | collective-permute-done | bytes 419872 | tf_op jit(solution)/shard_map/ppermute | solution.py:90
  625.3 10.7 collective-permute-done.30
  644.6 27.0 %collective-permute-done.32 = f16[656,320]{0,1:T(8,128)(2,1)S(1)} collective-permute-done((f16[656,320]{0,1:T(8,128)(2,1)S(1)}, f16[656,320]{0,1:T(8,128)(2,1)S(1)}, u32[]{:S(2)}, u32[]{:S(2)}) %collective-permute-start.32) | collective-permute-done | bytes 419872 | tf_op jit(solution)/shard_map/ppermute | solution.py:69
  671.7 10.1 collective-permute-done.33
  692.0 10.8 %collective-permute-done.35 = f16[656,320]{0,1:T(8,128)(2,1)} collective-permute-done((f16[656,320]{0,1:T(8,128)(2,1)}, f16[656,320]{0,1:T(8,128)(2,1)}, u32[]{:S(2)}, u32[]{:S(2)}) %collective-permute-start.35) | collective-permute-done | bytes 419872 | tf_op jit(solution)/shard_map/ppermute | solution.py:104
  702.9 8.5 collective-permute-done.37
  711.9 7.4 fusion.258
  723.3 20.5 %dynamic_update_slice.57 = f16[8,656,320]{2,0,1:T(8,128)(2,1)} dynamic-update-slice(f16[8,656,320]{2,0,1:T(8,128)(2,1)} %broadcast.747, f16[1,656,320]{2,0,1:T(2,128)(2,1)S(1)} %copy.85, s32[]{:T(128)S(6)} %select_n.104, s32[]{:T(128)} %constant.119.clone.1, s32[]{:T(128)} %constant.119.clone.1) | dynamic-update-slice | bytes 839684 | tf_op jit(solution)/shard_map/jit(dynamic_update_index_in_dim)/dynamic_update_slice | solution.py:107
  743.9 3.3 copy.86
  750.5 3.4 copy.89
  755.5 20.6 %dynamic_update_slice.58 = f16[8,656,320]{2,0,1:T(8,128)(2,1)} dynamic-update-slice(f16[8,656,320]{2,0,1:T(8,128)(2,1)} %dynamic_update_slice.57, f16[1,656,320]{2,0,1:T(2,128)(2,1)} %copy.86, s32[]{:T(128)S(6)} %select_n.105, s32[]{:T(128)} %constant.119.clone.1, s32[]{:T(128)} %constant.119.clone.1) | dynamic-update-slice | bytes 839684 | tf_op jit(solution)/shard_map/jit(dynamic_update_index_in_dim)/dynamic_update_slice | solution.py:110
  776.1 20.6 %dynamic_update_slice.59 = f16[8,656,320]{2,0,1:T(8,128)(2,1)} dynamic-update-slice(f16[8,656,320]{2,0,1:T(8,128)(2,1)} %dynamic_update_slice.58, f16[1,656,320]{2,0,1:T(2,128)(2,1)} %copy.87, s32[]{:T(128)S(6)} %select_n.106, s32[]{:T(128)} %constant.119.clone.1, s32[]{:T(128)} %constant.119.clone.1) | dynamic-update-slice | bytes 839684 | tf_op jit(solution)/shard_map/jit(dynamic_update_index_in_dim)/dynamic_update_slice | solution.py:107
  796.7 3.4 copy.88
  803.4 3.3 copy.92
  806.7 20.6 %dynamic_update_slice.60 = f16[8,656,320]{2,0,1:T(8,128)(2,1)} dynamic-update-slice(f16[8,656,320]{2,0,1:T(8,128)(2,1)} %dynamic_update_slice.59, f16[1,656,320]{2,0,1:T(2,128)(2,1)} %copy.88, s32[]{:T(128)S(6)} %select_n.107, s32[]{:T(128)} %constant.119.clone.1, s32[]{:T(128)} %constant.119.clone.1) | dynamic-update-slice | bytes 839684 | tf_op jit(solution)/shard_map/jit(dynamic_update_index_in_dim)/dynamic_update_slice | solution.py:110
  827.3 20.6 %dynamic_update_slice.61 = f16[8,656,320]{2,0,1:T(8,128)(2,1)} dynamic-update-slice(f16[8,656,320]{2,0,1:T(8,128)(2,1)} %dynamic_update_slice.60, f16[1,656,320]{2,0,1:T(2,128)(2,1)} %copy.89, s32[]{:T(128)S(6)} %select_n.108, s32[]{:T(128)} %constant.119.clone.1, s32[]{:T(128)} %constant.119.clone.1) | dynamic-update-slice | bytes 839684 | tf_op jit(solution)/shard_map/jit(dynamic_update_index_in_dim)/dynamic_update_slice | solution.py:107
  847.9 20.6 %dynamic_update_slice.62 = f16[8,656,320]{2,0,1:T(8,128)(2,1)} dynamic-update-slice(f16[8,656,320]{2,0,1:T(8,128)(2,1)} %dynamic_update_slice.61, f16[1,656,320]{2,0,1:T(2,128)(2,1)} %copy.90, s32[]{:T(128)S(6)} %select_n.109, s32[]{:T(128)} %constant.119.clone.1, s32[]{:T(128)} %constant.119.clone.1) | dynamic-update-slice | bytes 839684 | tf_op jit(solution)/shard_map/jit(dynamic_update_index_in_dim)/dynamic_update_slice | solution.py:110
  868.5 20.5 %dynamic_update_slice.63 = f16[8,656,320]{2,0,1:T(8,128)(2,1)} dynamic-update-slice(f16[8,656,320]{2,0,1:T(8,128)(2,1)} %dynamic_update_slice.62, f16[1,656,320]{2,0,1:T(2,128)(2,1)S(1)} %copy.91, s32[]{:T(128)S(6)} %select_n.110, s32[]{:T(128)} %constant.119.clone.1, s32[]{:T(128)} %constant.119.clone.1) | dynamic-update-slice | bytes 839684 | tf_op jit(solution)/shard_map/jit(dynamic_update_index_in_dim)/dynamic_update_slice | solution.py:107
  889.0 20.6 %dynamic_update_slice.64 = f16[8,656,320]{2,0,1:T(8,128)(2,1)} dynamic-update-slice(f16[8,656,320]{2,0,1:T(8,128)(2,1)} %dynamic_update_slice.63, f16[1,656,320]{2,0,1:T(2,128)(2,1)} %copy.92, s32[]{:T(128)S(6)} %select_n.111, s32[]{:T(128)} %constant.119.clone.1, s32[]{:T(128)} %constant.119.clone.1) | dynamic-update-slice | bytes 839684 | tf_op jit(solution)/shard_map/jit(dynamic_update_index_in_dim)/dynamic_update_slice | solution.py:110
  912.2 3.6 fusion
  915.8 8.9 copy.93
  936.8 8.7 collective-permute-done.41
  945.6 21.0 %collective-permute-done.42 = f16[656,320]{0,1:T(8,128)(2,1)S(1)} collective-permute-done((f16[656,320]{0,1:T(8,128)(2,1)S(1)}, f16[656,320]{0,1:T(8,128)(2,1)S(1)}, u32[]{:S(2)}, u32[]{:S(2)}) %collective-permute-start.42) | collective-permute-done | bytes 419872 | tf_op jit(solution)/shard_map/ppermute | solution.py:90
  966.7 10.7 collective-permute-done.43
  986.6 26.4 %collective-permute-done.45 = f16[656,320]{0,1:T(8,128)(2,1)S(1)} collective-permute-done((f16[656,320]{0,1:T(8,128)(2,1)S(1)}, f16[656,320]{0,1:T(8,128)(2,1)S(1)}, u32[]{:S(2)}, u32[]{:S(2)}) %collective-permute-start.45) | collective-permute-done | bytes 419872 | tf_op jit(solution)/shard_map/ppermute | solution.py:69
  1013.1 10.1 collective-permute-done.46
  1030.1 4.6 fusion.107
  1041.2 15.7 %collective-permute-done.10 = f16[640,320]{0,1:T(8,128)(2,1)S(1)} collective-permute-done((f16[640,320]{0,1:T(8,128)(2,1)S(1)}, f16[640,320]{0,1:T(8,128)(2,1)S(1)}, u32[]{:S(2)}, u32[]{:S(2)}) %collective-permute-start.10) | collective-permute-done | bytes 409632 | tf_op jit(solution)/shard_map/ppermute | solution.py:69
  1058.3 7.1 collective-permute-done.11
  (278 shorter events, 164.6 us)
Async XLA Ops:
  7.2 49.9 %copy-start.10 = (f32[2,640]{1,0:T(2,128)S(1)}, f32[2,640]{1,0:T(2,128)}, u32[]{:S(2)}) copy-start(f32[2,640]{1,0:T(2,128)} %param.10) | copy-start | bytes 15364
  7.2 36.8 %all-gather.5.cloned.1.call-start = ((), (), s32[]{:S(2)}) async-start(), calls=%async_computation.1 | async-start | bytes 3686400 | tf_op jit(solution)/shard_map/all_gather | solution.py:20
  7.9 169.9 %all-gather.7.cloned.1.call-start = ((), (), s32[]{:S(2)}) async-start(), calls=%async_computation.2 | async-start | bytes 7372800 | tf_op jit(solution)/shard_map/all_gather | solution.py:20
  44.0 13.8 %copy-start.4 = (bf16[640,2560]{0,1:T(8,128)(2,1)S(1)}, bf16[640,2560]{0,1:T(8,128)(2,1)}, u32[]{:S(2)}) copy-start(bf16[640,2560]{0,1:T(8,128)(2,1)} %all-gather.5.cloned.1.call-done) | copy-start | bytes 9830404
  52.1 63.3 %collective-permute-start.3 = (bf16[320,2560]{1,0:T(8,128)(2,1)}, bf16[320,2560]{1,0:T(8,128)(2,1)}, u32[]{:S(2)}, u32[]{:S(2)}) collective-permute-start(bf16[320,2560]{1,0:T(8,128)(2,1)} %copy.70), channel_id=1, source_target_pairs={{0,8},{1,9},{10,18},{11,19},{20,28},{21,29},{30,6},{31,7}} | collective-permute-start | bytes 4915208 | tf_op jit(solution)/shard_map/ppermute | solution.py:128
  53.4 65.9 %collective-permute-start.4 = (bf16[320,2560]{1,0:T(8,128)(2,1)}, bf16[320,2560]{1,0:T(8,128)(2,1)}, u32[]{:S(2)}, u32[]{:S(2)}) collective-permute-start(bf16[320,2560]{1,0:T(8,128)(2,1)} %copy.70), channel_id=1, source_target_pairs={{0,16},{1,17},{10,26},{11,27},{20,4},{21,5},{30,14},{31,15}} | collective-permute-start | bytes 4915208 | tf_op jit(solution)/shard_map/ppermute | solution.py:128
  55.3 67.9 %collective-permute-start.5 = (bf16[320,2560]{1,0:T(8,128)(2,1)}, bf16[320,2560]{1,0:T(8,128)(2,1)}, u32[]{:S(2)}, u32[]{:S(2)}) collective-permute-start(bf16[320,2560]{1,0:T(8,128)(2,1)} %copy.70), channel_id=1, source_target_pairs={{0,24},{1,25},{10,2},{11,3},{20,12},{21,13},{30,22},{31,23}} | collective-permute-start | bytes 4915208 | tf_op jit(solution)/shard_map/ppermute | solution.py:128
  61.3 49.3 %collective-permute-start = (f32[8,128]{1,0:T(8,128)S(1)}, f32[8,128]{1,0:T(8,128)S(1)}, u32[]{:S(2)}, u32[]{:S(2)}) collective-permute-start(f32[8,128]{1,0:T(8,128)S(1)} %broadcast_in_dim.139), channel_id=1, source_target_pairs={{0,8},{8,0},{16,24},{24,16},{1,9},{9,1},{17,25},{25,17},{2,10},{10... | collective-permute-start | bytes 12296 | tf_op jit(solution)/shard_map/ppermute | solution.py:58
  67.1 44.8 %collective-permute-start.1 = (f32[8,128]{1,0:T(8,128)S(1)}, f32[8,128]{1,0:T(8,128)S(1)}, u32[]{:S(2)}, u32[]{:S(2)}) collective-permute-start(f32[8,128]{1,0:T(8,128)S(1)} %broadcast_in_dim.139), channel_id=1, source_target_pairs={{0,16},{8,24},{16,0},{24,8},{1,17},{9,25},{17,1},{25,9},{2,18},{10... | collective-permute-start | bytes 12296 | tf_op jit(solution)/shard_map/ppermute | solution.py:58
  110.6 3.6 collective-permute-start.2
  132.6 106.8 %all-gather.9.cloned.1.call-start = ((), (), s32[]{:S(2)}) async-start(), calls=%async_computation.3 | async-start | bytes 7372800 | tf_op jit(solution)/shard_map/all_gather | solution.py:20
  132.6 48.3 %collective-permute-start.7 = (f32[640,320]{0,1:T(8,128)}, f32[640,320]{0,1:T(8,128)S(1)}, u32[]{:S(2)}, u32[]{:S(2)}) collective-permute-start(f32[640,320]{0,1:T(8,128)} %param.12), channel_id=1, source_target_pairs={{0,16},{8,24},{16,0},{24,8},{1,17},{9,25},{17,1},{25,9},{2,18},{10... | collective-permute-start | bytes 2457608 | tf_op jit(solution)/shard_map/ppermute | solution.py:69
  133.4 54.8 %collective-permute-start.8 = (f32[640,320]{0,1:T(8,128)}, f32[640,320]{0,1:T(8,128)S(1)}, u32[]{:S(2)}, u32[]{:S(2)}) collective-permute-start(f32[640,320]{0,1:T(8,128)} %param.12), channel_id=1, source_target_pairs={{0,24},{8,16},{16,8},{24,0},{1,25},{9,17},{17,9},{25,1},{2,26},{10... | collective-permute-start | bytes 2457608 | tf_op jit(solution)/shard_map/ppermute | solution.py:69
  136.1 53.4 %collective-permute-start.6 = (f32[640,320]{0,1:T(8,128)}, f32[640,320]{0,1:T(8,128)S(1)}, u32[]{:S(2)}, u32[]{:S(2)}) collective-permute-start(f32[640,320]{0,1:T(8,128)} %param.12), channel_id=1, source_target_pairs={{0,8},{8,0},{16,24},{24,16},{1,9},{9,1},{17,25},{25,17},{2,10},{10... | collective-permute-start | bytes 2457608 | tf_op jit(solution)/shard_map/ppermute | solution.py:69
  177.8 10.4 copy-start.5
  191.8 50.8 %copy-start.3 = (f32[640,320]{0,1:T(8,128)S(1)}, f32[640,320]{0,1:T(8,128)}, u32[]{:S(2)}) copy-start(f32[640,320]{0,1:T(8,128)} %fusion.95) | copy-start | bytes 2457604
  191.8 520.0 %all-gather.11.cloned.1.call-start = ((), (), s32[]{:S(2)}) async-start(), calls=%async_computation.4 | async-start | bytes 7372800 | tf_op jit(solution)/shard_map/all_gather | solution.py:20
  247.4 48.6 %collective-permute-start.15 = (f16[656,320]{0,1:T(8,128)(2,1)S(1)}, f16[656,320]{0,1:T(8,128)(2,1)S(1)}, u32[]{:S(2)}, u32[]{:S(2)}) collective-permute-start(f16[656,320]{0,1:T(8,128)(2,1)S(1)} %pad_maximum_fusion), channel_id=1, source_target_pairs={{0,8},{8,0},{16,24},{24,16},{1,9},{9,1},{17,25},{25,17},{2,10},{10... | collective-permute-start | bytes 1259528 | tf_op jit(solution)/shard_map/ppermute | solution.py:90
  248.4 47.6 %collective-permute-start.16 = (f16[656,320]{0,1:T(8,128)(2,1)S(1)}, f16[656,320]{0,1:T(8,128)(2,1)S(1)}, u32[]{:S(2)}, u32[]{:S(2)}) collective-permute-start(f16[656,320]{0,1:T(8,128)(2,1)S(1)} %pad_maximum_fusion.1), channel_id=1, source_target_pairs={{0,16},{8,24},{16,0},{24,8},{1,17},{9,25},{17,1},{25,9},{2,18},{10... | collective-permute-start | bytes 1259528 | tf_op jit(solution)/shard_map/ppermute | solution.py:90
  252.1 44.4 %collective-permute-start.17 = (f16[656,320]{0,1:T(8,128)(2,1)}, f16[656,320]{0,1:T(8,128)(2,1)}, u32[]{:S(2)}, u32[]{:S(2)}) collective-permute-start(f16[656,320]{0,1:T(8,128)(2,1)} %pad_maximum_fusion.2), channel_id=1, source_target_pairs={{0,24},{8,16},{16,8},{24,0},{1,25},{9,17},{17,9},{25,1},{2,26},{10... | collective-permute-start | bytes 1259528 | tf_op jit(solution)/shard_map/ppermute | solution.py:90
  255.5 26.5 %collective-permute-start.12 = (f32[8,128]{1,0:T(8,128)S(1)}, f32[8,128]{1,0:T(8,128)S(1)}, u32[]{:S(2)}, u32[]{:S(2)}) collective-permute-start(f32[8,128]{1,0:T(8,128)S(1)} %broadcast_in_dim.140), channel_id=1, source_target_pairs={{0,8},{8,0},{16,24},{24,16},{1,9},{9,1},{17,25},{25,17},{2,10},{10... | collective-permute-start | bytes 12296 | tf_op jit(solution)/shard_map/ppermute | solution.py:58
  257.0 36.5 %collective-permute-start.13 = (f32[8,128]{1,0:T(8,128)S(1)}, f32[8,128]{1,0:T(8,128)S(1)}, u32[]{:S(2)}, u32[]{:S(2)}) collective-permute-start(f32[8,128]{1,0:T(8,128)S(1)} %broadcast_in_dim.140), channel_id=1, source_target_pairs={{0,16},{8,24},{16,0},{24,8},{1,17},{9,25},{17,1},{25,9},{2,18},{10... | collective-permute-start | bytes 12296 | tf_op jit(solution)/shard_map/ppermute | solution.py:58
  282.1 12.6 %collective-permute-start.14 = (f32[8,128]{1,0:T(8,128)S(1)}, f32[8,128]{1,0:T(8,128)S(1)}, u32[]{:S(2)}, u32[]{:S(2)}) collective-permute-start(f32[8,128]{1,0:T(8,128)S(1)} %broadcast_in_dim.140), channel_id=1, source_target_pairs={{0,24},{8,16},{16,8},{24,0},{1,25},{9,17},{17,9},{25,1},{2,26},{10... | collective-permute-start | bytes 12296 | tf_op jit(solution)/shard_map/ppermute | solution.py:58
  283.6 744.0 %reduce-scatter.2.cloned.1.call-start = ((), (), s32[]{:S(2)}) async-start(), calls=%async_computation.5 | async-start | bytes 4096000 | tf_op jit(solution)/shard_map/reduce_scatter | solution.py:186
  295.9 10.7 slice-start
  297.9 8.7 slice-start.1
  301.7 33.4 %collective-permute-start.19 = (f16[656,320]{0,1:T(8,128)(2,1)S(1)}, f16[656,320]{0,1:T(8,128)(2,1)S(1)}, u32[]{:S(2)}, u32[]{:S(2)}) collective-permute-start(f16[656,320]{0,1:T(8,128)(2,1)S(1)} %pad_maximum_fusion.3), channel_id=1, source_target_pairs={{0,16},{8,24},{16,0},{24,8},{1,17},{9,25},{17,1},{25,9},{2,18},{10... | collective-permute-start | bytes 1259528 | tf_op jit(solution)/shard_map/ppermute | solution.py:69
  305.1 41.9 %collective-permute-start.20 = (f16[656,320]{0,1:T(8,128)(2,1)S(1)}, f16[656,320]{0,1:T(8,128)(2,1)S(1)}, u32[]{:S(2)}, u32[]{:S(2)}) collective-permute-start(f16[656,320]{0,1:T(8,128)(2,1)S(1)} %pad_maximum_fusion.3), channel_id=1, source_target_pairs={{0,24},{8,16},{16,8},{24,0},{1,25},{9,17},{17,9},{25,1},{2,26},{10... | collective-permute-start | bytes 1259528 | tf_op jit(solution)/shard_map/ppermute | solution.py:69
  305.6 41.4 %collective-permute-start.18 = (f16[656,320]{0,1:T(8,128)(2,1)S(1)}, f16[656,320]{0,1:T(8,128)(2,1)S(1)}, u32[]{:S(2)}, u32[]{:S(2)}) collective-permute-start(f16[656,320]{0,1:T(8,128)(2,1)S(1)} %pad_maximum_fusion.3), channel_id=1, source_target_pairs={{0,8},{8,0},{16,24},{24,16},{1,9},{9,1},{17,25},{25,17},{2,10},{10... | collective-permute-start | bytes 1259528 | tf_op jit(solution)/shard_map/ppermute | solution.py:69
  352.4 14.3 %collective-permute-start.22 = (f16[656,320]{0,1:T(8,128)(2,1)S(1)}, f16[656,320]{0,1:T(8,128)(2,1)}, u32[]{:S(2)}, u32[]{:S(2)}) collective-permute-start(f16[656,320]{0,1:T(8,128)(2,1)S(1)} %pad_maximum_fusion.5), channel_id=1, source_target_pairs={{0,1},{1,0},{2,3},{3,2},{4,5},{5,4},{6,7},{7,6},{8,9},{9,8},{10,11... | collective-permute-start | bytes 1259528 | tf_op jit(solution)/shard_map/ppermute | solution.py:104
  353.9 23.5 %collective-permute-start.24 = (f16[656,320]{0,1:T(8,128)(2,1)S(1)}, f16[656,320]{0,1:T(8,128)(2,1)}, u32[]{:S(2)}, u32[]{:S(2)}) collective-permute-start(f16[656,320]{0,1:T(8,128)(2,1)S(1)} %pad_maximum_fusion.5), channel_id=1, source_target_pairs={{0,2},{1,3},{2,0},{3,1},{4,6},{5,7},{6,4},{7,5},{8,10},{9,11},{10,... | collective-permute-start | bytes 1259528 | tf_op jit(solution)/shard_map/ppermute | solution.py:104
  354.5 23.0 %collective-permute-start.26 = (f16[656,320]{0,1:T(8,128)(2,1)S(1)}, f16[656,320]{0,1:T(8,128)(2,1)S(1)}, u32[]{:S(2)}, u32[]{:S(2)}) collective-permute-start(f16[656,320]{0,1:T(8,128)(2,1)S(1)} %pad_maximum_fusion.5), channel_id=1, source_target_pairs={{0,3},{1,2},{2,1},{3,0},{4,7},{5,6},{6,5},{7,4},{8,11},{9,10},{10,... | collective-permute-start | bytes 1259528 | tf_op jit(solution)/shard_map/ppermute | solution.py:104
  355.9 47.2 %collective-permute-start.21 = (f16[656,320]{0,1:T(8,128)(2,1)S(1)}, f16[656,320]{0,1:T(8,128)(2,1)}, u32[]{:S(2)}, u32[]{:S(2)}) collective-permute-start(f16[656,320]{0,1:T(8,128)(2,1)S(1)} %pad_maximum_fusion.5), channel_id=1, source_target_pairs={{0,4},{4,0},{1,5},{5,1},{2,6},{6,2},{3,7},{7,3},{8,12},{12,8},{9,1... | collective-permute-start | bytes 1259528 | tf_op jit(solution)/shard_map/ppermute | solution.py:111
  366.6 88.8 %collective-permute-start.23 = (f16[656,320]{0,1:T(8,128)(2,1)}, f16[656,320]{0,1:T(8,128)(2,1)}, u32[]{:S(2)}, u32[]{:S(2)}) collective-permute-start(f16[656,320]{0,1:T(8,128)(2,1)} %collective-permute-done.22), channel_id=1, source_target_pairs={{0,4},{4,0},{1,5},{5,1},{2,6},{6,2},{3,7},{7,3},{8,12},{12,8},{9,1... | collective-permute-start | bytes 1259528 | tf_op jit(solution)/shard_map/ppermute | solution.py:111
  377.4 81.3 %collective-permute-start.25 = (f16[656,320]{0,1:T(8,128)(2,1)}, f16[656,320]{0,1:T(8,128)(2,1)}, u32[]{:S(2)}, u32[]{:S(2)}) collective-permute-start(f16[656,320]{0,1:T(8,128)(2,1)} %collective-permute-done.24), channel_id=1, source_target_pairs={{0,4},{4,0},{1,5},{5,1},{2,6},{6,2},{3,7},{7,3},{8,12},{12,8},{9,1... | collective-permute-start | bytes 1259528 | tf_op jit(solution)/shard_map/ppermute | solution.py:111
  377.4 84.6 %collective-permute-start.27 = (f16[656,320]{0,1:T(8,128)(2,1)S(1)}, f16[656,320]{0,1:T(8,128)(2,1)}, u32[]{:S(2)}, u32[]{:S(2)}) collective-permute-start(f16[656,320]{0,1:T(8,128)(2,1)S(1)} %collective-permute-done.26), channel_id=1, source_target_pairs={{0,4},{4,0},{1,5},{5,1},{2,6},{6,2},{3,7},{7,3},{8,12},{12,8},{9,1... | collective-permute-start | bytes 1259528 | tf_op jit(solution)/shard_map/ppermute | solution.py:111
  506.5 41.2 %copy-start.6 = (f16[1,656,320]{2,0,1:T(2,128)(2,1)S(1)}, f16[1,656,320]{2,0,1:T(2,128)(2,1)}, u32[]{:S(2)}) copy-start(f16[1,656,320]{2,0,1:T(2,128)(2,1)} %copy.83) | copy-start | bytes 1259524
  586.6 17.5 %collective-permute-start.28 = (f16[656,320]{0,1:T(8,128)(2,1)S(1)}, f16[656,320]{0,1:T(8,128)(2,1)S(1)}, u32[]{:S(2)}, u32[]{:S(2)}) collective-permute-start(f16[656,320]{0,1:T(8,128)(2,1)S(1)} %pad_maximum_fusion.6), channel_id=1, source_target_pairs={{0,8},{8,0},{16,24},{24,16},{1,9},{9,1},{17,25},{25,17},{2,10},{10... | collective-permute-start | bytes 1259528 | tf_op jit(solution)/shard_map/ppermute | solution.py:90
  590.2 35.1 %collective-permute-start.29 = (f16[656,320]{0,1:T(8,128)(2,1)S(1)}, f16[656,320]{0,1:T(8,128)(2,1)S(1)}, u32[]{:S(2)}, u32[]{:S(2)}) collective-permute-start(f16[656,320]{0,1:T(8,128)(2,1)S(1)} %pad_maximum_fusion.7), channel_id=1, source_target_pairs={{0,16},{8,24},{16,0},{24,8},{1,17},{9,25},{17,1},{25,9},{2,18},{10... | collective-permute-start | bytes 1259528 | tf_op jit(solution)/shard_map/ppermute | solution.py:90
  594.4 41.6 %collective-permute-start.30 = (f16[656,320]{0,1:T(8,128)(2,1)S(1)}, f16[656,320]{0,1:T(8,128)(2,1)S(1)}, u32[]{:S(2)}, u32[]{:S(2)}) collective-permute-start(f16[656,320]{0,1:T(8,128)(2,1)S(1)} %pad_maximum_fusion.8), channel_id=1, source_target_pairs={{0,24},{8,16},{16,8},{24,0},{1,25},{9,17},{17,9},{25,1},{2,26},{10... | collective-permute-start | bytes 1259528 | tf_op jit(solution)/shard_map/ppermute | solution.py:90
  638.8 32.8 %collective-permute-start.32 = (f16[656,320]{0,1:T(8,128)(2,1)S(1)}, f16[656,320]{0,1:T(8,128)(2,1)S(1)}, u32[]{:S(2)}, u32[]{:S(2)}) collective-permute-start(f16[656,320]{0,1:T(8,128)(2,1)S(1)} %pad_maximum_fusion.9), channel_id=1, source_target_pairs={{0,16},{8,24},{16,0},{24,8},{1,17},{9,25},{17,1},{25,9},{2,18},{10... | collective-permute-start | bytes 1259528 | tf_op jit(solution)/shard_map/ppermute | solution.py:69
  638.9 42.9 %collective-permute-start.33 = (f16[656,320]{0,1:T(8,128)(2,1)S(1)}, f16[656,320]{0,1:T(8,128)(2,1)S(1)}, u32[]{:S(2)}, u32[]{:S(2)}) collective-permute-start(f16[656,320]{0,1:T(8,128)(2,1)S(1)} %pad_maximum_fusion.9), channel_id=1, source_target_pairs={{0,24},{8,16},{16,8},{24,0},{1,25},{9,17},{17,9},{25,1},{2,26},{10... | collective-permute-start | bytes 1259528 | tf_op jit(solution)/shard_map/ppermute | solution.py:69
  640.0 41.9 %collective-permute-start.31 = (f16[656,320]{0,1:T(8,128)(2,1)S(1)}, f16[656,320]{0,1:T(8,128)(2,1)S(1)}, u32[]{:S(2)}, u32[]{:S(2)}) collective-permute-start(f16[656,320]{0,1:T(8,128)(2,1)S(1)} %pad_maximum_fusion.9), channel_id=1, source_target_pairs={{0,8},{8,0},{16,24},{24,16},{1,9},{9,1},{17,25},{25,17},{2,10},{10... | collective-permute-start | bytes 1259528 | tf_op jit(solution)/shard_map/ppermute | solution.py:69
  685.5 26.3 %copy-start.7 = (bf16[640,320]{0,1:T(8,128)(2,1)S(1)}, bf16[640,320]{0,1:T(8,128)(2,1)}, u32[]{:S(2)}) copy-start(bf16[640,320]{0,1:T(8,128)(2,1)} %param.9) | copy-start | bytes 1228804
  688.4 14.5 %collective-permute-start.35 = (f16[656,320]{0,1:T(8,128)(2,1)}, f16[656,320]{0,1:T(8,128)(2,1)}, u32[]{:S(2)}, u32[]{:S(2)}) collective-permute-start(f16[656,320]{0,1:T(8,128)(2,1)} %pad_maximum_fusion.11), channel_id=1, source_target_pairs={{0,1},{1,0},{2,3},{3,2},{4,5},{5,4},{6,7},{7,6},{8,9},{9,8},{10,11... | collective-permute-start | bytes 1259528 | tf_op jit(solution)/shard_map/ppermute | solution.py:104
  688.9 22.4 %collective-permute-start.37 = (f16[656,320]{0,1:T(8,128)(2,1)}, f16[656,320]{0,1:T(8,128)(2,1)}, u32[]{:S(2)}, u32[]{:S(2)}) collective-permute-start(f16[656,320]{0,1:T(8,128)(2,1)} %pad_maximum_fusion.11), channel_id=1, source_target_pairs={{0,2},{1,3},{2,0},{3,1},{4,6},{5,7},{6,4},{7,5},{8,10},{9,11},{10,... | collective-permute-start | bytes 1259528 | tf_op jit(solution)/shard_map/ppermute | solution.py:104
  690.6 20.8 %collective-permute-start.39 = (f16[656,320]{0,1:T(8,128)(2,1)}, f16[656,320]{0,1:T(8,128)(2,1)S(1)}, u32[]{:S(2)}, u32[]{:S(2)}) collective-permute-start(f16[656,320]{0,1:T(8,128)(2,1)} %pad_maximum_fusion.11), channel_id=1, source_target_pairs={{0,3},{1,2},{2,1},{3,0},{4,7},{5,6},{6,5},{7,4},{8,11},{9,10},{10,... | collective-permute-start | bytes 1259528 | tf_op jit(solution)/shard_map/ppermute | solution.py:104
  691.9 52.0 %collective-permute-start.34 = (f16[656,320]{0,1:T(8,128)(2,1)}, f16[656,320]{0,1:T(8,128)(2,1)}, u32[]{:S(2)}, u32[]{:S(2)}) collective-permute-start(f16[656,320]{0,1:T(8,128)(2,1)} %pad_maximum_fusion.11), channel_id=1, source_target_pairs={{0,4},{4,0},{1,5},{5,1},{2,6},{6,2},{3,7},{7,3},{8,12},{12,8},{9,1... | collective-permute-start | bytes 1259528 | tf_op jit(solution)/shard_map/ppermute | solution.py:111
  702.9 93.8 %collective-permute-start.36 = (f16[656,320]{0,1:T(8,128)(2,1)}, f16[656,320]{0,1:T(8,128)(2,1)}, u32[]{:S(2)}, u32[]{:S(2)}) collective-permute-start(f16[656,320]{0,1:T(8,128)(2,1)} %collective-permute-done.35), channel_id=1, source_target_pairs={{0,4},{4,0},{1,5},{5,1},{2,6},{6,2},{3,7},{7,3},{8,12},{12,8},{9,1... | collective-permute-start | bytes 1259528 | tf_op jit(solution)/shard_map/ppermute | solution.py:111
  711.3 88.7 %collective-permute-start.38 = (f16[656,320]{0,1:T(8,128)(2,1)}, f16[656,320]{0,1:T(8,128)(2,1)}, u32[]{:S(2)}, u32[]{:S(2)}) collective-permute-start(f16[656,320]{0,1:T(8,128)(2,1)} %collective-permute-done.37), channel_id=1, source_target_pairs={{0,4},{4,0},{1,5},{5,1},{2,6},{6,2},{3,7},{7,3},{8,12},{12,8},{9,1... | collective-permute-start | bytes 1259528 | tf_op jit(solution)/shard_map/ppermute | solution.py:111
  711.4 92.0 %collective-permute-start.40 = (f16[656,320]{0,1:T(8,128)(2,1)S(1)}, f16[656,320]{0,1:T(8,128)(2,1)}, u32[]{:S(2)}, u32[]{:S(2)}) collective-permute-start(f16[656,320]{0,1:T(8,128)(2,1)S(1)} %collective-permute-done.39), channel_id=1, source_target_pairs={{0,4},{4,0},{1,5},{5,1},{2,6},{6,2},{3,7},{7,3},{8,12},{12,8},{9,1... | collective-permute-start | bytes 1259528 | tf_op jit(solution)/shard_map/ppermute | solution.py:111
  928.0 17.5 %collective-permute-start.41 = (f16[656,320]{0,1:T(8,128)(2,1)S(1)}, f16[656,320]{0,1:T(8,128)(2,1)S(1)}, u32[]{:S(2)}, u32[]{:S(2)}) collective-permute-start(f16[656,320]{0,1:T(8,128)(2,1)S(1)} %pad_maximum_fusion.12), channel_id=1, source_target_pairs={{0,8},{8,0},{16,24},{24,16},{1,9},{9,1},{17,25},{25,17},{2,10},{10... | collective-permute-start | bytes 1259528 | tf_op jit(solution)/shard_map/ppermute | solution.py:90
  931.6 35.1 %collective-permute-start.42 = (f16[656,320]{0,1:T(8,128)(2,1)S(1)}, f16[656,320]{0,1:T(8,128)(2,1)S(1)}, u32[]{:S(2)}, u32[]{:S(2)}) collective-permute-start(f16[656,320]{0,1:T(8,128)(2,1)S(1)} %pad_maximum_fusion.13), channel_id=1, source_target_pairs={{0,16},{8,24},{16,0},{24,8},{1,17},{9,25},{17,1},{25,9},{2,18},{10... | collective-permute-start | bytes 1259528 | tf_op jit(solution)/shard_map/ppermute | solution.py:90
  935.8 41.6 %collective-permute-start.43 = (f16[656,320]{0,1:T(8,128)(2,1)S(1)}, f16[656,320]{0,1:T(8,128)(2,1)S(1)}, u32[]{:S(2)}, u32[]{:S(2)}) collective-permute-start(f16[656,320]{0,1:T(8,128)(2,1)S(1)} %pad_maximum_fusion.14), channel_id=1, source_target_pairs={{0,24},{8,16},{16,8},{24,0},{1,25},{9,17},{17,9},{25,1},{2,26},{10... | collective-permute-start | bytes 1259528 | tf_op jit(solution)/shard_map/ppermute | solution.py:90
  980.2 32.8 %collective-permute-start.45 = (f16[656,320]{0,1:T(8,128)(2,1)S(1)}, f16[656,320]{0,1:T(8,128)(2,1)S(1)}, u32[]{:S(2)}, u32[]{:S(2)}) collective-permute-start(f16[656,320]{0,1:T(8,128)(2,1)S(1)} %pad_maximum_fusion.15), channel_id=1, source_target_pairs={{0,16},{8,24},{16,0},{24,8},{1,17},{9,25},{17,1},{25,9},{2,18},{10... | collective-permute-start | bytes 1259528 | tf_op jit(solution)/shard_map/ppermute | solution.py:69
  980.3 42.9 %collective-permute-start.46 = (f16[656,320]{0,1:T(8,128)(2,1)S(1)}, f16[656,320]{0,1:T(8,128)(2,1)S(1)}, u32[]{:S(2)}, u32[]{:S(2)}) collective-permute-start(f16[656,320]{0,1:T(8,128)(2,1)S(1)} %pad_maximum_fusion.15), channel_id=1, source_target_pairs={{0,24},{8,16},{16,8},{24,0},{1,25},{9,17},{17,9},{25,1},{2,26},{10... | collective-permute-start | bytes 1259528 | tf_op jit(solution)/shard_map/ppermute | solution.py:69
  981.4 41.9 %collective-permute-start.44 = (f16[656,320]{0,1:T(8,128)(2,1)S(1)}, f16[656,320]{0,1:T(8,128)(2,1)S(1)}, u32[]{:S(2)}, u32[]{:S(2)}) collective-permute-start(f16[656,320]{0,1:T(8,128)(2,1)S(1)} %pad_maximum_fusion.15), channel_id=1, source_target_pairs={{0,8},{8,0},{16,24},{24,16},{1,9},{9,1},{17,25},{25,17},{2,10},{10... | collective-permute-start | bytes 1259528 | tf_op jit(solution)/shard_map/ppermute | solution.py:69
  1027.6 29.3 %slice-start.2 = ((s8[6553600]{0:T(1024)(128)(4,1)}), s8[4194304]{0:T(1024)(128)(4,1)S(1)}, s32[]{:S(2)}) async-start(s8[6553600]{0:T(1024)(128)(4,1)} %bitcast.81), calls=%async_computation.8 | async-start | bytes 8388608
  1029.9 11.3 %copy-start.8 = (f32[640,320]{0,1:T(8,128)}, f32[640,320]{0,1:T(8,128)S(1)}, u32[]{:S(2)}) copy-start(f32[640,320]{0,1:T(8,128)S(1)} %get-tuple-element.16) | copy-start | bytes 2457604
  1030.0 11.3 %copy-start.9 = (f32[640,320]{0,1:T(8,128)}, f32[640,320]{0,1:T(8,128)S(1)}, u32[]{:S(2)}) copy-start(f32[640,320]{0,1:T(8,128)S(1)} %get-tuple-element.17) | copy-start | bytes 2457604
  1030.0 27.0 %slice-start.3 = ((s8[6553600]{0:T(1024)(128)(4,1)}), s8[2359296]{0:T(1024)(128)(4,1)S(1)}, s32[]{:S(2)}) async-start(s8[6553600]{0:T(1024)(128)(4,1)} %bitcast.81), calls=%async_computation.9 | async-start | bytes 4718592
  1030.0 27.0 %collective-permute-start.10 = (f16[640,320]{0,1:T(8,128)(2,1)S(1)}, f16[640,320]{0,1:T(8,128)(2,1)S(1)}, u32[]{:S(2)}, u32[]{:S(2)}) collective-permute-start(f16[640,320]{0,1:T(8,128)(2,1)S(1)} %get-tuple-element.15), channel_id=1, source_target_pairs={{0,16},{8,24},{16,0},{24,8},{1,17},{9,25},{17,1},{25,9},{2,18},{10... | collective-permute-start | bytes 1228808 | tf_op jit(solution)/shard_map/ppermute | solution.py:69
  1034.6 30.8 %collective-permute-start.11 = (f16[640,320]{0,1:T(8,128)(2,1)S(1)}, f16[640,320]{0,1:T(8,128)(2,1)S(1)}, u32[]{:S(2)}, u32[]{:S(2)}) collective-permute-start(f16[640,320]{0,1:T(8,128)(2,1)S(1)} %get-tuple-element.15), channel_id=1, source_target_pairs={{0,24},{8,16},{16,8},{24,0},{1,25},{9,17},{17,9},{25,1},{2,26},{10... | collective-permute-start | bytes 1228808 | tf_op jit(solution)/shard_map/ppermute | solution.py:69
  1035.6 31.1 %collective-permute-start.9 = (f16[640,320]{0,1:T(8,128)(2,1)S(1)}, f16[640,320]{0,1:T(8,128)(2,1)S(1)}, u32[]{:S(2)}, u32[]{:S(2)}) collective-permute-start(f16[640,320]{0,1:T(8,128)(2,1)S(1)} %get-tuple-element.15), channel_id=1, source_target_pairs={{0,8},{8,0},{16,24},{24,16},{1,9},{9,1},{17,25},{25,17},{2,10},{10... | collective-permute-start | bytes 1228808 | tf_op jit(solution)/shard_map/ppermute | solution.py:69
  (6 other events, 39.0 us)
Sparse Core Ops, SparseCore 0:
  9.9 34.0 all-gather.4
  132.7 45.0 all-gather.6
  191.9 47.4 all-gather.8
  283.7 44.7 all-gather.10
  719.4 60.7 reduce-scatter.1

commit v3 on v2

--- a/solution.py
+++ b/solution.py
@@ -18,6 +18,10 @@
 
 def row_panel(local_block):
     return lax.all_gather(local_block, GROUP, axis=1, tiled=True)
+
+
+def same(block):
+    return block
 
 
 def pack(block):
@@ -77,7 +81,7 @@
     return total
 
 
-def scatter_product(full_rows, block, shards, place):
+def scatter_product(full_rows, block, shards, place, encode, decode):
     if shards > 8:
         return lax.psum_scatter(
             matmul(full_rows.T, block), "shard", scatter_dimension=0, tiled=True
@@ -87,30 +91,11 @@
     for offset, pairs in enumerate(partners(shards), 1):
         target = place_of_target(place, offset, shards)
         chunk = matmul(lax.dynamic_slice_in_dim(full_rows, target * rows, rows, 1).T, block)
-        arrived.append(lax.ppermute(pack(chunk), "shard", pairs))
+        arrived.append(lax.ppermute(encode(chunk), "shard", pairs))
     total = matmul(lax.dynamic_slice_in_dim(full_rows, place * rows, rows, 1).T, block)
     for payload in arrived:
-        total = total + unpack(payload)
+        total = total + decode(payload)
     return total
-
-
-def packed_row_panel(block):
-    sections = lax.axis_size("section")
-    cores = lax.axis_size("tensor")
-    section = lax.axis_index("section")
-    core = lax.axis_index("tensor")
-    own = pack(block)
-    stack = jnp.zeros((cores * sections,) + own.shape, own.dtype)
-    pieces = [own] + [lax.ppermute(own, "section", pairs) for pairs in partners(sections)]
-    for offset, piece in enumerate(pieces):
-        column = place_of_source(section, offset, sections)
-        stack = lax.dynamic_update_index_in_dim(stack, piece, core * sections + column, 0)
-        for shift, pairs in enumerate(partners(cores), 1):
-            other = place_of_source(core, shift, cores)
-            stack = lax.dynamic_update_index_in_dim(
-                stack, lax.ppermute(piece, "tensor", pairs), other * sections + column, 0
-            )
-    return unpack(stack).transpose(1, 0, 2).reshape(block.shape[0], -1)
 
 
 def outer_block(gradient, grad_rows, shards, group, place, member):
@@ -151,6 +136,8 @@
     rows, cols = gradient.shape
     grad_float = gradient.astype(jnp.float32)
     grad_rows = row_panel(gradient)
+    late_basis, grad_rows = lax.optimization_barrier((left_basis, grad_rows))
+    basis_rows = row_panel(late_basis)
     grad_rows_float = grad_rows.astype(jnp.float32)
     squares_total = shard_total(
         jnp.sum(grad_rows_float * grad_rows_float) + jnp.sum(gain_grad * gain_grad), shards
@@ -158,33 +145,14 @@
     clip_factor = jnp.minimum(1.0, D / jnp.sqrt(squares_total + 1e-06))
     outer_part = outer_block(gradient, grad_rows, shards, group, place, member)
     new_statistic = 0.95 * left_statistic + (0.05 / D * clip_factor * clip_factor) * outer_part
-    statistic_rows = row_panel(new_statistic)
+    ready_statistic, basis_rows = lax.optimization_barrier((new_statistic, basis_rows))
+    statistic_rows = row_panel(ready_statistic)
     power_product = rows_times_shards(
-        statistic_rows, left_basis, shards, place, lambda x: x, lambda x: x
+        statistic_rows, left_basis, shards, place, same, same
     )
     power_rows = row_panel(power_product)
-    power_sum = shard_total(jnp.sum(power_rows * power_rows), shards)
-    scale = 0.9 * jnp.sqrt(D / (power_sum + 1e-06))
-    iterate = scale * power_product
-    iterate_rows = scale * power_rows
-    late_basis, power_rows = lax.optimization_barrier((left_basis, power_rows))
-    basis_rows = row_panel(late_basis)
-    row_index = place * rows + lax.broadcasted_iota(jnp.int32, (rows, cols), 0)
-    col_index = member * cols + lax.broadcasted_iota(jnp.int32, (rows, cols), 1)
-    eye = (row_index == col_index).astype(jnp.float32)
-    for sweep_index in range(NS_STEPS):
-        if sweep_index:
-            iterate_rows = packed_row_panel(iterate)
-            gram_block = scatter_product(iterate_rows, iterate, shards, place)
-        else:
-            gram_block = (scale * scale) * scatter_product(
-                power_rows, power_product, shards, place
-            )
-        iterate = iterate - 0.5 * rows_times_shards(
-            iterate_rows, gram_block - eye, shards, place, pack, unpack
-        )
-    rotated = clip_factor * lax.psum_scatter(
-        matmul(basis_rows.T, grad_float), "shard", scatter_dimension=0, tiled=True
+    rotated = clip_factor * scatter_product(
+        basis_rows, grad_float, shards, place, same, same
     )
     new_first = 0.9 * first_moment + 0.1 * rotated
     new_second = 0.95 * second_moment + 0.05 * rotated * rotated
@@ -197,6 +165,27 @@
         lambda x: x.astype(jnp.float16),
         lambda x: x.astype(jnp.float32),
     )
+    update, power_rows = lax.optimization_barrier((update, power_rows))
+    power_sum = shard_total(jnp.sum(power_rows * power_rows), shards)
+    scale = 0.9 * jnp.sqrt(D / (power_sum + 1e-06))
+    iterate = scale * power_product
+    iterate_rows = scale * power_rows
+    row_index = place * rows + lax.broadcasted_iota(jnp.int32, (rows, cols), 0)
+    col_index = member * cols + lax.broadcasted_iota(jnp.int32, (rows, cols), 1)
+    eye = (row_index == col_index).astype(jnp.float32)
+    for sweep_index in range(NS_STEPS):
+        if sweep_index:
+            iterate_rows = row_panel(iterate)
+            gram_block = scatter_product(
+                iterate_rows, iterate, shards, place, pack, unpack
+            )
+        else:
+            gram_block = (scale * scale) * scatter_product(
+                power_rows, power_product, shards, place, pack, unpack
+            )
+        iterate = iterate - 0.5 * rows_times_shards(
+            iterate_rows, gram_block - eye, shards, place, pack, unpack
+        )
     gain_clipped = clip_factor * gain_grad
     new_gain_first = 0.9 * gain_first + 0.1 * gain_clipped
     new_gain_second = 0.95 * gain_second + 0.05 * gain_clipped * gain_clipped

time: 1090 us -> 743 us (0.68)
  local copies, waits for them, and re-layouts: 423 us -> 25 us
  waiting for transfers between devices: 462 us -> 542 us
  other arithmetic: 32.4 us -> 15.3 us
    dynamic_update_slice x16 -> x0, local copies, waits for them, and re-layouts: 329 us -> none  [the longest x8 165 us: packed_row_panel(): lax.dynamic_update_index_in_dim(stack, lax.ppermute(piece, 'tensor', pair...]
    all_gather x4 -> x6, waiting for transfers between devices: 124 us -> 168 us  [row_panel(): return lax.all_gather(local_block, GROUP, axis=1, tiled=True)]
    broadcast_in_dim x14 -> x0, local copies, waits for them, and re-layouts: 42.7 us -> none  [the longest x8 26.7 us: packed_row_panel(): lax.dynamic_update_index_in_dim(stack, lax.ppermute(piece, 'tensor', pair...]
    ppermute x23 -> x12, waiting for transfers between devices: 122 us -> 151 us  [scatter_product(): arrived.append(lax.ppermute(encode(chunk), 'shard', pairs))]
    transpose x2 -> x0, local copies, waits for them, and re-layouts: 17.7 us -> none  [packed_row_panel(): return unpack(stack).transpose(1, 0, 2).reshape(block.shape[0], -1)]
    dot_general x33 -> x36, matrix products: 75.2 us -> 75.7 us  [matmul(): jnp.dot(left_side, right_side, precision=lax.Precision.HIGH, preferred_el...]
  transfers between devices with their start and end apart: 52 -> 42, of which waited for: 26 -> 27; matrix products, arithmetic and copies ran while one was open for 47% -> 11% of each run, Pallas kernels for 0% -> 0%
where the time goes in v3:
time: 743 us; the launch traced here: 734 us
  waiting for transfers between devices  542 us (73%)
  matrix products  81.2 us (11%)
  starting transfers between devices  49.9 us (7%)
  local copies, waits for them, and re-layouts  25 us (3%)
  between operations  21.4 us (3%)
  other arithmetic  15.3 us (2%)
    all_gather x6, waiting for transfers between devices, row_panel(): return lax.all_gather(local_block, GROUP, axis=1, tiled=True)  168 us
    ppermute x12, waiting for transfers between devices, scatter_product(): arrived.append(lax.ppermute(encode(chunk), 'shard', pairs))  151 us
    ppermute x15, waiting for transfers between devices, rows_times_shards(): lax.ppermute(sent, 'shard', pairs)  143 us
    ppermute x6, waiting for transfers between devices, shard_total(): total = total + lax.ppermute(tile, 'shard', pairs)[0, 0]  78.2 us
    dot_general x36, matrix products, matmul(): jnp.dot(left_side, right_side, precision=lax.Precision.HIGH, preferred_el...  75.7 us
    ppermute x15, starting transfers between devices, rows_times_shards(): lax.ppermute(sent, 'shard', pairs)  22.2 us
  transfers between devices with their start and end apart: 42, of which 27 were waited for; matrix products, arithmetic and copies ran while one was open for 11% of the time, Pallas kernels for 0%

profile of v3, /device:TPU:8, one launch (start us, length us, event | category | flops | bytes accessed | tf_op | source)
XLA Modules:
  0.0 734.5 jit_solution(14928106622082852291)
XLA Ops:
  7.9 36.0 %all-gather.7.cloned.1.call-done = bf16[640,2560]{0,1:T(8,128)(2,1)} async-done(((bf16[640,320]{0,1:T(8,128)(2,1)}), bf16[640,2560]{0,1:T(8,128)(2,1)}) %all-gather.7.cloned.1.call-update) | async-done | bytes 3276816 | tf_op jit(solution)/shard_map/all_gather | solution.py:20
  44.0 4.1 constant_dynamic-slice_fusion
  48.1 4.1 copy.18
  53.5 1.9 collective-permute-start.4
  57.8 2.3 multiply_reduce_fusion.1
  61.4 5.8 collective-permute-start
  67.2 43.5 %collective-permute-done = f32[8,128]{1,0:T(8,128)S(1)} collective-permute-done((f32[8,128]{1,0:T(8,128)S(1)}, f32[8,128]{1,0:T(8,128)S(1)}, u32[]{:S(2)}, u32[]{:S(2)}) %collective-permute-start) | collective-permute-done | bytes 4128 | tf_op jit(solution)/shard_map/ppermute | solution.py:62
  115.5 3.9 copy.20
  119.4 3.9 copy.21
  123.2 3.8 copy.23
  127.1 5.5 fusion.152
  133.5 3.6 collective-permute-start.13
  137.0 40.8 %all-gather.11.cloned.1.call-done = f32[640,2560]{0,1:T(8,128)} async-done(((f32[640,320]{0,1:T(8,128)}), f32[640,2560]{0,1:T(8,128)}) %all-gather.11.cloned.1.call-update) | async-done | bytes 6553616 | tf_op jit(solution)/shard_map/all_gather | solution.py:20
  177.9 3.1 fusion.27
  181.0 2.7 fusion.21
  183.7 2.8 collective-permute-done.13
  187.8 2.2 fusion.101
  190.4 2.5 fusion.71
  192.9 2.6 fusion.67
  195.4 2.5 fusion.63
  197.9 2.5 collective-permute-start.6
  202.0 29.3 %collective-permute-done.6 = f32[640,320]{0,1:T(8,128)S(1)} collective-permute-done((f32[640,320]{0,1:T(8,128)S(1)}, f32[640,320]{0,1:T(8,128)S(1)}, u32[]{:S(2)}, u32[]{:S(2)}) %collective-permute-start.6) | collective-permute-done | bytes 819232 | tf_op jit(solution)/shard_map/ppermute | solution.py:94
  231.3 23.9 %collective-permute-done.7 = f32[640,320]{0,1:T(8,128)S(1)} collective-permute-done((f32[640,320]{0,1:T(8,128)S(1)}, f32[640,320]{0,1:T(8,128)S(1)}, u32[]{:S(2)}, u32[]{:S(2)}) %collective-permute-start.7) | collective-permute-done | bytes 819232 | tf_op jit(solution)/shard_map/ppermute | solution.py:94
  255.2 16.5 %collective-permute-done.8 = f32[640,320]{0,1:T(8,128)S(1)} collective-permute-done((f32[640,320]{0,1:T(8,128)S(1)}, f32[640,320]{0,1:T(8,128)S(1)}, u32[]{:S(2)}, u32[]{:S(2)}) %collective-permute-start.8) | collective-permute-done | bytes 819232 | tf_op jit(solution)/shard_map/ppermute | solution.py:94
  271.7 2.8 fusion.268
  276.2 2.8 collective-permute-start.9
  280.4 21.3 %collective-permute-done.10 = f16[640,320]{0,1:T(8,128)(2,1)S(1)} collective-permute-done((f16[640,320]{0,1:T(8,128)(2,1)S(1)}, f16[640,320]{0,1:T(8,128)(2,1)S(1)}, u32[]{:S(2)}, u32[]{:S(2)}) %collective-permute-start.10) | collective-permute-done | bytes 409632 | tf_op jit(solution)/shard_map/ppermute | solution.py:73
  303.0 7.1 collective-permute-done.11
  311.5 2.2 fusion.146
  313.8 3.0 abs_reduce_fusion.11
  316.8 3.3 abs_reduce_fusion.10
  322.5 1.9 collective-permute-start.19
  326.5 2.3 multiply_reduce_fusion
  331.4 24.1 %collective-permute-done.15 = f32[8,128]{1,0:T(8,128)S(1)} collective-permute-done((f32[8,128]{1,0:T(8,128)S(1)}, f32[8,128]{1,0:T(8,128)S(1)}, u32[]{:S(2)}, u32[]{:S(2)}) %collective-permute-start.15) | collective-permute-done | bytes 4128 | tf_op jit(solution)/shard_map/ppermute | solution.py:62
  357.3 7.6 %collective-permute-done.16 = f32[8,128]{1,0:T(8,128)S(1)} collective-permute-done((f32[8,128]{1,0:T(8,128)S(1)}, f32[8,128]{1,0:T(8,128)S(1)}, u32[]{:S(2)}, u32[]{:S(2)}) %collective-permute-start.16) | collective-permute-done | bytes 4128 | tf_op jit(solution)/shard_map/ppermute | solution.py:62
  371.1 3.4 abs_reduce_fusion.8
  376.9 2.5 collective-permute-start.23
  381.2 25.5 %collective-permute-done.22 = f16[656,320]{0,1:T(8,128)(2,1)S(1)} collective-permute-done((f16[656,320]{0,1:T(8,128)(2,1)S(1)}, f16[656,320]{0,1:T(8,128)(2,1)S(1)}, u32[]{:S(2)}, u32[]{:S(2)}) %collective-permute-start.22) | collective-permute-done | bytes 419872 | tf_op jit(solution)/shard_map/ppermute | solution.py:73
  408.2 10.3 %collective-permute-done.23 = f16[656,320]{0,1:T(8,128)(2,1)S(1)} collective-permute-done((f16[656,320]{0,1:T(8,128)(2,1)S(1)}, f16[656,320]{0,1:T(8,128)(2,1)S(1)}, u32[]{:S(2)}, u32[]{:S(2)}) %collective-permute-start.23) | collective-permute-done | bytes 419872 | tf_op jit(solution)/shard_map/ppermute | solution.py:73
  420.5 2.4 multiply_subtract_fusion
  423.0 46.7 %all-gather.15.cloned.1.call-done = f32[640,2560]{0,1:T(8,128)} async-done(((f32[640,320]{0,1:T(8,128)}), f32[640,2560]{0,1:T(8,128)}) %all-gather.15.cloned.1.call-update) | async-done | bytes 6553616 | tf_op jit(solution)/shard_map/all_gather | solution.py:20
  469.6 3.1 abs_reduce_fusion.7
  473.9 3.2 abs_reduce_fusion.6
  477.5 2.5 collective-permute-start.25
  482.2 9.0 %collective-permute-done.24 = f16[656,320]{0,1:T(8,128)(2,1)S(1)} collective-permute-done((f16[656,320]{0,1:T(8,128)(2,1)S(1)}, f16[656,320]{0,1:T(8,128)(2,1)S(1)}, u32[]{:S(2)}, u32[]{:S(2)}) %collective-permute-start.24) | collective-permute-done | bytes 419872 | tf_op jit(solution)/shard_map/ppermute | solution.py:94
  491.2 21.4 %collective-permute-done.25 = f16[656,320]{0,1:T(8,128)(2,1)S(1)} collective-permute-done((f16[656,320]{0,1:T(8,128)(2,1)S(1)}, f16[656,320]{0,1:T(8,128)(2,1)S(1)}, u32[]{:S(2)}, u32[]{:S(2)}) %collective-permute-start.25) | collective-permute-done | bytes 419872 | tf_op jit(solution)/shard_map/ppermute | solution.py:94
  513.0 10.2 %collective-permute-done.26 = f16[656,320]{0,1:T(8,128)(2,1)S(1)} collective-permute-done((f16[656,320]{0,1:T(8,128)(2,1)S(1)}, f16[656,320]{0,1:T(8,128)(2,1)S(1)}, u32[]{:S(2)}, u32[]{:S(2)}) %collective-permute-start.26) | collective-permute-done | bytes 419872 | tf_op jit(solution)/shard_map/ppermute | solution.py:94
  523.5 1.8 abs_reduce_fusion.4
  527.6 2.5 collective-permute-start.27
  531.5 27.0 %collective-permute-done.28 = f16[656,320]{0,1:T(8,128)(2,1)S(1)} collective-permute-done((f16[656,320]{0,1:T(8,128)(2,1)S(1)}, f16[656,320]{0,1:T(8,128)(2,1)S(1)}, u32[]{:S(2)}, u32[]{:S(2)}) %collective-permute-start.28) | collective-permute-done | bytes 419872 | tf_op jit(solution)/shard_map/ppermute | solution.py:73
  558.6 11.4 %collective-permute-done.29 = f16[656,320]{0,1:T(8,128)(2,1)S(1)} collective-permute-done((f16[656,320]{0,1:T(8,128)(2,1)S(1)}, f16[656,320]{0,1:T(8,128)(2,1)S(1)}, u32[]{:S(2)}, u32[]{:S(2)}) %collective-permute-start.29) | collective-permute-done | bytes 419872 | tf_op jit(solution)/shard_map/ppermute | solution.py:73
  573.6 2.3 fusion.125
  575.9 44.9 %all-gather.17.cloned.1.call-done = f32[640,2560]{0,1:T(8,128)} async-done(((f32[640,320]{0,1:T(8,128)}), f32[640,2560]{0,1:T(8,128)}) %all-gather.17.cloned.1.call-update) | async-done | bytes 6553616 | tf_op jit(solution)/shard_map/all_gather | solution.py:20
  620.9 3.1 abs_reduce_fusion.3
  625.1 3.2 abs_reduce_fusion.2
  628.8 2.5 collective-permute-start.31
  633.4 9.0 %collective-permute-done.30 = f16[656,320]{0,1:T(8,128)(2,1)S(1)} collective-permute-done((f16[656,320]{0,1:T(8,128)(2,1)S(1)}, f16[656,320]{0,1:T(8,128)(2,1)S(1)}, u32[]{:S(2)}, u32[]{:S(2)}) %collective-permute-start.30) | collective-permute-done | bytes 419872 | tf_op jit(solution)/shard_map/ppermute | solution.py:94
  642.5 21.4 %collective-permute-done.31 = f16[656,320]{0,1:T(8,128)(2,1)S(1)} collective-permute-done((f16[656,320]{0,1:T(8,128)(2,1)S(1)}, f16[656,320]{0,1:T(8,128)(2,1)S(1)}, u32[]{:S(2)}, u32[]{:S(2)}) %collective-permute-start.31) | collective-permute-done | bytes 419872 | tf_op jit(solution)/shard_map/ppermute | solution.py:94
  664.3 10.2 %collective-permute-done.32 = f16[656,320]{0,1:T(8,128)(2,1)S(1)} collective-permute-done((f16[656,320]{0,1:T(8,128)(2,1)S(1)}, f16[656,320]{0,1:T(8,128)(2,1)S(1)}, u32[]{:S(2)}, u32[]{:S(2)}) %collective-permute-start.32) | collective-permute-done | bytes 419872 | tf_op jit(solution)/shard_map/ppermute | solution.py:94
  674.7 1.8 abs_reduce_fusion
  679.5 2.5 collective-permute-start.33
  683.4 26.4 %collective-permute-done.34 = f16[656,320]{0,1:T(8,128)(2,1)S(1)} collective-permute-done((f16[656,320]{0,1:T(8,128)(2,1)S(1)}, f16[656,320]{0,1:T(8,128)(2,1)S(1)}, u32[]{:S(2)}, u32[]{:S(2)}) %collective-permute-start.34) | collective-permute-done | bytes 419872 | tf_op jit(solution)/shard_map/ppermute | solution.py:73
  709.9 11.4 %collective-permute-done.35 = f16[656,320]{0,1:T(8,128)(2,1)S(1)} collective-permute-done((f16[656,320]{0,1:T(8,128)(2,1)S(1)}, f16[656,320]{0,1:T(8,128)(2,1)S(1)}, u32[]{:S(2)}, u32[]{:S(2)}) %collective-permute-start.35) | collective-permute-done | bytes 419872 | tf_op jit(solution)/shard_map/ppermute | solution.py:73
  724.9 2.3 fusion.113
  (211 shorter events, 60.9 us)
Async XLA Ops:
  7.2 36.8 %all-gather.7.cloned.1.call-start = ((), (), s32[]{:S(2)}) async-start(), calls=%async_computation | async-start | bytes 3686400 | tf_op jit(solution)/shard_map/all_gather | solution.py:20
  7.9 124.7 %all-gather.9.cloned.1.call-start = ((), (), s32[]{:S(2)}) async-start(), calls=%async_computation.1 | async-start | bytes 7372800 | tf_op jit(solution)/shard_map/all_gather | solution.py:20
  44.0 133.9 %all-gather.11.cloned.1.call-start = ((), (), s32[]{:S(2)}) async-start(), calls=%async_computation.2 | async-start | bytes 7372800 | tf_op jit(solution)/shard_map/all_gather | solution.py:20
  48.1 9.1 %copy-start.13 = (f32[2,640]{1,0:T(2,128)S(1)}, f32[2,640]{1,0:T(2,128)}, u32[]{:S(2)}) copy-start(f32[2,640]{1,0:T(2,128)} %param.10) | copy-start | bytes 15364
  48.1 9.7 %copy-start.7 = (bf16[640,2560]{0,1:T(8,128)(2,1)S(1)}, bf16[640,2560]{0,1:T(8,128)(2,1)}, u32[]{:S(2)}) copy-start(bf16[640,2560]{0,1:T(8,128)(2,1)} %all-gather.7.cloned.1.call-done) | copy-start | bytes 9830404
  52.2 63.3 %collective-permute-start.3 = (bf16[320,2560]{1,0:T(8,128)(2,1)}, bf16[320,2560]{1,0:T(8,128)(2,1)}, u32[]{:S(2)}, u32[]{:S(2)}) collective-permute-start(bf16[320,2560]{1,0:T(8,128)(2,1)} %copy.18), channel_id=1, source_target_pairs={{0,8},{1,9},{10,18},{11,19},{20,28},{21,29},{30,6},{31,7}} | collective-permute-start | bytes 4915208 | tf_op jit(solution)/shard_map/ppermute | solution.py:113
  53.5 65.9 %collective-permute-start.4 = (bf16[320,2560]{1,0:T(8,128)(2,1)}, bf16[320,2560]{1,0:T(8,128)(2,1)}, u32[]{:S(2)}, u32[]{:S(2)}) collective-permute-start(bf16[320,2560]{1,0:T(8,128)(2,1)} %copy.18), channel_id=1, source_target_pairs={{0,16},{1,17},{10,26},{11,27},{20,4},{21,5},{30,14},{31,15}} | collective-permute-start | bytes 4915208 | tf_op jit(solution)/shard_map/ppermute | solution.py:113
  55.4 67.9 %collective-permute-start.5 = (bf16[320,2560]{1,0:T(8,128)(2,1)}, bf16[320,2560]{1,0:T(8,128)(2,1)}, u32[]{:S(2)}, u32[]{:S(2)}) collective-permute-start(bf16[320,2560]{1,0:T(8,128)(2,1)} %copy.18), channel_id=1, source_target_pairs={{0,24},{1,25},{10,2},{11,3},{20,12},{21,13},{30,22},{31,23}} | collective-permute-start | bytes 4915208 | tf_op jit(solution)/shard_map/ppermute | solution.py:113
  61.4 49.3 %collective-permute-start = (f32[8,128]{1,0:T(8,128)S(1)}, f32[8,128]{1,0:T(8,128)S(1)}, u32[]{:S(2)}, u32[]{:S(2)}) collective-permute-start(f32[8,128]{1,0:T(8,128)S(1)} %broadcast_in_dim.28), channel_id=1, source_target_pairs={{0,8},{8,0},{16,24},{24,16},{1,9},{9,1},{17,25},{25,17},{2,10},{10... | collective-permute-start | bytes 12296 | tf_op jit(solution)/shard_map/ppermute | solution.py:62
  67.2 44.7 %collective-permute-start.1 = (f32[8,128]{1,0:T(8,128)S(1)}, f32[8,128]{1,0:T(8,128)S(1)}, u32[]{:S(2)}, u32[]{:S(2)}) collective-permute-start(f32[8,128]{1,0:T(8,128)S(1)} %broadcast_in_dim.28), channel_id=1, source_target_pairs={{0,16},{8,24},{16,0},{24,8},{1,17},{9,25},{17,1},{25,9},{2,18},{10... | collective-permute-start | bytes 12296 | tf_op jit(solution)/shard_map/ppermute | solution.py:62
  110.7 3.6 collective-permute-start.2
  132.6 181.2 %all-gather.13.cloned.1.call-start = ((), (), s32[]{:S(2)}) async-start(), calls=%async_computation.3 | async-start | bytes 7372800 | tf_op jit(solution)/shard_map/all_gather | solution.py:20
  132.6 48.3 %collective-permute-start.14 = (f32[640,320]{0,1:T(8,128)}, f32[640,320]{0,1:T(8,128)S(1)}, u32[]{:S(2)}, u32[]{:S(2)}) collective-permute-start(f32[640,320]{0,1:T(8,128)} %param.12), channel_id=1, source_target_pairs={{0,24},{8,16},{16,8},{24,0},{1,25},{9,17},{17,9},{25,1},{2,26},{10... | collective-permute-start | bytes 2457608 | tf_op jit(solution)/shard_map/ppermute | solution.py:73
  133.5 53.0 %collective-permute-start.13 = (f32[640,320]{0,1:T(8,128)}, f32[640,320]{0,1:T(8,128)S(1)}, u32[]{:S(2)}, u32[]{:S(2)}) collective-permute-start(f32[640,320]{0,1:T(8,128)} %param.12), channel_id=1, source_target_pairs={{0,16},{8,24},{16,0},{24,8},{1,17},{9,25},{17,1},{25,9},{2,18},{10... | collective-permute-start | bytes 2457608 | tf_op jit(solution)/shard_map/ppermute | solution.py:73
  137.0 50.8 %collective-permute-start.12 = (f32[640,320]{0,1:T(8,128)}, f32[640,320]{0,1:T(8,128)S(1)}, u32[]{:S(2)}, u32[]{:S(2)}) collective-permute-start(f32[640,320]{0,1:T(8,128)} %param.12), channel_id=1, source_target_pairs={{0,8},{8,0},{16,24},{24,16},{1,9},{9,1},{17,25},{25,17},{2,10},{10... | collective-permute-start | bytes 2457608 | tf_op jit(solution)/shard_map/ppermute | solution.py:73
  177.9 8.6 %copy-start.8 = (f32[640,2560]{0,1:T(8,128)S(1)}, f32[640,2560]{0,1:T(8,128)}, u32[]{:S(2)}) copy-start(f32[640,2560]{0,1:T(8,128)} %all-gather.11.cloned.1.call-done) | copy-start | bytes 19660804
  187.8 2.6 copy-start.6
  190.1 279.5 %all-gather.15.cloned.1.call-start = ((), (), s32[]{:S(2)}) async-start(), calls=%async_computation.4 | async-start | bytes 7372800 | tf_op jit(solution)/shard_map/all_gather | solution.py:20
  190.4 81.3 %copy-start.10 = (f32[640,320]{0,1:T(8,128)S(1)}, f32[640,320]{0,1:T(8,128)}, u32[]{:S(2)}) copy-start(f32[640,320]{0,1:T(8,128)} %param.13) | copy-start | bytes 2457604
  192.8 86.1 %slice-start.2 = ((s8[6553600]{0:T(1024)(128)(4,1)}), s8[4194304]{0:T(1024)(128)(4,1)S(1)}, s32[]{:S(2)}) async-start(s8[6553600]{0:T(1024)(128)(4,1)} %bitcast.35), calls=%async_computation.8 | async-start | bytes 8388608
  195.4 76.2 %copy-start.9 = (f32[640,320]{0,1:T(8,128)S(1)}, f32[640,320]{0,1:T(8,128)}, u32[]{:S(2)}) copy-start(f32[640,320]{0,1:T(8,128)} %param.14) | copy-start | bytes 2457604
  197.9 81.1 %slice-start.3 = ((s8[6553600]{0:T(1024)(128)(4,1)}), s8[2359296]{0:T(1024)(128)(4,1)S(1)}, s32[]{:S(2)}) async-start(s8[6553600]{0:T(1024)(128)(4,1)} %bitcast.35), calls=%async_computation.9 | async-start | bytes 4718592
  197.9 33.4 %collective-permute-start.6 = (f32[640,320]{0,1:T(8,128)S(1)}, f32[640,320]{0,1:T(8,128)S(1)}, u32[]{:S(2)}, u32[]{:S(2)}) collective-permute-start(f32[640,320]{0,1:T(8,128)S(1)} %fusion.71), channel_id=1, source_target_pairs={{0,8},{8,0},{16,24},{24,16},{1,9},{9,1},{17,25},{25,17},{2,10},{10... | collective-permute-start | bytes 2457608 | tf_op jit(solution)/shard_map/ppermute | solution.py:94
  200.4 54.8 %collective-permute-start.7 = (f32[640,320]{0,1:T(8,128)S(1)}, f32[640,320]{0,1:T(8,128)S(1)}, u32[]{:S(2)}, u32[]{:S(2)}) collective-permute-start(f32[640,320]{0,1:T(8,128)S(1)} %fusion.67), channel_id=1, source_target_pairs={{0,16},{8,24},{16,0},{24,8},{1,17},{9,25},{17,1},{25,9},{2,18},{10... | collective-permute-start | bytes 2457608 | tf_op jit(solution)/shard_map/ppermute | solution.py:94
  201.4 70.3 %collective-permute-start.8 = (f32[640,320]{0,1:T(8,128)S(1)}, f32[640,320]{0,1:T(8,128)S(1)}, u32[]{:S(2)}, u32[]{:S(2)}) collective-permute-start(f32[640,320]{0,1:T(8,128)S(1)} %fusion.63), channel_id=1, source_target_pairs={{0,24},{8,16},{16,8},{24,0},{1,25},{9,17},{17,9},{25,1},{2,26},{10... | collective-permute-start | bytes 2457608 | tf_op jit(solution)/shard_map/ppermute | solution.py:94
  274.5 5.9 copy-start.11
  274.5 5.9 copy-start.12
  274.5 27.2 %collective-permute-start.10 = (f16[640,320]{0,1:T(8,128)(2,1)S(1)}, f16[640,320]{0,1:T(8,128)(2,1)S(1)}, u32[]{:S(2)}, u32[]{:S(2)}) collective-permute-start(f16[640,320]{0,1:T(8,128)(2,1)S(1)} %get-tuple-element.23), channel_id=1, source_target_pairs={{0,16},{8,24},{16,0},{24,8},{1,17},{9,25},{17,1},{25,9},{2,18},{10... | collective-permute-start | bytes 1228808 | tf_op jit(solution)/shard_map/ppermute | solution.py:73
  274.6 35.6 %collective-permute-start.11 = (f16[640,320]{0,1:T(8,128)(2,1)S(1)}, f16[640,320]{0,1:T(8,128)(2,1)S(1)}, u32[]{:S(2)}, u32[]{:S(2)}) collective-permute-start(f16[640,320]{0,1:T(8,128)(2,1)S(1)} %get-tuple-element.23), channel_id=1, source_target_pairs={{0,24},{8,16},{16,8},{24,0},{1,25},{9,17},{17,9},{25,1},{2,26},{10... | collective-permute-start | bytes 1228808 | tf_op jit(solution)/shard_map/ppermute | solution.py:73
  276.2 35.3 %collective-permute-start.9 = (f16[640,320]{0,1:T(8,128)(2,1)S(1)}, f16[640,320]{0,1:T(8,128)(2,1)S(1)}, u32[]{:S(2)}, u32[]{:S(2)}) collective-permute-start(f16[640,320]{0,1:T(8,128)(2,1)S(1)} %get-tuple-element.23), channel_id=1, source_target_pairs={{0,8},{8,0},{16,24},{24,16},{1,9},{9,1},{17,25},{25,17},{2,10},{10... | collective-permute-start | bytes 1228808 | tf_op jit(solution)/shard_map/ppermute | solution.py:73
  311.5 2.3 copy-start.3
  313.8 6.4 copy-start
  322.0 47.1 %collective-permute-start.18 = (f16[656,320]{0,1:T(8,128)(2,1)S(1)}, f16[656,320]{0,1:T(8,128)(2,1)S(1)}, u32[]{:S(2)}, u32[]{:S(2)}) collective-permute-start(f16[656,320]{0,1:T(8,128)(2,1)S(1)} %pad_maximum_fusion), channel_id=1, source_target_pairs={{0,8},{8,0},{16,24},{24,16},{1,9},{9,1},{17,25},{25,17},{2,10},{10... | collective-permute-start | bytes 1259528 | tf_op jit(solution)/shard_map/ppermute | solution.py:94
  322.5 46.7 %collective-permute-start.19 = (f16[656,320]{0,1:T(8,128)(2,1)S(1)}, f16[656,320]{0,1:T(8,128)(2,1)S(1)}, u32[]{:S(2)}, u32[]{:S(2)}) collective-permute-start(f16[656,320]{0,1:T(8,128)(2,1)S(1)} %pad_maximum_fusion.1), channel_id=1, source_target_pairs={{0,16},{8,24},{16,0},{24,8},{1,17},{9,25},{17,1},{25,9},{2,18},{10... | collective-permute-start | bytes 1259528 | tf_op jit(solution)/shard_map/ppermute | solution.py:94
  324.8 44.8 %collective-permute-start.20 = (f16[656,320]{0,1:T(8,128)(2,1)S(1)}, f16[656,320]{0,1:T(8,128)(2,1)}, u32[]{:S(2)}, u32[]{:S(2)}) collective-permute-start(f16[656,320]{0,1:T(8,128)(2,1)S(1)} %pad_maximum_fusion.2), channel_id=1, source_target_pairs={{0,24},{8,16},{16,8},{24,0},{1,25},{9,17},{17,9},{25,1},{2,26},{10... | collective-permute-start | bytes 1259528 | tf_op jit(solution)/shard_map/ppermute | solution.py:94
  329.5 26.0 %collective-permute-start.15 = (f32[8,128]{1,0:T(8,128)S(1)}, f32[8,128]{1,0:T(8,128)S(1)}, u32[]{:S(2)}, u32[]{:S(2)}) collective-permute-start(f32[8,128]{1,0:T(8,128)S(1)} %broadcast_in_dim.29), channel_id=1, source_target_pairs={{0,8},{8,0},{16,24},{24,16},{1,9},{9,1},{17,25},{25,17},{2,10},{10... | collective-permute-start | bytes 12296 | tf_op jit(solution)/shard_map/ppermute | solution.py:62
  330.5 34.4 %collective-permute-start.16 = (f32[8,128]{1,0:T(8,128)S(1)}, f32[8,128]{1,0:T(8,128)S(1)}, u32[]{:S(2)}, u32[]{:S(2)}) collective-permute-start(f32[8,128]{1,0:T(8,128)S(1)} %broadcast_in_dim.29), channel_id=1, source_target_pairs={{0,16},{8,24},{16,0},{24,8},{1,17},{9,25},{17,1},{25,9},{2,18},{10... | collective-permute-start | bytes 12296 | tf_op jit(solution)/shard_map/ppermute | solution.py:62
  355.4 12.4 %collective-permute-start.17 = (f32[8,128]{1,0:T(8,128)S(1)}, f32[8,128]{1,0:T(8,128)S(1)}, u32[]{:S(2)}, u32[]{:S(2)}) collective-permute-start(f32[8,128]{1,0:T(8,128)S(1)} %broadcast_in_dim.29), channel_id=1, source_target_pairs={{0,24},{8,16},{16,8},{24,0},{1,25},{9,17},{17,9},{25,1},{2,26},{10... | collective-permute-start | bytes 12296 | tf_op jit(solution)/shard_map/ppermute | solution.py:62
  369.1 7.4 %slice-start = ((s8[6553600]{0:T(1024)(128)(4,1)}), s8[4194304]{0:T(1024)(128)(4,1)S(1)}, s32[]{:S(2)}) async-start(s8[6553600]{0:T(1024)(128)(4,1)} %bitcast.33), calls=%async_computation.6 | async-start | bytes 8388608
  371.1 5.4 slice-start.1
  374.9 31.7 %collective-permute-start.22 = (f16[656,320]{0,1:T(8,128)(2,1)S(1)}, f16[656,320]{0,1:T(8,128)(2,1)S(1)}, u32[]{:S(2)}, u32[]{:S(2)}) collective-permute-start(f16[656,320]{0,1:T(8,128)(2,1)S(1)} %pad_maximum_fusion.3), channel_id=1, source_target_pairs={{0,16},{8,24},{16,0},{24,8},{1,17},{9,25},{17,1},{25,9},{2,18},{10... | collective-permute-start | bytes 1259528 | tf_op jit(solution)/shard_map/ppermute | solution.py:73
  376.9 41.6 %collective-permute-start.23 = (f16[656,320]{0,1:T(8,128)(2,1)S(1)}, f16[656,320]{0,1:T(8,128)(2,1)S(1)}, u32[]{:S(2)}, u32[]{:S(2)}) collective-permute-start(f16[656,320]{0,1:T(8,128)(2,1)S(1)} %pad_maximum_fusion.3), channel_id=1, source_target_pairs={{0,24},{8,16},{16,8},{24,0},{1,25},{9,17},{17,9},{25,1},{2,26},{10... | collective-permute-start | bytes 1259528 | tf_op jit(solution)/shard_map/ppermute | solution.py:73
  379.5 40.6 %collective-permute-start.21 = (f16[656,320]{0,1:T(8,128)(2,1)S(1)}, f16[656,320]{0,1:T(8,128)(2,1)S(1)}, u32[]{:S(2)}, u32[]{:S(2)}) collective-permute-start(f16[656,320]{0,1:T(8,128)(2,1)S(1)} %pad_maximum_fusion.3), channel_id=1, source_target_pairs={{0,8},{8,0},{16,24},{24,16},{1,9},{9,1},{17,25},{25,17},{2,10},{10... | collective-permute-start | bytes 1259528 | tf_op jit(solution)/shard_map/ppermute | solution.py:73
  422.9 198.0 %all-gather.17.cloned.1.call-start = ((), (), s32[]{:S(2)}) async-start(), calls=%async_computation.5 | async-start | bytes 7372800 | tf_op jit(solution)/shard_map/all_gather | solution.py:20
  472.7 1.1 copy-start.2
  473.0 7.0 copy-start.5
  473.1 18.0 %collective-permute-start.24 = (f16[656,320]{0,1:T(8,128)(2,1)S(1)}, f16[656,320]{0,1:T(8,128)(2,1)S(1)}, u32[]{:S(2)}, u32[]{:S(2)}) collective-permute-start(f16[656,320]{0,1:T(8,128)(2,1)S(1)} %pad_maximum_fusion.4), channel_id=1, source_target_pairs={{0,8},{8,0},{16,24},{24,16},{1,9},{9,1},{17,25},{25,17},{2,10},{10... | collective-permute-start | bytes 1259528 | tf_op jit(solution)/shard_map/ppermute | solution.py:94
  477.5 35.2 %collective-permute-start.25 = (f16[656,320]{0,1:T(8,128)(2,1)S(1)}, f16[656,320]{0,1:T(8,128)(2,1)S(1)}, u32[]{:S(2)}, u32[]{:S(2)}) collective-permute-start(f16[656,320]{0,1:T(8,128)(2,1)S(1)} %pad_maximum_fusion.5), channel_id=1, source_target_pairs={{0,16},{8,24},{16,0},{24,8},{1,17},{9,25},{17,1},{25,9},{2,18},{10... | collective-permute-start | bytes 1259528 | tf_op jit(solution)/shard_map/ppermute | solution.py:94
  481.9 41.4 %collective-permute-start.26 = (f16[656,320]{0,1:T(8,128)(2,1)S(1)}, f16[656,320]{0,1:T(8,128)(2,1)S(1)}, u32[]{:S(2)}, u32[]{:S(2)}) collective-permute-start(f16[656,320]{0,1:T(8,128)(2,1)S(1)} %pad_maximum_fusion.6), channel_id=1, source_target_pairs={{0,24},{8,16},{16,8},{24,0},{1,25},{9,17},{17,9},{25,1},{2,26},{10... | collective-permute-start | bytes 1259528 | tf_op jit(solution)/shard_map/ppermute | solution.py:94
  525.7 32.8 %collective-permute-start.28 = (f16[656,320]{0,1:T(8,128)(2,1)S(1)}, f16[656,320]{0,1:T(8,128)(2,1)S(1)}, u32[]{:S(2)}, u32[]{:S(2)}) collective-permute-start(f16[656,320]{0,1:T(8,128)(2,1)S(1)} %pad_maximum_fusion.7), channel_id=1, source_target_pairs={{0,16},{8,24},{16,0},{24,8},{1,17},{9,25},{17,1},{25,9},{2,18},{10... | collective-permute-start | bytes 1259528 | tf_op jit(solution)/shard_map/ppermute | solution.py:73
  525.8 44.2 %collective-permute-start.29 = (f16[656,320]{0,1:T(8,128)(2,1)S(1)}, f16[656,320]{0,1:T(8,128)(2,1)S(1)}, u32[]{:S(2)}, u32[]{:S(2)}) collective-permute-start(f16[656,320]{0,1:T(8,128)(2,1)S(1)} %pad_maximum_fusion.7), channel_id=1, source_target_pairs={{0,24},{8,16},{16,8},{24,0},{1,25},{9,17},{17,9},{25,1},{2,26},{10... | collective-permute-start | bytes 1259528 | tf_op jit(solution)/shard_map/ppermute | solution.py:73
  527.6 42.8 %collective-permute-start.27 = (f16[656,320]{0,1:T(8,128)(2,1)S(1)}, f16[656,320]{0,1:T(8,128)(2,1)S(1)}, u32[]{:S(2)}, u32[]{:S(2)}) collective-permute-start(f16[656,320]{0,1:T(8,128)(2,1)S(1)} %pad_maximum_fusion.7), channel_id=1, source_target_pairs={{0,8},{8,0},{16,24},{24,16},{1,9},{9,1},{17,25},{25,17},{2,10},{10... | collective-permute-start | bytes 1259528 | tf_op jit(solution)/shard_map/ppermute | solution.py:73
  624.0 1.1 copy-start.1
  624.2 7.0 copy-start.4
  624.4 18.0 %collective-permute-start.30 = (f16[656,320]{0,1:T(8,128)(2,1)S(1)}, f16[656,320]{0,1:T(8,128)(2,1)S(1)}, u32[]{:S(2)}, u32[]{:S(2)}) collective-permute-start(f16[656,320]{0,1:T(8,128)(2,1)S(1)} %pad_maximum_fusion.8), channel_id=1, source_target_pairs={{0,8},{8,0},{16,24},{24,16},{1,9},{9,1},{17,25},{25,17},{2,10},{10... | collective-permute-start | bytes 1259528 | tf_op jit(solution)/shard_map/ppermute | solution.py:94
  628.8 35.2 %collective-permute-start.31 = (f16[656,320]{0,1:T(8,128)(2,1)S(1)}, f16[656,320]{0,1:T(8,128)(2,1)S(1)}, u32[]{:S(2)}, u32[]{:S(2)}) collective-permute-start(f16[656,320]{0,1:T(8,128)(2,1)S(1)} %pad_maximum_fusion.9), channel_id=1, source_target_pairs={{0,16},{8,24},{16,0},{24,8},{1,17},{9,25},{17,1},{25,9},{2,18},{10... | collective-permute-start | bytes 1259528 | tf_op jit(solution)/shard_map/ppermute | solution.py:94
  633.1 41.4 %collective-permute-start.32 = (f16[656,320]{0,1:T(8,128)(2,1)S(1)}, f16[656,320]{0,1:T(8,128)(2,1)S(1)}, u32[]{:S(2)}, u32[]{:S(2)}) collective-permute-start(f16[656,320]{0,1:T(8,128)(2,1)S(1)} %pad_maximum_fusion.10), channel_id=1, source_target_pairs={{0,24},{8,16},{16,8},{24,0},{1,25},{9,17},{17,9},{25,1},{2,26},{10... | collective-permute-start | bytes 1259528 | tf_op jit(solution)/shard_map/ppermute | solution.py:94
  676.6 2.4 copy-start.14
  676.6 2.4 copy-start.15
  676.6 2.3 copy-start.16
  677.0 32.8 %collective-permute-start.34 = (f16[656,320]{0,1:T(8,128)(2,1)S(1)}, f16[656,320]{0,1:T(8,128)(2,1)S(1)}, u32[]{:S(2)}, u32[]{:S(2)}) collective-permute-start(f16[656,320]{0,1:T(8,128)(2,1)S(1)} %pad_maximum_fusion.11), channel_id=1, source_target_pairs={{0,16},{8,24},{16,0},{24,8},{1,17},{9,25},{17,1},{25,9},{2,18},{10... | collective-permute-start | bytes 1259528 | tf_op jit(solution)/shard_map/ppermute | solution.py:73
  677.1 44.2 %collective-permute-start.35 = (f16[656,320]{0,1:T(8,128)(2,1)S(1)}, f16[656,320]{0,1:T(8,128)(2,1)S(1)}, u32[]{:S(2)}, u32[]{:S(2)}) collective-permute-start(f16[656,320]{0,1:T(8,128)(2,1)S(1)} %pad_maximum_fusion.11), channel_id=1, source_target_pairs={{0,24},{8,16},{16,8},{24,0},{1,25},{9,17},{17,9},{25,1},{2,26},{10... | collective-permute-start | bytes 1259528 | tf_op jit(solution)/shard_map/ppermute | solution.py:73
  679.5 42.2 %collective-permute-start.33 = (f16[656,320]{0,1:T(8,128)(2,1)S(1)}, f16[656,320]{0,1:T(8,128)(2,1)S(1)}, u32[]{:S(2)}, u32[]{:S(2)}) collective-permute-start(f16[656,320]{0,1:T(8,128)(2,1)S(1)} %pad_maximum_fusion.11), channel_id=1, source_target_pairs={{0,8},{8,0},{16,24},{24,16},{1,9},{9,1},{17,25},{25,17},{2,10},{10... | collective-permute-start | bytes 1259528 | tf_op jit(solution)/shard_map/ppermute | solution.py:73
Sparse Core Ops, SparseCore 0:
  9.9 34.0 all-gather.6
  45.8 46.6 all-gather.8
  132.7 45.0 all-gather.10
  190.2 47.2 all-gather.12
  423.0 46.5 all-gather.14
  576.1 44.7 all-gather.16

commit v4 on v3

--- a/solution.py
+++ b/solution.py
@@ -147,13 +147,14 @@
     new_statistic = 0.95 * left_statistic + (0.05 / D * clip_factor * clip_factor) * outer_part
     ready_statistic, basis_rows = lax.optimization_barrier((new_statistic, basis_rows))
     statistic_rows = row_panel(ready_statistic)
+    rotated = clip_factor * scatter_product(
+        basis_rows, grad_float, shards, place, same, same
+    )
+    rotated, statistic_rows = lax.optimization_barrier((rotated, statistic_rows))
     power_product = rows_times_shards(
         statistic_rows, left_basis, shards, place, same, same
     )
     power_rows = row_panel(power_product)
-    rotated = clip_factor * scatter_product(
-        basis_rows, grad_float, shards, place, same, same
-    )
     new_first = 0.9 * first_moment + 0.1 * rotated
     new_second = 0.95 * second_moment + 0.05 * rotated * rotated
     direction = new_first / (jnp.sqrt(new_second) + 1e-08)

time: 743 us -> 746 us (level)
  waiting for transfers between devices: 542 us -> 531 us
  matrix products: 81.2 us -> 90.7 us
    all_gather x6, waiting for transfers between devices: 168 us -> 137 us  [row_panel(): return lax.all_gather(local_block, GROUP, axis=1, tiled=True)]
    ppermute x12, waiting for transfers between devices: 151 us -> 165 us  [scatter_product(): arrived.append(lax.ppermute(encode(chunk), 'shard', pairs))]
    dot_general x36, matrix products: 75.7 us -> 84.4 us  [matmul(): jnp.dot(left_side, right_side, precision=lax.Precision.HIGH, preferred_el...]
    ppermute x15, waiting for transfers between devices: 143 us -> 152 us  [rows_times_shards(): lax.ppermute(sent, 'shard', pairs)]
  transfers between devices with their start and end apart: 42 -> 42, of which waited for: 27 -> 27; matrix products, arithmetic and copies ran while one was open for 11% -> 12% of each run, Pallas kernels for 0% -> 0%
where the time goes in v4:
time: 746 us; the launch traced here: 741 us
  waiting for transfers between devices  531 us (71%)
  matrix products  90.7 us (12%)
  starting transfers between devices  57.1 us (8%)
  local copies, waits for them, and re-layouts  25.2 us (3%)
  between operations  21.2 us (3%)
  other arithmetic  15.8 us (2%)
    ppermute x12, waiting for transfers between devices, scatter_product(): arrived.append(lax.ppermute(encode(chunk), 'shard', pairs))  165 us
    ppermute x15, waiting for transfers between devices, rows_times_shards(): lax.ppermute(sent, 'shard', pairs)  152 us
    all_gather x6, waiting for transfers between devices, row_panel(): return lax.all_gather(local_block, GROUP, axis=1, tiled=True)  137 us
    dot_general x36, matrix products, matmul(): jnp.dot(left_side, right_side, precision=lax.Precision.HIGH, preferred_el...  84.4 us
    ppermute x6, waiting for transfers between devices, shard_total(): total = total + lax.ppermute(tile, 'shard', pairs)[0, 0]  76.6 us
    ppermute x15, starting transfers between devices, rows_times_shards(): lax.ppermute(sent, 'shard', pairs)  26.2 us
  transfers between devices with their start and end apart: 42, of which 27 were waited for; matrix products, arithmetic and copies ran while one was open for 12% of the time, Pallas kernels for 0%

profile of v4, /device:TPU:8, one launch (start us, length us, event | category | flops | bytes accessed | tf_op | source)
XLA Modules:
  0.0 741.1 jit_solution(10693423935516945272)
XLA Ops:
  7.9 36.0 %all-gather.7.cloned.1.call-done = bf16[640,2560]{0,1:T(8,128)(2,1)} async-done(((bf16[640,320]{0,1:T(8,128)(2,1)}), bf16[640,2560]{0,1:T(8,128)(2,1)}) %all-gather.7.cloned.1.call-update) | async-done | bytes 3276816 | tf_op jit(solution)/shard_map/all_gather | solution.py:20
  44.0 4.1 constant_dynamic-slice_fusion
  48.1 4.1 copy.18
  61.4 5.7 collective-permute-start
  67.1 43.6 %collective-permute-done = f32[8,128]{1,0:T(8,128)S(1)} collective-permute-done((f32[8,128]{1,0:T(8,128)S(1)}, f32[8,128]{1,0:T(8,128)S(1)}, u32[]{:S(2)}, u32[]{:S(2)}) %collective-permute-start) | collective-permute-done | bytes 4128 | tf_op jit(solution)/shard_map/ppermute | solution.py:62
  115.5 3.9 copy.20
  119.4 3.9 copy.21
  123.2 4.0 copy.23
  127.3 6.3 fusion.152
  133.9 3.3 fusion.71
  138.6 2.6 fusion.67
  141.9 3.3 fusion.63
  147.3 4.1 collective-permute-start.13
  151.3 33.7 %collective-permute-done.6 = f32[640,320]{0,1:T(8,128)} collective-permute-done((f32[640,320]{0,1:T(8,128)}, f32[640,320]{0,1:T(8,128)}, u32[]{:S(2)}, u32[]{:S(2)}) %collective-permute-start.6) | collective-permute-done | bytes 819232 | tf_op jit(solution)/shard_map/ppermute | solution.py:94
  185.0 2.6 collective-permute-start.12
  187.7 31.8 %collective-permute-done.7 = f32[640,320]{0,1:T(8,128)} collective-permute-done((f32[640,320]{0,1:T(8,128)S(1)}, f32[640,320]{0,1:T(8,128)}, u32[]{:S(2)}, u32[]{:S(2)}) %collective-permute-start.7) | collective-permute-done | bytes 819232 | tf_op jit(solution)/shard_map/ppermute | solution.py:94
  219.5 18.6 %collective-permute-done.8 = f32[640,320]{0,1:T(8,128)} collective-permute-done((f32[640,320]{0,1:T(8,128)}, f32[640,320]{0,1:T(8,128)}, u32[]{:S(2)}, u32[]{:S(2)}) %collective-permute-start.8) | collective-permute-done | bytes 819232 | tf_op jit(solution)/shard_map/ppermute | solution.py:94
  238.1 3.1 fusion.137
  241.2 2.9 fusion.27
  244.1 11.5 %collective-permute-done.14 = f32[640,320]{0,1:T(8,128)} collective-permute-done((f32[640,320]{0,1:T(8,128)S(1)}, f32[640,320]{0,1:T(8,128)}, u32[]{:S(2)}, u32[]{:S(2)}) %collective-permute-start.14) | collective-permute-done | bytes 819232 | tf_op jit(solution)/shard_map/ppermute | solution.py:73
  255.6 2.9 fusion.21
  258.6 5.8 collective-permute-done.13
  265.7 3.5 fusion.101
  270.4 3.4 collective-permute-start.10
  275.4 2.9 fusion.73
  278.3 15.2 %collective-permute-done.10 = f16[640,320]{0,1:T(8,128)(2,1)S(1)} collective-permute-done((f16[640,320]{0,1:T(8,128)(2,1)S(1)}, f16[640,320]{0,1:T(8,128)(2,1)S(1)}, u32[]{:S(2)}, u32[]{:S(2)}) %collective-permute-start.10) | collective-permute-done | bytes 409632 | tf_op jit(solution)/shard_map/ppermute | solution.py:73
  293.5 2.7 fusion.65
  296.3 6.0 collective-permute-done.11
  302.2 2.7 fusion.61
  305.0 3.8 fusion.146
  308.8 10.6 %all-gather.13.cloned.1.call-done = f32[640,2560]{0,1:T(8,128)} async-done(((f32[640,320]{0,1:T(8,128)}), f32[640,2560]{0,1:T(8,128)}) %all-gather.13.cloned.1.call-update) | async-done | bytes 6553616 | tf_op jit(solution)/shard_map/all_gather | solution.py:20
  319.3 3.0 abs_reduce_fusion.11
  322.3 2.9 abs_reduce_fusion.10
  328.1 2.5 collective-permute-start.19
  331.6 2.4 multiply_reduce_fusion
  338.1 23.6 %collective-permute-done.15 = f32[8,128]{1,0:T(8,128)S(1)} collective-permute-done((f32[8,128]{1,0:T(8,128)S(1)}, f32[8,128]{1,0:T(8,128)S(1)}, u32[]{:S(2)}, u32[]{:S(2)}) %collective-permute-start.15) | collective-permute-done | bytes 4128 | tf_op jit(solution)/shard_map/ppermute | solution.py:62
  365.1 8.1 %collective-permute-done.16 = f32[8,128]{1,0:T(8,128)S(1)} collective-permute-done((f32[8,128]{1,0:T(8,128)S(1)}, f32[8,128]{1,0:T(8,128)S(1)}, u32[]{:S(2)}, u32[]{:S(2)}) %collective-permute-start.16) | collective-permute-done | bytes 4128 | tf_op jit(solution)/shard_map/ppermute | solution.py:62
  377.6 3.4 abs_reduce_fusion.8
  381.4 3.4 collective-permute-start.22
  388.1 26.6 %collective-permute-done.22 = f16[656,320]{0,1:T(8,128)(2,1)S(1)} collective-permute-done((f16[656,320]{0,1:T(8,128)(2,1)S(1)}, f16[656,320]{0,1:T(8,128)(2,1)S(1)}, u32[]{:S(2)}, u32[]{:S(2)}) %collective-permute-start.22) | collective-permute-done | bytes 419872 | tf_op jit(solution)/shard_map/ppermute | solution.py:73
  416.4 10.3 %collective-permute-done.23 = f16[656,320]{0,1:T(8,128)(2,1)S(1)} collective-permute-done((f16[656,320]{0,1:T(8,128)(2,1)S(1)}, f16[656,320]{0,1:T(8,128)(2,1)S(1)}, u32[]{:S(2)}, u32[]{:S(2)}) %collective-permute-start.23) | collective-permute-done | bytes 419872 | tf_op jit(solution)/shard_map/ppermute | solution.py:73
  428.5 2.4 multiply_subtract_fusion
  431.2 45.2 %all-gather.15.cloned.1.call-done = f32[640,2560]{0,1:T(8,128)} async-done(((f32[640,320]{0,1:T(8,128)}), f32[640,2560]{0,1:T(8,128)}) %all-gather.15.cloned.1.call-update) | async-done | bytes 6553616 | tf_op jit(solution)/shard_map/all_gather | solution.py:20
  476.3 3.1 abs_reduce_fusion.7
  480.6 3.2 abs_reduce_fusion.6
  484.2 2.5 collective-permute-start.25
  488.9 9.0 %collective-permute-done.24 = f16[656,320]{0,1:T(8,128)(2,1)S(1)} collective-permute-done((f16[656,320]{0,1:T(8,128)(2,1)S(1)}, f16[656,320]{0,1:T(8,128)(2,1)S(1)}, u32[]{:S(2)}, u32[]{:S(2)}) %collective-permute-start.24) | collective-permute-done | bytes 419872 | tf_op jit(solution)/shard_map/ppermute | solution.py:94
  497.9 21.4 %collective-permute-done.25 = f16[656,320]{0,1:T(8,128)(2,1)S(1)} collective-permute-done((f16[656,320]{0,1:T(8,128)(2,1)S(1)}, f16[656,320]{0,1:T(8,128)(2,1)S(1)}, u32[]{:S(2)}, u32[]{:S(2)}) %collective-permute-start.25) | collective-permute-done | bytes 419872 | tf_op jit(solution)/shard_map/ppermute | solution.py:94
  519.7 10.2 %collective-permute-done.26 = f16[656,320]{0,1:T(8,128)(2,1)S(1)} collective-permute-done((f16[656,320]{0,1:T(8,128)(2,1)S(1)}, f16[656,320]{0,1:T(8,128)(2,1)S(1)}, u32[]{:S(2)}, u32[]{:S(2)}) %collective-permute-start.26) | collective-permute-done | bytes 419872 | tf_op jit(solution)/shard_map/ppermute | solution.py:94
  534.3 2.5 collective-permute-start.27
  538.2 27.0 %collective-permute-done.28 = f16[656,320]{0,1:T(8,128)(2,1)S(1)} collective-permute-done((f16[656,320]{0,1:T(8,128)(2,1)S(1)}, f16[656,320]{0,1:T(8,128)(2,1)S(1)}, u32[]{:S(2)}, u32[]{:S(2)}) %collective-permute-start.28) | collective-permute-done | bytes 419872 | tf_op jit(solution)/shard_map/ppermute | solution.py:73
  565.3 11.4 %collective-permute-done.29 = f16[656,320]{0,1:T(8,128)(2,1)S(1)} collective-permute-done((f16[656,320]{0,1:T(8,128)(2,1)S(1)}, f16[656,320]{0,1:T(8,128)(2,1)S(1)}, u32[]{:S(2)}, u32[]{:S(2)}) %collective-permute-start.29) | collective-permute-done | bytes 419872 | tf_op jit(solution)/shard_map/ppermute | solution.py:73
  580.5 2.3 fusion.125
  582.8 44.9 %all-gather.17.cloned.1.call-done = f32[640,2560]{0,1:T(8,128)} async-done(((f32[640,320]{0,1:T(8,128)}), f32[640,2560]{0,1:T(8,128)}) %all-gather.17.cloned.1.call-update) | async-done | bytes 6553616 | tf_op jit(solution)/shard_map/all_gather | solution.py:20
  627.8 3.1 abs_reduce_fusion.3
  632.0 3.2 abs_reduce_fusion.2
  635.6 2.5 collective-permute-start.31
  640.3 9.0 %collective-permute-done.30 = f16[656,320]{0,1:T(8,128)(2,1)S(1)} collective-permute-done((f16[656,320]{0,1:T(8,128)(2,1)S(1)}, f16[656,320]{0,1:T(8,128)(2,1)S(1)}, u32[]{:S(2)}, u32[]{:S(2)}) %collective-permute-start.30) | collective-permute-done | bytes 419872 | tf_op jit(solution)/shard_map/ppermute | solution.py:94
  649.4 21.4 %collective-permute-done.31 = f16[656,320]{0,1:T(8,128)(2,1)S(1)} collective-permute-done((f16[656,320]{0,1:T(8,128)(2,1)S(1)}, f16[656,320]{0,1:T(8,128)(2,1)S(1)}, u32[]{:S(2)}, u32[]{:S(2)}) %collective-permute-start.31) | collective-permute-done | bytes 419872 | tf_op jit(solution)/shard_map/ppermute | solution.py:94
  671.2 10.2 %collective-permute-done.32 = f16[656,320]{0,1:T(8,128)(2,1)S(1)} collective-permute-done((f16[656,320]{0,1:T(8,128)(2,1)S(1)}, f16[656,320]{0,1:T(8,128)(2,1)S(1)}, u32[]{:S(2)}, u32[]{:S(2)}) %collective-permute-start.32) | collective-permute-done | bytes 419872 | tf_op jit(solution)/shard_map/ppermute | solution.py:94
  686.4 2.5 collective-permute-start.33
  690.3 26.4 %collective-permute-done.34 = f16[656,320]{0,1:T(8,128)(2,1)S(1)} collective-permute-done((f16[656,320]{0,1:T(8,128)(2,1)S(1)}, f16[656,320]{0,1:T(8,128)(2,1)S(1)}, u32[]{:S(2)}, u32[]{:S(2)}) %collective-permute-start.34) | collective-permute-done | bytes 419872 | tf_op jit(solution)/shard_map/ppermute | solution.py:73
  716.8 11.4 %collective-permute-done.35 = f16[656,320]{0,1:T(8,128)(2,1)S(1)} collective-permute-done((f16[656,320]{0,1:T(8,128)(2,1)S(1)}, f16[656,320]{0,1:T(8,128)(2,1)S(1)}, u32[]{:S(2)}, u32[]{:S(2)}) %collective-permute-start.35) | collective-permute-done | bytes 419872 | tf_op jit(solution)/shard_map/ppermute | solution.py:73
  731.7 2.3 fusion.113
  (213 shorter events, 67.8 us)
Async XLA Ops:
  7.2 36.8 %all-gather.7.cloned.1.call-start = ((), (), s32[]{:S(2)}) async-start(), calls=%async_computation | async-start | bytes 3686400 | tf_op jit(solution)/shard_map/all_gather | solution.py:20
  7.9 125.6 %all-gather.9.cloned.1.call-start = ((), (), s32[]{:S(2)}) async-start(), calls=%async_computation.1 | async-start | bytes 7372800 | tf_op jit(solution)/shard_map/all_gather | solution.py:20
  44.0 197.2 %all-gather.11.cloned.1.call-start = ((), (), s32[]{:S(2)}) async-start(), calls=%async_computation.2 | async-start | bytes 7372800 | tf_op jit(solution)/shard_map/all_gather | solution.py:20
  48.1 9.1 %copy-start.15 = (f32[2,640]{1,0:T(2,128)S(1)}, f32[2,640]{1,0:T(2,128)}, u32[]{:S(2)}) copy-start(f32[2,640]{1,0:T(2,128)} %param.10) | copy-start | bytes 15364
  48.1 9.7 %copy-start.7 = (bf16[640,2560]{0,1:T(8,128)(2,1)S(1)}, bf16[640,2560]{0,1:T(8,128)(2,1)}, u32[]{:S(2)}) copy-start(bf16[640,2560]{0,1:T(8,128)(2,1)} %all-gather.7.cloned.1.call-done) | copy-start | bytes 9830404
  52.2 63.3 %collective-permute-start.3 = (bf16[320,2560]{1,0:T(8,128)(2,1)}, bf16[320,2560]{1,0:T(8,128)(2,1)}, u32[]{:S(2)}, u32[]{:S(2)}) collective-permute-start(bf16[320,2560]{1,0:T(8,128)(2,1)} %copy.18), channel_id=1, source_target_pairs={{0,8},{1,9},{10,18},{11,19},{20,28},{21,29},{30,6},{31,7}} | collective-permute-start | bytes 4915208 | tf_op jit(solution)/shard_map/ppermute | solution.py:113
  53.5 65.9 %collective-permute-start.4 = (bf16[320,2560]{1,0:T(8,128)(2,1)}, bf16[320,2560]{1,0:T(8,128)(2,1)}, u32[]{:S(2)}, u32[]{:S(2)}) collective-permute-start(bf16[320,2560]{1,0:T(8,128)(2,1)} %copy.18), channel_id=1, source_target_pairs={{0,16},{1,17},{10,26},{11,27},{20,4},{21,5},{30,14},{31,15}} | collective-permute-start | bytes 4915208 | tf_op jit(solution)/shard_map/ppermute | solution.py:113
  55.3 67.9 %collective-permute-start.5 = (bf16[320,2560]{1,0:T(8,128)(2,1)}, bf16[320,2560]{1,0:T(8,128)(2,1)}, u32[]{:S(2)}, u32[]{:S(2)}) collective-permute-start(bf16[320,2560]{1,0:T(8,128)(2,1)} %copy.18), channel_id=1, source_target_pairs={{0,24},{1,25},{10,2},{11,3},{20,12},{21,13},{30,22},{31,23}} | collective-permute-start | bytes 4915208 | tf_op jit(solution)/shard_map/ppermute | solution.py:113
  61.4 49.3 %collective-permute-start = (f32[8,128]{1,0:T(8,128)S(1)}, f32[8,128]{1,0:T(8,128)S(1)}, u32[]{:S(2)}, u32[]{:S(2)}) collective-permute-start(f32[8,128]{1,0:T(8,128)S(1)} %broadcast_in_dim.28), channel_id=1, source_target_pairs={{0,8},{8,0},{16,24},{24,16},{1,9},{9,1},{17,25},{25,17},{2,10},{10... | collective-permute-start | bytes 12296 | tf_op jit(solution)/shard_map/ppermute | solution.py:62
  67.1 44.8 %collective-permute-start.1 = (f32[8,128]{1,0:T(8,128)S(1)}, f32[8,128]{1,0:T(8,128)S(1)}, u32[]{:S(2)}, u32[]{:S(2)}) collective-permute-start(f32[8,128]{1,0:T(8,128)S(1)} %broadcast_in_dim.28), channel_id=1, source_target_pairs={{0,16},{8,24},{16,0},{24,8},{1,17},{9,25},{17,1},{25,9},{2,18},{10... | collective-permute-start | bytes 12296 | tf_op jit(solution)/shard_map/ppermute | solution.py:62
  110.7 3.6 collective-permute-start.2
  123.2 4.0 copy-start.8
  123.2 4.0 copy-start.19
  127.2 6.7 copy-start.6
  133.6 185.7 %all-gather.13.cloned.1.call-start = ((), (), s32[]{:S(2)}) async-start(), calls=%async_computation.3 | async-start | bytes 7372800 | tf_op jit(solution)/shard_map/all_gather | solution.py:20
  137.2 47.8 %collective-permute-start.6 = (f32[640,320]{0,1:T(8,128)}, f32[640,320]{0,1:T(8,128)}, u32[]{:S(2)}, u32[]{:S(2)}) collective-permute-start(f32[640,320]{0,1:T(8,128)} %fusion.71), channel_id=1, source_target_pairs={{0,8},{8,0},{16,24},{24,16},{1,9},{9,1},{17,25},{25,17},{2,10},{10... | collective-permute-start | bytes 2457608 | tf_op jit(solution)/shard_map/ppermute | solution.py:94
  141.2 5.4 copy-start.10
  141.2 78.2 %collective-permute-start.7 = (f32[640,320]{0,1:T(8,128)S(1)}, f32[640,320]{0,1:T(8,128)}, u32[]{:S(2)}, u32[]{:S(2)}) collective-permute-start(f32[640,320]{0,1:T(8,128)S(1)} %fusion.67), channel_id=1, source_target_pairs={{0,16},{8,24},{16,0},{24,8},{1,17},{9,25},{17,1},{25,9},{2,18},{10... | collective-permute-start | bytes 2457608 | tf_op jit(solution)/shard_map/ppermute | solution.py:94
  145.2 92.9 %collective-permute-start.8 = (f32[640,320]{0,1:T(8,128)}, f32[640,320]{0,1:T(8,128)}, u32[]{:S(2)}, u32[]{:S(2)}) collective-permute-start(f32[640,320]{0,1:T(8,128)} %fusion.63), channel_id=1, source_target_pairs={{0,24},{8,16},{16,8},{24,0},{1,25},{9,17},{17,9},{25,1},{2,26},{10... | collective-permute-start | bytes 2457608 | tf_op jit(solution)/shard_map/ppermute | solution.py:94
  146.7 109.0 %collective-permute-start.14 = (f32[640,320]{0,1:T(8,128)S(1)}, f32[640,320]{0,1:T(8,128)}, u32[]{:S(2)}, u32[]{:S(2)}) collective-permute-start(f32[640,320]{0,1:T(8,128)S(1)} %copy-done.10), channel_id=1, source_target_pairs={{0,24},{8,16},{16,8},{24,0},{1,25},{9,17},{17,9},{25,1},{2,26},{10... | collective-permute-start | bytes 2457608 | tf_op jit(solution)/shard_map/ppermute | solution.py:73
  147.3 117.1 %collective-permute-start.13 = (f32[640,320]{0,1:T(8,128)S(1)}, f32[640,320]{0,1:T(8,128)S(1)}, u32[]{:S(2)}, u32[]{:S(2)}) collective-permute-start(f32[640,320]{0,1:T(8,128)S(1)} %copy-done.10), channel_id=1, source_target_pairs={{0,16},{8,24},{16,0},{24,8},{1,17},{9,25},{17,1},{25,9},{2,18},{10... | collective-permute-start | bytes 2457608 | tf_op jit(solution)/shard_map/ppermute | solution.py:73
  185.0 80.7 %collective-permute-start.12 = (f32[640,320]{0,1:T(8,128)S(1)}, f32[640,320]{0,1:T(8,128)}, u32[]{:S(2)}, u32[]{:S(2)}) collective-permute-start(f32[640,320]{0,1:T(8,128)S(1)} %copy-done.10), channel_id=1, source_target_pairs={{0,8},{8,0},{16,24},{24,16},{1,9},{9,1},{17,25},{25,17},{2,10},{10... | collective-permute-start | bytes 2457608 | tf_op jit(solution)/shard_map/ppermute | solution.py:73
  241.2 23.2 %copy-start.9 = (f32[640,2560]{0,1:T(8,128)S(1)}, f32[640,2560]{0,1:T(8,128)}, u32[]{:S(2)}) copy-start(f32[640,2560]{0,1:T(8,128)} %all-gather.11.cloned.1.call-done) | copy-start | bytes 19660804
  265.7 4.1 copy-start.11
  265.7 4.1 copy-start.12
  269.3 207.1 %all-gather.15.cloned.1.call-start = ((), (), s32[]{:S(2)}) async-start(), calls=%async_computation.4 | async-start | bytes 7372800 | tf_op jit(solution)/shard_map/all_gather | solution.py:20
  270.4 7.9 %copy-start.13 = (f32[640,320]{0,1:T(8,128)}, f32[640,320]{0,1:T(8,128)S(1)}, u32[]{:S(2)}) copy-start(f32[640,320]{0,1:T(8,128)S(1)} %get-tuple-element.28) | copy-start | bytes 2457604
  270.4 7.9 %copy-start.14 = (f32[640,320]{0,1:T(8,128)}, f32[640,320]{0,1:T(8,128)S(1)}, u32[]{:S(2)}) copy-start(f32[640,320]{0,1:T(8,128)S(1)} %get-tuple-element.29) | copy-start | bytes 2457604
  270.4 23.1 %collective-permute-start.10 = (f16[640,320]{0,1:T(8,128)(2,1)S(1)}, f16[640,320]{0,1:T(8,128)(2,1)S(1)}, u32[]{:S(2)}, u32[]{:S(2)}) collective-permute-start(f16[640,320]{0,1:T(8,128)(2,1)S(1)} %get-tuple-element.27), channel_id=1, source_target_pairs={{0,16},{8,24},{16,0},{24,8},{1,17},{9,25},{17,1},{25,9},{2,18},{10... | collective-permute-start | bytes 1228808 | tf_op jit(solution)/shard_map/ppermute | solution.py:73
  273.8 28.4 %collective-permute-start.11 = (f16[640,320]{0,1:T(8,128)(2,1)S(1)}, f16[640,320]{0,1:T(8,128)(2,1)S(1)}, u32[]{:S(2)}, u32[]{:S(2)}) collective-permute-start(f16[640,320]{0,1:T(8,128)(2,1)S(1)} %get-tuple-element.27), channel_id=1, source_target_pairs={{0,24},{8,16},{16,8},{24,0},{1,25},{9,17},{17,9},{25,1},{2,26},{10... | collective-permute-start | bytes 1228808 | tf_op jit(solution)/shard_map/ppermute | solution.py:73
  275.3 29.7 %collective-permute-start.9 = (f16[640,320]{0,1:T(8,128)(2,1)S(1)}, f16[640,320]{0,1:T(8,128)(2,1)S(1)}, u32[]{:S(2)}, u32[]{:S(2)}) collective-permute-start(f16[640,320]{0,1:T(8,128)(2,1)S(1)} %get-tuple-element.27), channel_id=1, source_target_pairs={{0,8},{8,0},{16,24},{24,16},{1,9},{9,1},{17,25},{25,17},{2,10},{10... | collective-permute-start | bytes 1228808 | tf_op jit(solution)/shard_map/ppermute | solution.py:73
  305.0 14.3 %copy-start.3 = (f32[640,320]{0,1:T(8,128)S(1)}, f32[640,320]{0,1:T(8,128)}, u32[]{:S(2)}) copy-start(f32[640,320]{0,1:T(8,128)} %fusion.101) | copy-start | bytes 2457604
  319.3 5.9 copy-start
  327.1 48.5 %collective-permute-start.18 = (f16[656,320]{0,1:T(8,128)(2,1)S(1)}, f16[656,320]{0,1:T(8,128)(2,1)S(1)}, u32[]{:S(2)}, u32[]{:S(2)}) collective-permute-start(f16[656,320]{0,1:T(8,128)(2,1)S(1)} %pad_maximum_fusion), channel_id=1, source_target_pairs={{0,8},{8,0},{16,24},{24,16},{1,9},{9,1},{17,25},{25,17},{2,10},{10... | collective-permute-start | bytes 1259528 | tf_op jit(solution)/shard_map/ppermute | solution.py:94
  328.1 47.6 %collective-permute-start.19 = (f16[656,320]{0,1:T(8,128)(2,1)S(1)}, f16[656,320]{0,1:T(8,128)(2,1)S(1)}, u32[]{:S(2)}, u32[]{:S(2)}) collective-permute-start(f16[656,320]{0,1:T(8,128)(2,1)S(1)} %pad_maximum_fusion.1), channel_id=1, source_target_pairs={{0,16},{8,24},{16,0},{24,8},{1,17},{9,25},{17,1},{25,9},{2,18},{10... | collective-permute-start | bytes 1259528 | tf_op jit(solution)/shard_map/ppermute | solution.py:94
  331.0 45.1 %collective-permute-start.20 = (f16[656,320]{0,1:T(8,128)(2,1)S(1)}, f16[656,320]{0,1:T(8,128)(2,1)}, u32[]{:S(2)}, u32[]{:S(2)}) collective-permute-start(f16[656,320]{0,1:T(8,128)(2,1)S(1)} %pad_maximum_fusion.2), channel_id=1, source_target_pairs={{0,24},{8,16},{16,8},{24,0},{1,25},{9,17},{17,9},{25,1},{2,26},{10... | collective-permute-start | bytes 1259528 | tf_op jit(solution)/shard_map/ppermute | solution.py:94
  334.7 27.1 %collective-permute-start.15 = (f32[8,128]{1,0:T(8,128)S(1)}, f32[8,128]{1,0:T(8,128)S(1)}, u32[]{:S(2)}, u32[]{:S(2)}) collective-permute-start(f32[8,128]{1,0:T(8,128)S(1)} %broadcast_in_dim.29), channel_id=1, source_target_pairs={{0,8},{8,0},{16,24},{24,16},{1,9},{9,1},{17,25},{25,17},{2,10},{10... | collective-permute-start | bytes 12296 | tf_op jit(solution)/shard_map/ppermute | solution.py:62
  336.2 37.0 %collective-permute-start.16 = (f32[8,128]{1,0:T(8,128)S(1)}, f32[8,128]{1,0:T(8,128)S(1)}, u32[]{:S(2)}, u32[]{:S(2)}) collective-permute-start(f32[8,128]{1,0:T(8,128)S(1)} %broadcast_in_dim.29), channel_id=1, source_target_pairs={{0,16},{8,24},{16,0},{24,8},{1,17},{9,25},{17,1},{25,9},{2,18},{10... | collective-permute-start | bytes 12296 | tf_op jit(solution)/shard_map/ppermute | solution.py:62
  361.8 12.5 %collective-permute-start.17 = (f32[8,128]{1,0:T(8,128)S(1)}, f32[8,128]{1,0:T(8,128)S(1)}, u32[]{:S(2)}, u32[]{:S(2)}) collective-permute-start(f32[8,128]{1,0:T(8,128)S(1)} %broadcast_in_dim.29), channel_id=1, source_target_pairs={{0,24},{8,16},{16,8},{24,0},{1,25},{9,17},{17,9},{25,1},{2,26},{10... | collective-permute-start | bytes 12296 | tf_op jit(solution)/shard_map/ppermute | solution.py:62
  375.6 9.2 %slice-start = ((s8[6553600]{0:T(1024)(128)(4,1)}), s8[4194304]{0:T(1024)(128)(4,1)S(1)}, s32[]{:S(2)}) async-start(s8[6553600]{0:T(1024)(128)(4,1)} %bitcast.33), calls=%async_computation.6 | async-start | bytes 8388608
  377.6 7.2 slice-start.1
  381.4 33.4 %collective-permute-start.22 = (f16[656,320]{0,1:T(8,128)(2,1)S(1)}, f16[656,320]{0,1:T(8,128)(2,1)S(1)}, u32[]{:S(2)}, u32[]{:S(2)}) collective-permute-start(f16[656,320]{0,1:T(8,128)(2,1)S(1)} %pad_maximum_fusion.3), channel_id=1, source_target_pairs={{0,16},{8,24},{16,0},{24,8},{1,17},{9,25},{17,1},{25,9},{2,18},{10... | collective-permute-start | bytes 1259528 | tf_op jit(solution)/shard_map/ppermute | solution.py:73
  385.2 41.4 %collective-permute-start.23 = (f16[656,320]{0,1:T(8,128)(2,1)S(1)}, f16[656,320]{0,1:T(8,128)(2,1)S(1)}, u32[]{:S(2)}, u32[]{:S(2)}) collective-permute-start(f16[656,320]{0,1:T(8,128)(2,1)S(1)} %pad_maximum_fusion.3), channel_id=1, source_target_pairs={{0,24},{8,16},{16,8},{24,0},{1,25},{9,17},{17,9},{25,1},{2,26},{10... | collective-permute-start | bytes 1259528 | tf_op jit(solution)/shard_map/ppermute | solution.py:73
  385.8 42.4 %collective-permute-start.21 = (f16[656,320]{0,1:T(8,128)(2,1)S(1)}, f16[656,320]{0,1:T(8,128)(2,1)S(1)}, u32[]{:S(2)}, u32[]{:S(2)}) collective-permute-start(f16[656,320]{0,1:T(8,128)(2,1)S(1)} %pad_maximum_fusion.3), channel_id=1, source_target_pairs={{0,8},{8,0},{16,24},{24,16},{1,9},{9,1},{17,25},{25,17},{2,10},{10... | collective-permute-start | bytes 1259528 | tf_op jit(solution)/shard_map/ppermute | solution.py:73
  430.9 196.9 %all-gather.17.cloned.1.call-start = ((), (), s32[]{:S(2)}) async-start(), calls=%async_computation.5 | async-start | bytes 7372800 | tf_op jit(solution)/shard_map/all_gather | solution.py:20
  479.4 1.1 copy-start.2
  479.7 7.0 copy-start.5
  479.8 18.0 %collective-permute-start.24 = (f16[656,320]{0,1:T(8,128)(2,1)S(1)}, f16[656,320]{0,1:T(8,128)(2,1)S(1)}, u32[]{:S(2)}, u32[]{:S(2)}) collective-permute-start(f16[656,320]{0,1:T(8,128)(2,1)S(1)} %pad_maximum_fusion.4), channel_id=1, source_target_pairs={{0,8},{8,0},{16,24},{24,16},{1,9},{9,1},{17,25},{25,17},{2,10},{10... | collective-permute-start | bytes 1259528 | tf_op jit(solution)/shard_map/ppermute | solution.py:94
  484.2 35.2 %collective-permute-start.25 = (f16[656,320]{0,1:T(8,128)(2,1)S(1)}, f16[656,320]{0,1:T(8,128)(2,1)S(1)}, u32[]{:S(2)}, u32[]{:S(2)}) collective-permute-start(f16[656,320]{0,1:T(8,128)(2,1)S(1)} %pad_maximum_fusion.5), channel_id=1, source_target_pairs={{0,16},{8,24},{16,0},{24,8},{1,17},{9,25},{17,1},{25,9},{2,18},{10... | collective-permute-start | bytes 1259528 | tf_op jit(solution)/shard_map/ppermute | solution.py:94
  488.6 41.4 %collective-permute-start.26 = (f16[656,320]{0,1:T(8,128)(2,1)S(1)}, f16[656,320]{0,1:T(8,128)(2,1)S(1)}, u32[]{:S(2)}, u32[]{:S(2)}) collective-permute-start(f16[656,320]{0,1:T(8,128)(2,1)S(1)} %pad_maximum_fusion.6), channel_id=1, source_target_pairs={{0,24},{8,16},{16,8},{24,0},{1,25},{9,17},{17,9},{25,1},{2,26},{10... | collective-permute-start | bytes 1259528 | tf_op jit(solution)/shard_map/ppermute | solution.py:94
  532.4 32.8 %collective-permute-start.28 = (f16[656,320]{0,1:T(8,128)(2,1)S(1)}, f16[656,320]{0,1:T(8,128)(2,1)S(1)}, u32[]{:S(2)}, u32[]{:S(2)}) collective-permute-start(f16[656,320]{0,1:T(8,128)(2,1)S(1)} %pad_maximum_fusion.7), channel_id=1, source_target_pairs={{0,16},{8,24},{16,0},{24,8},{1,17},{9,25},{17,1},{25,9},{2,18},{10... | collective-permute-start | bytes 1259528 | tf_op jit(solution)/shard_map/ppermute | solution.py:73
  532.5 44.2 %collective-permute-start.29 = (f16[656,320]{0,1:T(8,128)(2,1)S(1)}, f16[656,320]{0,1:T(8,128)(2,1)S(1)}, u32[]{:S(2)}, u32[]{:S(2)}) collective-permute-start(f16[656,320]{0,1:T(8,128)(2,1)S(1)} %pad_maximum_fusion.7), channel_id=1, source_target_pairs={{0,24},{8,16},{16,8},{24,0},{1,25},{9,17},{17,9},{25,1},{2,26},{10... | collective-permute-start | bytes 1259528 | tf_op jit(solution)/shard_map/ppermute | solution.py:73
  534.3 42.8 %collective-permute-start.27 = (f16[656,320]{0,1:T(8,128)(2,1)S(1)}, f16[656,320]{0,1:T(8,128)(2,1)S(1)}, u32[]{:S(2)}, u32[]{:S(2)}) collective-permute-start(f16[656,320]{0,1:T(8,128)(2,1)S(1)} %pad_maximum_fusion.7), channel_id=1, source_target_pairs={{0,8},{8,0},{16,24},{24,16},{1,9},{9,1},{17,25},{25,17},{2,10},{10... | collective-permute-start | bytes 1259528 | tf_op jit(solution)/shard_map/ppermute | solution.py:73
  630.8 1.1 copy-start.1
  631.1 7.0 copy-start.4
  631.3 18.0 %collective-permute-start.30 = (f16[656,320]{0,1:T(8,128)(2,1)S(1)}, f16[656,320]{0,1:T(8,128)(2,1)S(1)}, u32[]{:S(2)}, u32[]{:S(2)}) collective-permute-start(f16[656,320]{0,1:T(8,128)(2,1)S(1)} %pad_maximum_fusion.8), channel_id=1, source_target_pairs={{0,8},{8,0},{16,24},{24,16},{1,9},{9,1},{17,25},{25,17},{2,10},{10... | collective-permute-start | bytes 1259528 | tf_op jit(solution)/shard_map/ppermute | solution.py:94
  635.6 35.2 %collective-permute-start.31 = (f16[656,320]{0,1:T(8,128)(2,1)S(1)}, f16[656,320]{0,1:T(8,128)(2,1)S(1)}, u32[]{:S(2)}, u32[]{:S(2)}) collective-permute-start(f16[656,320]{0,1:T(8,128)(2,1)S(1)} %pad_maximum_fusion.9), channel_id=1, source_target_pairs={{0,16},{8,24},{16,0},{24,8},{1,17},{9,25},{17,1},{25,9},{2,18},{10... | collective-permute-start | bytes 1259528 | tf_op jit(solution)/shard_map/ppermute | solution.py:94
  640.0 41.4 %collective-permute-start.32 = (f16[656,320]{0,1:T(8,128)(2,1)S(1)}, f16[656,320]{0,1:T(8,128)(2,1)S(1)}, u32[]{:S(2)}, u32[]{:S(2)}) collective-permute-start(f16[656,320]{0,1:T(8,128)(2,1)S(1)} %pad_maximum_fusion.10), channel_id=1, source_target_pairs={{0,24},{8,16},{16,8},{24,0},{1,25},{9,17},{17,9},{25,1},{2,26},{10... | collective-permute-start | bytes 1259528 | tf_op jit(solution)/shard_map/ppermute | solution.py:94
  683.4 2.4 copy-start.16
  683.5 2.4 copy-start.17
  683.5 2.3 copy-start.18
  683.9 32.8 %collective-permute-start.34 = (f16[656,320]{0,1:T(8,128)(2,1)S(1)}, f16[656,320]{0,1:T(8,128)(2,1)S(1)}, u32[]{:S(2)}, u32[]{:S(2)}) collective-permute-start(f16[656,320]{0,1:T(8,128)(2,1)S(1)} %pad_maximum_fusion.11), channel_id=1, source_target_pairs={{0,16},{8,24},{16,0},{24,8},{1,17},{9,25},{17,1},{25,9},{2,18},{10... | collective-permute-start | bytes 1259528 | tf_op jit(solution)/shard_map/ppermute | solution.py:73
  684.0 44.2 %collective-permute-start.35 = (f16[656,320]{0,1:T(8,128)(2,1)S(1)}, f16[656,320]{0,1:T(8,128)(2,1)S(1)}, u32[]{:S(2)}, u32[]{:S(2)}) collective-permute-start(f16[656,320]{0,1:T(8,128)(2,1)S(1)} %pad_maximum_fusion.11), channel_id=1, source_target_pairs={{0,24},{8,16},{16,8},{24,0},{1,25},{9,17},{17,9},{25,1},{2,26},{10... | collective-permute-start | bytes 1259528 | tf_op jit(solution)/shard_map/ppermute | solution.py:73
  686.4 42.2 %collective-permute-start.33 = (f16[656,320]{0,1:T(8,128)(2,1)S(1)}, f16[656,320]{0,1:T(8,128)(2,1)S(1)}, u32[]{:S(2)}, u32[]{:S(2)}) collective-permute-start(f16[656,320]{0,1:T(8,128)(2,1)S(1)} %pad_maximum_fusion.11), channel_id=1, source_target_pairs={{0,8},{8,0},{16,24},{24,16},{1,9},{9,1},{17,25},{25,17},{2,10},{10... | collective-permute-start | bytes 1259528 | tf_op jit(solution)/shard_map/ppermute | solution.py:73
Sparse Core Ops, SparseCore 0:
  9.9 34.0 all-gather.6
  45.8 46.6 all-gather.8
  133.7 44.7 all-gather.10
  269.4 49.8 all-gather.12
  431.0 45.2 all-gather.14
  582.9 44.7 all-gather.16
